TPU v7x, 32 devices: a whole 2x2x4 slice. The times are simulated.
32 devices in a mesh: dp: 4 (over z), seq: 8 (over y, x, core).
Axes of the slice: x: 2, y: 2, z: 4, core: 2. Of those that a mesh axis runs over, the one named last changes fastest.
Arguments:
- tiles: bfloat16 [4, 1536, 768], P('dp', 'seq'), may hold values from -40 to 40
- cotangent: bfloat16 [4, 1536, 768], P('dp', 'seq'), may hold values from -0.078125 to 0.078125
- segment_of: int32 [4, 1536, 1], P('dp', 'seq'), may hold values from 0 to 15; in each aligned block of 192 rows (0 to 191, 192 to 383, ..., all dimensions but the last counted through in order) at most 20 rows name the same one
- tissue_count: int32 [4], P('dp'), may hold values from 768 to 1536
- w_query: bfloat16 [768, 768], P('seq'), may hold values from -0.21875 to 0.21875
- w_key: bfloat16 [768, 768], P('seq'), may hold values from -0.21875 to 0.21875
- w_value: bfloat16 [768, 768], P('seq'), may hold values from -0.21875 to 0.21875
- w_out: bfloat16 [768, 768], P('seq'), may hold values from -2.390625 to 2.390625
Outputs:
- layer_out: bfloat16 [4, 1536, 768], P('dp', 'seq')
- grad_value: float32 [768, 768], P('seq')
Inputs may be any that keep to these rules, and one draw needn't show every extreme that they name: `segment_of`: within one slide, the 192 tiles of one block name one group at most 20 times; some group is named exactly 20 times.
All inputs are finite; a program needn't handle non-finite values.
Results may differ from a plain program's by a relative error of at most 0.014.
Values may be sent and summed in bfloat16 or wider, within the bound.
No kernel may reach another device: no remote copies, remote signals or barrier semaphores. Data moves between devices by JAX's collectives and lax.ppermute only.
A program may use at most 64 MiB of HBM per device.

v0:
```python
import functools
import math

import jax
import jax.numpy as jnp
from jax import lax
from jax.experimental import pallas as pl
from jax.experimental.pallas import tpu as pltpu
from jax.sharding import PartitionSpec as P


HEADS = 12
NEG_BIG = -1e30
LOG2E = 1.4426950408889634


VM = pl.BlockSpec(memory_space=pltpu.VMEM)
ANY = pl.BlockSpec(memory_space=pl.ANY)
SM = pl.BlockSpec(memory_space=pltpu.SMEM)


def dot_last(a, b):
    return lax.dot_general(a, b, (((1,), (1,)), ((), ())), preferred_element_type=jnp.float32)


def dot(a, b):
    return lax.dot_general(a, b, (((1,), (0,)), ((), ())), preferred_element_type=jnp.float32)


def pack_kernel(hg, tg, wr, cw, wq, wk, wv, seg, *outs):
    group = lax.axis_index("seq") // tg
    for k in range(hg):
        for part in range(hg):

            @pl.when((group ^ k) == part)
            def _():
                cols = slice(part * cw, (part + 1) * cw)
                outs[k][0, :wr] = wq[:, cols]
                outs[k][1, :wr] = wk[:, cols]
                outs[k][2, :wr] = wv[:, cols]

        for i in range(3):
            outs[k][i, wr:] = jnp.broadcast_to(seg[...], (8, cw)).astype(jnp.bfloat16)


def dout_kernel(hg, tg, wr, count, cot, *refs):
    n = hg * tg
    pieces, outs, wout = refs[:n], refs[n : n + hg], refs[n + hg]
    own = lax.axis_index("seq")
    member = own % tg
    rows = cot.shape[0]
    position = own * rows + lax.broadcasted_iota(jnp.int32, cot.shape, 0)
    masked = jnp.where(position < count[0], cot[...].astype(jnp.float32), 0.0).astype(jnp.bfloat16)
    for k in range(hg):
        for tau in range(tg):
            to = pl.multiple_of((member ^ tau) * wr, wr)
            wout[k, pl.ds(to, wr), :] = pieces[tau * hg + k][...].astype(wout.dtype)
        block = wout[k].astype(jnp.bfloat16)
        outs[k][...] = dot_last(masked, block).astype(jnp.bfloat16)


def proj_kernel(hg, wout, *refs):
    out = refs[hg]
    total = None
    for k in range(hg):
        term = dot(refs[k][...], wout[k].astype(jnp.bfloat16))
        total = term if total is None else total + term
    out[0] = total.astype(jnp.bfloat16)


def main_kernel(hg, tg, parts, rows, wr, head_dim, by_dp, count, *refs):
    n = hg * tg
    refs = list(refs)
    tiles = [[refs.pop(0) for _ in range(parts)] for _ in range(n)]
    packed = [refs.pop(0) for _ in range(n)]
    douts = [refs.pop(0) for _ in range(hg)]
    o_out = [refs.pop(0) for _ in range(hg)]
    g_out = [refs.pop(0) for _ in range(tg)]
    wp_s, w_s, seg_s, col_s, q_s, k_s, v_s, t_s, bias_s, p_s, d_s, o_s, gt_s, grad_s, sems = refs
    cw = q_s.shape[1]
    own = lax.axis_index("seq")
    group = own // tg
    member = own % tg
    keys = n * rows
    heads = cw // head_dim
    packed_copies = [
        pltpu.make_async_copy(packed[r], wp_s.at[r], sems.at[n * parts + r]) for r in range(n)
    ]
    size = rows // parts
    tile_copies = [
        pltpu.make_async_copy(
            tiles[r][i], t_s.at[pl.ds(r * rows + i * size, size), :], sems.at[r * parts + i]
        )
        for r in range(n)
        for i in range(parts)
    ]
    dout_copies = [
        pltpu.make_async_copy(
            douts[k], d_s.at[pl.ds(k * rows, rows), :], sems.at[n * parts + n + k]
        )
        for k in range(hg)
    ]
    for copy in packed_copies + tile_copies + dout_copies:
        copy.start()
    for tau in range(tg):
        for k in range(hg):
            r = tau * hg + k
            packed_copies[r].wait()
            source = (group ^ k) * tg + (member ^ tau)
            to = pl.multiple_of(source * wr, wr)
            for i in range(3):
                w_s[i, pl.ds(to, wr), :] = wp_s[r, i, :wr].astype(w_s.dtype)
            line = wp_s[r, 0, wr : wr + 8, :].astype(jnp.float32)[:1]
            at = source * rows + lax.broadcasted_iota(jnp.int32, (1, rows), 1)
            columns = slice(r * rows, (r + 1) * rows)
            seg_s[0:1, columns] = line
            seg_s[1:2, columns] = jnp.where(at < count[0], line, -1.0)
    for copy in tile_copies:
        copy.wait()
    for tau in range(tg):
        at = slice(tau * hg * rows, (tau + 1) * hg * rows)
        block = t_s[at, :]
        if tau == 0:
            q_s[at, :] = dot(block, w_s[0].astype(jnp.bfloat16)).astype(jnp.bfloat16)
        k_s[at, :] = dot(block, w_s[1].astype(jnp.bfloat16)).astype(jnp.bfloat16)
        v_s[at, :] = dot(block, w_s[2].astype(jnp.bfloat16)).astype(jnp.bfloat16)
    for copy in dout_copies:
        copy.wait()
    gt_s[...] = jnp.zeros_like(gt_s)
    scale = head_dim ** (-0.5) * LOG2E
    lane_head = lax.broadcasted_iota(jnp.int32, (rows, cw), 1) // head_dim
    label = seg_s[1:2, :]
    square_row = lax.broadcasted_iota(jnp.int32, (rows, rows), 0)
    square_col = lax.broadcasted_iota(jnp.int32, (rows, rows), 1)

    for k in range(hg):
        at = slice(k * rows, (k + 1) * rows)
        line = jnp.where(square_row == square_col, seg_s[0:1, at], 0.0)
        col_s[:, k : k + 1] = jnp.sum(line, axis=1, keepdims=True)

    def chunk(k, carry):
        start = pl.multiple_of(k * rows, rows)
        column = lax.broadcasted_iota(jnp.int32, (1, keys), 1)
        in_block = (column >= start) & (column < start + rows) & (label >= 0.0)
        same_value = jnp.where(in_block, 1.0, 0.0)
        other_value = jnp.where(in_block, 0.0, NEG_BIG)
        chosen = lax.broadcasted_iota(jnp.int32, (rows, 128), 1) == k
        segment = jnp.sum(
            jnp.where(chosen, col_s[...], 0.0), axis=1, keepdims=True
        )
        bias = jnp.where(segment == label, same_value, other_value)
        row_at = start + lax.broadcasted_iota(jnp.int32, (rows, keys), 0)
        col_at = lax.broadcasted_iota(jnp.int32, (rows, keys), 1)
        bias_s[...] = jnp.where(row_at == col_at, 1.0, bias)
        q = q_s[pl.ds(start, rows), :]
        scaled = jnp.zeros((rows, cw), jnp.float32)
        for h in range(heads):
            qh = jnp.where(lane_head == h, q, jnp.zeros_like(q))
            s = dot_last(qh, k_s[...]) * scale + bias_s[...]
            top = jnp.max(s, axis=1, keepdims=True)
            p = jnp.exp2(s - top)
            total = jnp.sum(p, axis=1, keepdims=True)
            p_s[h] = p.astype(jnp.bfloat16)
            inverse = 1.0 / total
            scaled = jnp.where(lane_head == h, inverse, scaled)
        acc = jnp.zeros((rows, cw), jnp.float32)
        for h in range(heads):
            acc = jnp.where(lane_head == h, dot(p_s[h], v_s[...]), acc)
        o_s[pl.ds(start, rows), :] = (acc * scaled).astype(jnp.bfloat16)
        d = (d_s[pl.ds(start, rows), :].astype(jnp.float32) * scaled).T.astype(jnp.bfloat16)
        for h in range(heads):
            at = slice(h * head_dim, (h + 1) * head_dim)
            gt_s[at, :] += dot(d[at, :], p_s[h])
        return carry

    lax.fori_loop(0, hg, chunk, 0, unroll=True)
    for k in range(hg):
        o_out[k][...] = o_s[k * rows : (k + 1) * rows, :]
    grad_s[...] = dot(gt_s[...].astype(jnp.bfloat16), t_s[...]).T
    first = lax.axis_index("dp") if by_dp else 0
    for tau in range(tg):
        for m in range(hg):
            to = ((group ^ m ^ first) * tg + (member ^ tau)) * wr
            to = pl.multiple_of(to, wr)
            g_out[tau][m] = grad_s[pl.ds(to, wr), :].astype(jnp.bfloat16)


def main_call(hg, tg, parts, rows, width, wr, cw, head_dim, by_dp):
    n = hg * tg
    keys = n * rows
    bf16 = jnp.bfloat16
    wide = bf16 if wr % 16 == 0 else jnp.float32
    return pl.pallas_call(
        functools.partial(main_kernel, hg, tg, parts, rows, wr, head_dim, by_dp),
        out_shape=[jax.ShapeDtypeStruct((rows, cw), bf16)] * hg
        + [jax.ShapeDtypeStruct((hg, wr, cw), bf16)] * tg,
        in_specs=[SM] + [ANY] * (n * parts + n + hg),
        out_specs=[VM] * (hg + tg),
        scratch_shapes=[
            pltpu.VMEM((n, 3, wr + 8, cw), bf16),
            pltpu.VMEM((3, width, cw), wide),
            pltpu.VMEM((8, keys), jnp.float32),
            pltpu.VMEM((rows, 128), jnp.float32),
            pltpu.VMEM((hg * rows, cw), bf16),
            pltpu.VMEM((keys, cw), bf16),
            pltpu.VMEM((keys, cw), bf16),
            pltpu.VMEM((keys, width), bf16),
            pltpu.VMEM((rows, keys), jnp.float32),
            pltpu.VMEM((cw // head_dim, rows, keys), bf16),
            pltpu.VMEM((hg * rows, cw), bf16),
            pltpu.VMEM((hg * rows, cw), bf16),
            pltpu.VMEM((cw, keys), jnp.float32),
            pltpu.VMEM((width, cw), jnp.float32),
            pltpu.SemaphoreType.DMA((n * parts + n + hg,)),
        ],
        compiler_params=pltpu.CompilerParams(vmem_limit_bytes=60 * 1024 * 1024),
    )


def local(tiles, cotangent, segment_of, tissue_count, w_query, w_key, w_value, w_out):
    rows, width = tiles.shape[1:]
    wr = w_query.shape[0]
    n = lax.axis_size("seq")
    dp = lax.axis_size("dp")
    hg = math.gcd(HEADS, n)
    tg = n // hg
    cw = width // hg
    head_dim = width // HEADS
    by_dp = dp == hg
    own = lax.axis_index("seq")
    group = own // tg
    bf16 = jnp.bfloat16

    def hop(x, step):
        return lax.ppermute(x, "seq", [(s, s ^ step) for s in range(n)])

    def over_groups(pieces):
        return [pieces[0]] + [hop(pieces[k], k * tg) for k in range(1, hg)]

    def over_members(pieces):
        return [pieces] + [[hop(x, tau) for x in pieces] for tau in range(1, tg)]

    def flat(table):
        return [table[tau][k] for tau in range(tg) for k in range(hg)]

    wide = bf16 if wr % 16 == 0 else jnp.float32
    parts = 2 if hg == 4 and rows % 32 == 0 else 1
    segment_line = segment_of.reshape(1, rows)
    wout_table = over_members(over_groups([w_out] * hg))
    packed = pl.pallas_call(
        functools.partial(pack_kernel, hg, tg, wr, cw),
        out_shape=[jax.ShapeDtypeStruct((3, wr + 8, cw), bf16)] * hg,
        in_specs=[VM] * 4,
        out_specs=[VM] * hg,
    )(w_query, w_key, w_value, segment_line)
    weight_table = over_members(over_groups(packed))
    if parts == 2:
        half = rows // 2
        upper, lower = tiles[0, :half], tiles[0, half:]
        first = [hop(upper, tg), hop(lower, tg)]
        second = [hop(upper, 2 * tg), hop(lower, 2 * tg)]
        third = [hop(first[0], 2 * tg), hop(second[1], tg)]
        tile_pieces = [[upper, lower], first, second, third]
    else:
        tile_pieces = [[x] for x in over_groups([tiles[0]] * hg)]
    tile_pieces = tile_pieces + [
        [hop(x, tau) for x in piece]
        for tau in range(1, tg)
        for piece in tile_pieces
    ]

    *douts, wout = pl.pallas_call(
        functools.partial(dout_kernel, hg, tg, wr),
        out_shape=[jax.ShapeDtypeStruct((rows, cw), bf16)] * hg
        + [jax.ShapeDtypeStruct((hg, cw, width), wide)],
        in_specs=[SM] + [VM] * (1 + n),
        out_specs=[VM] * (hg + 1),
    )(tissue_count, cotangent[0], *flat(wout_table))
    douts = over_groups(douts)

    results = main_call(hg, tg, parts, rows, width, wr, cw, head_dim, by_dp)(
        tissue_count,
        *[x for piece in tile_pieces for x in piece],
        *flat(weight_table),
        *douts,
    )
    attention = over_groups(results[:hg])
    grads = results[hg:]
    summed = grads[0].astype(jnp.float32)
    for tau in range(1, tg):
        summed = summed + hop(grads[tau], tau).astype(jnp.float32)
    summed = summed.astype(bf16)

    layer_rows = pl.pallas_call(
        functools.partial(proj_kernel, hg),
        out_shape=jax.ShapeDtypeStruct((1, rows, width), bf16),
        in_specs=[VM] * (1 + hg),
        out_specs=VM,
    )(wout, *attention)

    if by_dp:
        own_dp = lax.axis_index("dp")
        mine = summed[0].astype(jnp.float32)
        for m in range(1, hg):
            got = lax.ppermute(summed[m], "dp", [(z, z ^ m) for z in range(dp)])
            mine = mine + got.astype(jnp.float32)
        mine = mine.astype(bf16)
        parts = []
        for m in range(dp):
            pairs = [
                (z * n + s, (z ^ m) * n + (s ^ (z * tg))) for z in range(dp) for s in range(n)
            ]
            parts.append(lax.ppermute(mine, ("dp", "seq"), pairs))
        index = group ^ own_dp
    else:
        total = lax.psum(summed, "dp")
        parts = over_groups([total[k] for k in range(hg)])
        index = group
    columns = []
    for p in range(hg):
        piece = parts[0]
        for m in range(1, hg):
            piece = jnp.where((index ^ p) == m, parts[m], piece)
        columns.append(piece)
    return (layer_rows, jnp.concatenate(columns, axis=1).astype(jnp.float32))


def solution(mesh):
    placed = (
        P("dp", "seq", None),
        P("dp", "seq", None),
        P("dp", "seq", None),
        P("dp"),
        P("seq", None),
        P("seq", None),
        P("seq", None),
        P("seq", None),
    )
    return jax.shard_map(
        local,
        mesh=mesh,
        in_specs=placed,
        out_specs=(P("dp", "seq", None), P("seq", None)),
        check_vma=False,
    )
```

profile of v0, /device:TPU:0, one launch (start us, length us, event | category | flops | bytes accessed | tf_op | source)
XLA Modules:
  0.0 86.5 jit_solution(14503284546969683808)
XLA Ops:
  0.6 2.2 %shard_map.96 = (bf16[3,104,192]{2,1,0:T(8,128)(2,1)}, bf16[3,104,192]{2,1,0:T(8,128)(2,1)}, bf16[3,104,192]{2,1,0:T(8,128)(2,1)}, bf16[3,104,192]{2,1,0:T(8,128)(2,1)}) custom-call(bf16[96,768]{1,0:T(8,128)(2,1)} %wq.1, bf16[96,768]{1,0:T(8,128)(2,1)} %wk.1, bf16[96,768]{1,0:T(8,128)(2,1)} %wv.1, s32[1,192]{1,0:T(1,128)} %bitcast.18), custom_call_target="tpu_custom_call" | custom-call | tf_op jit(solution)/shard_map/pallas_call | solution.py:250
  2.8 3.0 %collective-permute-start.21 = (bf16[3,104,192]{2,1,0:T(8,128)(2,1)}, bf16[3,104,192]{2,1,0:T(8,128)(2,1)S(1)}, u32[]{:S(2)}, u32[]{:S(2)}) collective-permute-start(bf16[3,104,192]{2,1,0:T(8,128)(2,1)} %get-tuple-element.19), channel_id=1, source_target_pairs={{0,2},{1,3},{2,0},{3,1},{4,6},{5,7},{6,4},{7,5},{8,10},{9,11},{10,... | collective-permute-start | bytes 359432 | tf_op jit(solution)/shard_map/ppermute | solution.py:235
  5.8 1.5 %collective-permute-start.22 = (bf16[3,104,192]{2,1,0:T(8,128)(2,1)}, bf16[3,104,192]{2,1,0:T(8,128)(2,1)S(1)}, u32[]{:S(2)}, u32[]{:S(2)}) collective-permute-start(bf16[3,104,192]{2,1,0:T(8,128)(2,1)} %get-tuple-element.20), channel_id=1, source_target_pairs={{0,4},{1,5},{2,6},{3,7},{4,0},{5,1},{6,2},{7,3},{8,12},{9,13},{10,... | collective-permute-start | bytes 359432 | tf_op jit(solution)/shard_map/ppermute | solution.py:235
  7.3 2.0 %collective-permute-start = (bf16[96,768]{1,0:T(8,128)(2,1)}, bf16[96,768]{1,0:T(8,128)(2,1)S(1)}, u32[]{:S(2)}, u32[]{:S(2)}) collective-permute-start(bf16[96,768]{1,0:T(8,128)(2,1)} %refs_0_.1), channel_id=1, source_target_pairs={{0,2},{1,3},{2,0},{3,1},{4,6},{5,7},{6,4},{7,5},{8,10},{9,11},{10,... | collective-permute-start | bytes 442376 | tf_op jit(solution)/shard_map/ppermute | solution.py:235
  9.3 1.5 %collective-permute-start.1 = (bf16[96,768]{1,0:T(8,128)(2,1)}, bf16[96,768]{1,0:T(8,128)(2,1)S(1)}, u32[]{:S(2)}, u32[]{:S(2)}) collective-permute-start(bf16[96,768]{1,0:T(8,128)(2,1)} %refs_0_.1), channel_id=1, source_target_pairs={{0,4},{1,5},{2,6},{3,7},{4,0},{5,1},{6,2},{7,3},{8,12},{9,13},{10,... | collective-permute-start | bytes 442376 | tf_op jit(solution)/shard_map/ppermute | solution.py:235
  10.9 3.0 %collective-permute-start.2 = (bf16[96,768]{1,0:T(8,128)(2,1)}, bf16[96,768]{1,0:T(8,128)(2,1)S(1)}, u32[]{:S(2)}, u32[]{:S(2)}) collective-permute-start(bf16[96,768]{1,0:T(8,128)(2,1)} %refs_0_.1), channel_id=1, source_target_pairs={{0,6},{1,7},{2,4},{3,5},{4,2},{5,3},{6,0},{7,1},{8,14},{9,15},{10,... | collective-permute-start | bytes 442376 | tf_op jit(solution)/shard_map/ppermute | solution.py:235
  13.9 2.1 %collective-permute-done.22.refs_18_ = bf16[3,104,192]{2,1,0:T(8,128)(2,1)S(1)} collective-permute-done((bf16[3,104,192]{2,1,0:T(8,128)(2,1)}, bf16[3,104,192]{2,1,0:T(8,128)(2,1)S(1)}, u32[]{:S(2)}, u32[]{:S(2)}) %collective-permute-start.22) | collective-permute-done | bytes 119840 | tf_op jit(solution)/shard_map/ppermute | solution.py:235
  21.3 1.5 %collective-permute-start.9 = (bf16[96,768]{1,0:T(8,128)(2,1)S(1)}, bf16[96,768]{1,0:T(8,128)(2,1)S(1)}, u32[]{:S(2)}, u32[]{:S(2)}) collective-permute-start(bf16[96,768]{1,0:T(8,128)(2,1)S(1)} %get-tuple-element.33.refs_0_), channel_id=1, source_target_pairs={{0,4},{1,5},{2,6},{3,7},{4,0},{5,1},{6,2},{7,3},{8,12},{9,13},{10,... | collective-permute-start | bytes 442376 | tf_op jit(solution)/shard_map/ppermute | solution.py:235
  24.6 2.5 %collective-permute-done.8.refs_3_ = bf16[96,768]{1,0:T(8,128)(2,1)S(1)} collective-permute-done((bf16[96,768]{1,0:T(8,128)(2,1)S(1)}, bf16[96,768]{1,0:T(8,128)(2,1)S(1)}, u32[]{:S(2)}, u32[]{:S(2)}) %collective-permute-start.8) | collective-permute-done | bytes 147488 | tf_op jit(solution)/shard_map/ppermute | solution.py:235
  27.6 1.5 %collective-permute-done.10.refs_5_ = bf16[96,768]{1,0:T(8,128)(2,1)S(1)} collective-permute-done((bf16[96,768]{1,0:T(8,128)(2,1)S(1)}, bf16[96,768]{1,0:T(8,128)(2,1)S(1)}, u32[]{:S(2)}, u32[]{:S(2)}) %collective-permute-start.10) | collective-permute-done | bytes 147488 | tf_op jit(solution)/shard_map/ppermute | solution.py:235
  30.1 1.7 %collective-permute-start.11 = (bf16[96,768]{1,0:T(8,128)(2,1)S(1)}, bf16[96,768]{1,0:T(8,128)(2,1)S(1)}, u32[]{:S(2)}, u32[]{:S(2)}) collective-permute-start(bf16[96,768]{1,0:T(8,128)(2,1)S(1)} %collective-permute-done.7.refs_2_), channel_id=1, source_target_pairs={{0,4},{1,5},{2,6},{3,7},{4,0},{5,1},{6,2},{7,3},{8,12},{9,13},{10,... | collective-permute-start | bytes 442376 | tf_op jit(solution)/shard_map/ppermute | solution.py:235
  32.8 3.1 %collective-permute-done.11.refs_6_ = bf16[96,768]{1,0:T(8,128)(2,1)S(1)} collective-permute-done((bf16[96,768]{1,0:T(8,128)(2,1)S(1)}, bf16[96,768]{1,0:T(8,128)(2,1)S(1)}, u32[]{:S(2)}, u32[]{:S(2)}) %collective-permute-start.11) | collective-permute-done | bytes 147488 | tf_op jit(solution)/shard_map/ppermute | solution.py:235
  35.9 1.5 %collective-permute-done.12.refs_7_ = bf16[96,768]{1,0:T(8,128)(2,1)S(1)} collective-permute-done((bf16[96,768]{1,0:T(8,128)(2,1)S(1)}, bf16[96,768]{1,0:T(8,128)(2,1)S(1)}, u32[]{:S(2)}, u32[]{:S(2)}) %collective-permute-start.12) | collective-permute-done | bytes 147488 | tf_op jit(solution)/shard_map/ppermute | solution.py:235
  38.7 3.1 %shard_map.95 = (bf16[192,192]{1,0:T(8,128)(2,1)}, bf16[192,192]{1,0:T(8,128)(2,1)}, bf16[192,192]{1,0:T(8,128)(2,1)}, bf16[192,192]{1,0:T(8,128)(2,1)}, bf16[4,192,768]{2,1,0:T(8,128)(2,1)}) custom-call(s32[1]{0:T(128)S(6)} %copy.10.count, bf16[192,768]{1,0:T(8,128)(2,1)} %bitcast.17, bf16[96,768]{1,0:T(8,128)(2,1)} %refs_0_.1, bf16[96,768]{1,0:T(8,128)(2,1)} %copy-done.23, ...), custom_call_target="tpu_custom_call" | custom-call | tf_op jit(solution)/shard_map/pallas_call | solution.py:272
  43.3 2.1 %collective-permute-start.30 = (bf16[192,192]{1,0:T(8,128)(2,1)}, bf16[192,192]{1,0:T(8,128)(2,1)S(1)}, u32[]{:S(2)}, u32[]{:S(2)}) collective-permute-start(bf16[192,192]{1,0:T(8,128)(2,1)} %get-tuple-element.25), channel_id=1, source_target_pairs={{0,6},{1,7},{2,4},{3,5},{4,2},{5,3},{6,0},{7,1},{8,14},{9,15},{10,... | collective-permute-start | bytes 221192 | tf_op jit(solution)/shard_map/ppermute | solution.py:235
  45.3 2.2 %collective-permute-done.28.refs_25_ = bf16[192,192]{1,0:T(8,128)(2,1)S(1)} collective-permute-done((bf16[192,192]{1,0:T(8,128)(2,1)}, bf16[192,192]{1,0:T(8,128)(2,1)S(1)}, u32[]{:S(2)}, u32[]{:S(2)}) %collective-permute-start.28) | collective-permute-done | bytes 73760 | tf_op jit(solution)/shard_map/ppermute | solution.py:235
  47.6 1.7 %collective-permute-done.30.refs_27_ = bf16[192,192]{1,0:T(8,128)(2,1)S(1)} collective-permute-done((bf16[192,192]{1,0:T(8,128)(2,1)}, bf16[192,192]{1,0:T(8,128)(2,1)S(1)}, u32[]{:S(2)}, u32[]{:S(2)}) %collective-permute-start.30) | collective-permute-done | bytes 73760 | tf_op jit(solution)/shard_map/ppermute | solution.py:235
  50.1 14.5 %shard_map.97 = (bf16[192,192]{1,0:T(8,128)(2,1)}, bf16[192,192]{1,0:T(8,128)(2,1)}, bf16[192,192]{1,0:T(8,128)(2,1)}, bf16[192,192]{1,0:T(8,128)(2,1)}, bf16[4,...) custom-call(s32[1]{0:T(128)S(6)} %copy.10.count, bf16[96,768]{1,0:T(8,128)(2,1)} %copy-done.1, bf16[96,768]{1,0:T(8,128)(2,1)} %copy-done, ...), custom_call_target="tpu_custom_call" | custom-call | tf_op jit(solution)/shard_map/pallas_call | solution.py:281
  64.7 1.6 %collective-permute-done.34 = bf16[4,96,192]{2,1,0:T(8,128)(2,1)S(1)} collective-permute-done((bf16[4,96,192]{2,1,0:T(8,128)(2,1)}, bf16[4,96,192]{2,1,0:T(8,128)(2,1)S(1)}, u32[]{:S(2)}, u32[]{:S(2)}) %collective-permute-start.34) | collective-permute-done | bytes 147488 | tf_op jit(solution)/shard_map/ppermute | solution.py:235
  67.3 3.5 %collective-permute-start.37 = (bf16[96,192]{1,0:T(8,128)(2,1)S(1)}, bf16[96,192]{1,0:T(8,128)(2,1)S(1)}, u32[]{:S(2)}, u32[]{:S(2)}) collective-permute-start(bf16[96,192]{1,0:T(8,128)(2,1)S(1)} %get-tuple-element.39), channel_id=1, source_target_pairs={{0,24},{8,16},{16,8},{24,0},{1,25},{9,17},{17,9},{25,1},{2,26},{10... | collective-permute-start | bytes 110600 | tf_op jit(solution)/shard_map/ppermute | solution.py:305
  71.8 1.5 %collective-permute-start.31 = (bf16[192,192]{1,0:T(8,128)(2,1)}, bf16[192,192]{1,0:T(8,128)(2,1)S(1)}, u32[]{:S(2)}, u32[]{:S(2)}) collective-permute-start(bf16[192,192]{1,0:T(8,128)(2,1)} %get-tuple-element.27), channel_id=1, source_target_pairs={{0,2},{1,3},{2,0},{3,1},{4,6},{5,7},{6,4},{7,5},{8,10},{9,11},{10,... | collective-permute-start | bytes 221192 | tf_op jit(solution)/shard_map/ppermute | solution.py:235
  75.9 3.4 %collective-permute-start.38 = (bf16[96,192]{1,0:T(8,128)(2,1)S(1)}, bf16[96,192]{1,0:T(8,128)(2,1)S(1)}, u32[]{:S(2)}, u32[]{:S(2)}) collective-permute-start(bf16[96,192]{1,0:T(8,128)(2,1)S(1)} %fusion.2), channel_id=1, source_target_pairs={{0,24},{1,25},{2,26},{3,27},{4,28},{5,29},{6,30},{7,31},{8,18},{9,... | collective-permute-start | bytes 110600 | tf_op jit(solution)/shard_map/ppermute | solution.py:313
  79.3 2.3 %collective-permute-start.40 = (bf16[96,192]{1,0:T(8,128)(2,1)S(1)}, bf16[96,192]{1,0:T(8,128)(2,1)S(1)}, u32[]{:S(2)}, u32[]{:S(2)}) collective-permute-start(bf16[96,192]{1,0:T(8,128)(2,1)S(1)} %fusion.2), channel_id=1, source_target_pairs={{0,8},{1,9},{2,10},{3,11},{4,12},{5,13},{6,14},{7,15},{8,2},{9,3},... | collective-permute-start | bytes 110600 | tf_op jit(solution)/shard_map/ppermute | solution.py:313
  83.0 2.6 %shard_map.98 = bf16[1,192,768]{2,1,0:T(8,128)(2,1)} custom-call(bf16[4,192,768]{2,1,0:T(8,128)(2,1)} %get-tuple-element.17.wout, bf16[192,192]{1,0:T(8,128)(2,1)} %get-tuple-element.26.refs_0_, bf16[192,192]{1,0:T(8,128)(2,1)} %copy-done.30, bf16[192,192]{1,0:T(8,128)(2,1)} %copy-done.31, bf16[192,192]{1,0:T(8,128)(2,1)} %copy-done.32), custom_call_target="tpu_custom_call" | custom-call | tf_op jit(solution)/shard_map/pallas_call | solution.py:294
  (142 shorter events, 19.0 us)
Async XLA Ops:
  2.8 8.1 %collective-permute-start.21 = (bf16[3,104,192]{2,1,0:T(8,128)(2,1)}, bf16[3,104,192]{2,1,0:T(8,128)(2,1)S(1)}, u32[]{:S(2)}, u32[]{:S(2)}) collective-permute-start(bf16[3,104,192]{2,1,0:T(8,128)(2,1)} %get-tuple-element.19), channel_id=1, source_target_pairs={{0,2},{1,3},{2,0},{3,1},{4,6},{5,7},{6,4},{7,5},{8,10},{9,11},{10,... | collective-permute-start | bytes 359432 | tf_op jit(solution)/shard_map/ppermute | solution.py:235
  5.8 10.2 %collective-permute-start.22 = (bf16[3,104,192]{2,1,0:T(8,128)(2,1)}, bf16[3,104,192]{2,1,0:T(8,128)(2,1)S(1)}, u32[]{:S(2)}, u32[]{:S(2)}) collective-permute-start(bf16[3,104,192]{2,1,0:T(8,128)(2,1)} %get-tuple-element.20), channel_id=1, source_target_pairs={{0,4},{1,5},{2,6},{3,7},{4,0},{5,1},{6,2},{7,3},{8,12},{9,13},{10,... | collective-permute-start | bytes 359432 | tf_op jit(solution)/shard_map/ppermute | solution.py:235
  7.3 8.7 %collective-permute-start.23 = (bf16[3,104,192]{2,1,0:T(8,128)(2,1)}, bf16[3,104,192]{2,1,0:T(8,128)(2,1)S(1)}, u32[]{:S(2)}, u32[]{:S(2)}) collective-permute-start(bf16[3,104,192]{2,1,0:T(8,128)(2,1)} %get-tuple-element.21), channel_id=1, source_target_pairs={{0,6},{1,7},{2,4},{3,5},{4,2},{5,3},{6,0},{7,1},{8,14},{9,15},{10,... | collective-permute-start | bytes 359432 | tf_op jit(solution)/shard_map/ppermute | solution.py:235
  7.3 11.7 %collective-permute-start = (bf16[96,768]{1,0:T(8,128)(2,1)}, bf16[96,768]{1,0:T(8,128)(2,1)S(1)}, u32[]{:S(2)}, u32[]{:S(2)}) collective-permute-start(bf16[96,768]{1,0:T(8,128)(2,1)} %refs_0_.1), channel_id=1, source_target_pairs={{0,2},{1,3},{2,0},{3,1},{4,6},{5,7},{6,4},{7,5},{8,10},{9,11},{10,... | collective-permute-start | bytes 442376 | tf_op jit(solution)/shard_map/ppermute | solution.py:235
  9.3 12.0 %collective-permute-start.1 = (bf16[96,768]{1,0:T(8,128)(2,1)}, bf16[96,768]{1,0:T(8,128)(2,1)S(1)}, u32[]{:S(2)}, u32[]{:S(2)}) collective-permute-start(bf16[96,768]{1,0:T(8,128)(2,1)} %refs_0_.1), channel_id=1, source_target_pairs={{0,4},{1,5},{2,6},{3,7},{4,0},{5,1},{6,2},{7,3},{8,12},{9,13},{10,... | collective-permute-start | bytes 442376 | tf_op jit(solution)/shard_map/ppermute | solution.py:235
  10.9 11.9 %collective-permute-start.2 = (bf16[96,768]{1,0:T(8,128)(2,1)}, bf16[96,768]{1,0:T(8,128)(2,1)S(1)}, u32[]{:S(2)}, u32[]{:S(2)}) collective-permute-start(bf16[96,768]{1,0:T(8,128)(2,1)} %refs_0_.1), channel_id=1, source_target_pairs={{0,6},{1,7},{2,4},{3,5},{4,2},{5,3},{6,0},{7,1},{8,14},{9,15},{10,... | collective-permute-start | bytes 442376 | tf_op jit(solution)/shard_map/ppermute | solution.py:235
  16.0 7.3 %collective-permute-start.3 = (bf16[96,768]{1,0:T(8,128)(2,1)}, bf16[96,768]{1,0:T(8,128)(2,1)S(1)}, u32[]{:S(2)}, u32[]{:S(2)}) collective-permute-start(bf16[96,768]{1,0:T(8,128)(2,1)} %refs_0_.1), channel_id=1, source_target_pairs={{0,1},{1,0},{2,3},{3,2},{4,5},{5,4},{6,7},{7,6},{8,9},{9,8},{10,11... | collective-permute-start | bytes 442376 | tf_op jit(solution)/shard_map/ppermute | solution.py:235
  17.8 6.7 %collective-permute-start.7 = (bf16[96,768]{1,0:T(8,128)(2,1)S(1)}, bf16[96,768]{1,0:T(8,128)(2,1)S(1)}, u32[]{:S(2)}, u32[]{:S(2)}) collective-permute-start(bf16[96,768]{1,0:T(8,128)(2,1)S(1)} %get-tuple-element.33.refs_0_), channel_id=1, source_target_pairs={{0,2},{1,3},{2,0},{3,1},{4,6},{5,7},{6,4},{7,5},{8,10},{9,11},{10,... | collective-permute-start | bytes 442376 | tf_op jit(solution)/shard_map/ppermute | solution.py:235
  19.0 8.1 %collective-permute-start.8 = (bf16[96,768]{1,0:T(8,128)(2,1)S(1)}, bf16[96,768]{1,0:T(8,128)(2,1)S(1)}, u32[]{:S(2)}, u32[]{:S(2)}) collective-permute-start(bf16[96,768]{1,0:T(8,128)(2,1)S(1)} %get-tuple-element.32.refs_1_), channel_id=1, source_target_pairs={{0,2},{1,3},{2,0},{3,1},{4,6},{5,7},{6,4},{7,5},{8,10},{9,11},{10,... | collective-permute-start | bytes 442376 | tf_op jit(solution)/shard_map/ppermute | solution.py:235
  21.3 6.1 %collective-permute-start.9 = (bf16[96,768]{1,0:T(8,128)(2,1)S(1)}, bf16[96,768]{1,0:T(8,128)(2,1)S(1)}, u32[]{:S(2)}, u32[]{:S(2)}) collective-permute-start(bf16[96,768]{1,0:T(8,128)(2,1)S(1)} %get-tuple-element.33.refs_0_), channel_id=1, source_target_pairs={{0,4},{1,5},{2,6},{3,7},{4,0},{5,1},{6,2},{7,3},{8,12},{9,13},{10,... | collective-permute-start | bytes 442376 | tf_op jit(solution)/shard_map/ppermute | solution.py:235
  22.8 6.2 %collective-permute-start.10 = (bf16[96,768]{1,0:T(8,128)(2,1)S(1)}, bf16[96,768]{1,0:T(8,128)(2,1)S(1)}, u32[]{:S(2)}, u32[]{:S(2)}) collective-permute-start(bf16[96,768]{1,0:T(8,128)(2,1)S(1)} %get-tuple-element.32.refs_1_), channel_id=1, source_target_pairs={{0,4},{1,5},{2,6},{3,7},{4,0},{5,1},{6,2},{7,3},{8,12},{9,13},{10,... | collective-permute-start | bytes 442376 | tf_op jit(solution)/shard_map/ppermute | solution.py:235
  32.2 9.6 %collective-permute-start.16 = (bf16[96,768]{1,0:T(8,128)(2,1)S(1)}, bf16[96,768]{1,0:T(8,128)(2,1)S(1)}, u32[]{:S(2)}, u32[]{:S(2)}) collective-permute-start(bf16[96,768]{1,0:T(8,128)(2,1)S(1)} %collective-permute-done.8.refs_3_), channel_id=1, source_target_pairs={{0,1},{1,0},{2,3},{3,2},{4,5},{5,4},{6,7},{7,6},{8,9},{9,8},{10,11... | collective-permute-start | bytes 442376 | tf_op jit(solution)/shard_map/ppermute | solution.py:235
  32.7 9.5 %collective-permute-start.17 = (bf16[96,768]{1,0:T(8,128)(2,1)S(1)}, bf16[96,768]{1,0:T(8,128)(2,1)S(1)}, u32[]{:S(2)}, u32[]{:S(2)}) collective-permute-start(bf16[96,768]{1,0:T(8,128)(2,1)S(1)} %collective-permute-done.9.refs_4_), channel_id=1, source_target_pairs={{0,1},{1,0},{2,3},{3,2},{4,5},{5,4},{6,7},{7,6},{8,9},{9,8},{10,11... | collective-permute-start | bytes 442376 | tf_op jit(solution)/shard_map/ppermute | solution.py:235
  35.9 7.4 %collective-permute-start.18 = (bf16[96,768]{1,0:T(8,128)(2,1)S(1)}, bf16[96,768]{1,0:T(8,128)(2,1)S(1)}, u32[]{:S(2)}, u32[]{:S(2)}) collective-permute-start(bf16[96,768]{1,0:T(8,128)(2,1)S(1)} %collective-permute-done.10.refs_5_), channel_id=1, source_target_pairs={{0,1},{1,0},{2,3},{3,2},{4,5},{5,4},{6,7},{7,6},{8,9},{9,8},{10,11... | collective-permute-start | bytes 442376 | tf_op jit(solution)/shard_map/ppermute | solution.py:235
  37.4 12.0 %collective-permute-start.19 = (bf16[96,768]{1,0:T(8,128)(2,1)S(1)}, bf16[96,768]{1,0:T(8,128)(2,1)S(1)}, u32[]{:S(2)}, u32[]{:S(2)}) collective-permute-start(bf16[96,768]{1,0:T(8,128)(2,1)S(1)} %collective-permute-done.11.refs_6_), channel_id=1, source_target_pairs={{0,1},{1,0},{2,3},{3,2},{4,5},{5,4},{6,7},{7,6},{8,9},{9,8},{10,11... | collective-permute-start | bytes 442376 | tf_op jit(solution)/shard_map/ppermute | solution.py:235
  37.4 11.9 %collective-permute-start.20 = (bf16[96,768]{1,0:T(8,128)(2,1)S(1)}, bf16[96,768]{1,0:T(8,128)(2,1)S(1)}, u32[]{:S(2)}, u32[]{:S(2)}) collective-permute-start(bf16[96,768]{1,0:T(8,128)(2,1)S(1)} %collective-permute-done.12.refs_7_), channel_id=1, source_target_pairs={{0,1},{1,0},{2,3},{3,2},{4,5},{5,4},{6,7},{7,6},{8,9},{9,8},{10,11... | collective-permute-start | bytes 442376 | tf_op jit(solution)/shard_map/ppermute | solution.py:235
  43.3 6.1 %collective-permute-start.30 = (bf16[192,192]{1,0:T(8,128)(2,1)}, bf16[192,192]{1,0:T(8,128)(2,1)S(1)}, u32[]{:S(2)}, u32[]{:S(2)}) collective-permute-start(bf16[192,192]{1,0:T(8,128)(2,1)} %get-tuple-element.25), channel_id=1, source_target_pairs={{0,6},{1,7},{2,4},{3,5},{4,2},{5,3},{6,0},{7,1},{8,14},{9,15},{10,... | collective-permute-start | bytes 221192 | tf_op jit(solution)/shard_map/ppermute | solution.py:235
  67.3 7.0 %collective-permute-start.37 = (bf16[96,192]{1,0:T(8,128)(2,1)S(1)}, bf16[96,192]{1,0:T(8,128)(2,1)S(1)}, u32[]{:S(2)}, u32[]{:S(2)}) collective-permute-start(bf16[96,192]{1,0:T(8,128)(2,1)S(1)} %get-tuple-element.39), channel_id=1, source_target_pairs={{0,24},{8,16},{16,8},{24,0},{1,25},{9,17},{17,9},{25,1},{2,26},{10... | collective-permute-start | bytes 110600 | tf_op jit(solution)/shard_map/ppermute | solution.py:305
  71.8 7.5 %collective-permute-start.31 = (bf16[192,192]{1,0:T(8,128)(2,1)}, bf16[192,192]{1,0:T(8,128)(2,1)S(1)}, u32[]{:S(2)}, u32[]{:S(2)}) collective-permute-start(bf16[192,192]{1,0:T(8,128)(2,1)} %get-tuple-element.27), channel_id=1, source_target_pairs={{0,2},{1,3},{2,0},{3,1},{4,6},{5,7},{6,4},{7,5},{8,10},{9,11},{10,... | collective-permute-start | bytes 221192 | tf_op jit(solution)/shard_map/ppermute | solution.py:235
  73.3 8.4 %collective-permute-start.32 = (bf16[192,192]{1,0:T(8,128)(2,1)}, bf16[192,192]{1,0:T(8,128)(2,1)S(1)}, u32[]{:S(2)}, u32[]{:S(2)}) collective-permute-start(bf16[192,192]{1,0:T(8,128)(2,1)} %get-tuple-element.28), channel_id=1, source_target_pairs={{0,4},{1,5},{2,6},{3,7},{4,0},{5,1},{6,2},{7,3},{8,12},{9,13},{10,... | collective-permute-start | bytes 221192 | tf_op jit(solution)/shard_map/ppermute | solution.py:235
  74.3 8.0 %collective-permute-start.33 = (bf16[192,192]{1,0:T(8,128)(2,1)}, bf16[192,192]{1,0:T(8,128)(2,1)S(1)}, u32[]{:S(2)}, u32[]{:S(2)}) collective-permute-start(bf16[192,192]{1,0:T(8,128)(2,1)} %get-tuple-element.29), channel_id=1, source_target_pairs={{0,6},{1,7},{2,4},{3,5},{4,2},{5,3},{6,0},{7,1},{8,14},{9,15},{10,... | collective-permute-start | bytes 221192 | tf_op jit(solution)/shard_map/ppermute | solution.py:235
  75.9 9.7 %collective-permute-start.38 = (bf16[96,192]{1,0:T(8,128)(2,1)S(1)}, bf16[96,192]{1,0:T(8,128)(2,1)S(1)}, u32[]{:S(2)}, u32[]{:S(2)}) collective-permute-start(bf16[96,192]{1,0:T(8,128)(2,1)S(1)} %fusion.2), channel_id=1, source_target_pairs={{0,24},{1,25},{2,26},{3,27},{4,28},{5,29},{6,30},{7,31},{8,18},{9,... | collective-permute-start | bytes 110600 | tf_op jit(solution)/shard_map/ppermute | solution.py:313
  79.3 6.2 %collective-permute-start.39 = (bf16[96,192]{1,0:T(8,128)(2,1)S(1)}, bf16[96,192]{1,0:T(8,128)(2,1)S(1)}, u32[]{:S(2)}, u32[]{:S(2)}) collective-permute-start(bf16[96,192]{1,0:T(8,128)(2,1)S(1)} %fusion.2), channel_id=1, source_target_pairs={{0,16},{1,17},{2,18},{3,19},{4,20},{5,21},{6,22},{7,23},{8,26},{9,... | collective-permute-start | bytes 110600 | tf_op jit(solution)/shard_map/ppermute | solution.py:313
  79.3 6.2 %collective-permute-start.40 = (bf16[96,192]{1,0:T(8,128)(2,1)S(1)}, bf16[96,192]{1,0:T(8,128)(2,1)S(1)}, u32[]{:S(2)}, u32[]{:S(2)}) collective-permute-start(bf16[96,192]{1,0:T(8,128)(2,1)S(1)} %fusion.2), channel_id=1, source_target_pairs={{0,8},{1,9},{2,10},{3,11},{4,12},{5,13},{6,14},{7,15},{8,2},{9,3},... | collective-permute-start | bytes 110600 | tf_op jit(solution)/shard_map/ppermute | solution.py:313
  (54 other events, 598.1 us)
where the time goes:
time: 88 us; the launch traced here: 86.5 us
  starting transfers between devices  38 us (43%)
  Pallas kernels  22.3 us (25%)
  waiting for transfers between devices  20.2 us (23%)
  local copies, waits for them, and re-layouts  2.24 us (3%)
  other arithmetic  1.87 us (2%)
  between operations  1.79 us (2%)
    ppermute x35, starting transfers between devices, hop(): return lax.ppermute(x, 'seq', [(s, s ^ step) for s in range(n)])  27.1 us
    ppermute x35, waiting for transfers between devices, hop(): return lax.ppermute(x, 'seq', [(s, s ^ step) for s in range(n)])  19.7 us
    pallas_call x1, Pallas kernels, local(): main_call(hg, tg, parts, rows, width, wr, cw, head_dim, by_dp)  14.5 us
    ppermute x4, starting transfers between devices, local(): parts.append(lax.ppermute(mine, ('dp', 'seq'), pairs))  6.4 us
    ppermute x3, starting transfers between devices, local(): got = lax.ppermute(summed[m], 'dp', [(z, z ^ m) for z in range(dp)])  4.45 us
    pallas_call x1, Pallas kernels, local(): pl.pallas_call(functools.partial(dout_kernel, hg, tg, wr), out_shape=[jax...  3.11 us
    pallas_call x1, Pallas kernels, local(): pl.pallas_call(functools.partial(proj_kernel, hg), out_shape=jax.ShapeDty...  2.56 us
    pallas_call x1, Pallas kernels, local(): pl.pallas_call(functools.partial(pack_kernel, hg, tg, wr, cw), out_shape=...  2.17 us
  transfers between devices with their start and end apart: 42, of which 14 were waited for; matrix products, arithmetic and copies ran while one was open for 1% of the time, Pallas kernels for 7%

commit v1 on v0

v1 whole, which is shorter than its diff:
```python
import functools
import math

import jax
import jax.numpy as jnp
from jax import lax
from jax.experimental import pallas as pl
from jax.experimental.pallas import tpu as pltpu
from jax.sharding import PartitionSpec as P


HEADS = 12
NEG_BIG = -1e30
LOG2E = 1.4426950408889634


VM = pl.BlockSpec(memory_space=pltpu.VMEM)
ANY = pl.BlockSpec(memory_space=pl.ANY)
SM = pl.BlockSpec(memory_space=pltpu.SMEM)


def dot_last(a, b):
    return lax.dot_general(a, b, (((1,), (1,)), ((), ())), preferred_element_type=jnp.float32)


def dot(a, b):
    return lax.dot_general(a, b, (((1,), (0,)), ((), ())), preferred_element_type=jnp.float32)


def pack_kernel(hg, tg, wr, cw, wq, wk, wv, seg, *outs):
    group = lax.axis_index("seq") // tg
    for k in range(hg):
        for part in range(hg):

            @pl.when((group ^ k) == part)
            def _():
                cols = slice(part * cw, (part + 1) * cw)
                outs[k][0, :wr] = wq[:, cols]
                outs[k][1, :wr] = wk[:, cols]
                outs[k][2, :wr] = wv[:, cols]

        for i in range(3):
            outs[k][i, wr:] = jnp.broadcast_to(seg[...], (8, cw)).astype(jnp.bfloat16)


def place_rows(scratch, pieces, member, wr):
    for tau, piece in enumerate(pieces):
        to = pl.multiple_of((member ^ tau) * wr, wr)
        scratch[pl.ds(to, wr), :] = piece[...].astype(scratch.dtype)
    return scratch[...].astype(jnp.bfloat16)


def proj_kernel(hg, tg, wr, *refs):
    n = hg * tg
    attention, pieces, out, wout = refs[:hg], refs[hg : hg + n], refs[hg + n], refs[hg + n + 1]
    member = lax.axis_index("seq") % tg
    total = None
    for k in range(hg):
        block = place_rows(wout.at[k], pieces[k::hg], member, wr)
        term = dot(attention[k][...], block)
        total = term if total is None else total + term
    out[0] = total.astype(jnp.bfloat16)


def attention_kernel(hg, tg, parts, rows, wr, head_dim, count, *refs):
    n = hg * tg
    refs = list(refs)
    tiles = [[refs.pop(0) for _ in range(parts)] for _ in range(n)]
    packed = [refs.pop(0) for _ in range(n)]
    o_out = [refs.pop(0) for _ in range(hg)]
    scaled_out, p_out = refs.pop(0), refs.pop(0)
    wp_s, w_s, seg_s, col_s, q_s, k_s, v_s, t_s, bias_s, p_s, o_s, sems = refs
    cw = q_s.shape[1]
    own = lax.axis_index("seq")
    group = own // tg
    member = own % tg
    keys = n * rows
    heads = cw // head_dim
    packed_copies = [
        pltpu.make_async_copy(packed[r], wp_s.at[r], sems.at[n * parts + r]) for r in range(n)
    ]
    size = rows // parts
    tile_copies = [
        pltpu.make_async_copy(
            tiles[r][i], t_s.at[pl.ds(r * rows + i * size, size), :], sems.at[r * parts + i]
        )
        for r in range(n)
        for i in range(parts)
    ]
    for copy in packed_copies + tile_copies:
        copy.start()
    for tau in range(tg):
        for k in range(hg):
            r = tau * hg + k
            packed_copies[r].wait()
            source = (group ^ k) * tg + (member ^ tau)
            to = pl.multiple_of(source * wr, wr)
            for i in range(3):
                w_s[i, pl.ds(to, wr), :] = wp_s[r, i, :wr].astype(w_s.dtype)
            line = wp_s[r, 0, wr : wr + 8, :].astype(jnp.float32)[:1]
            at = source * rows + lax.broadcasted_iota(jnp.int32, (1, rows), 1)
            columns = slice(r * rows, (r + 1) * rows)
            seg_s[0:1, columns] = line
            seg_s[1:2, columns] = jnp.where(at < count[0], line, -1.0)
    for copy in tile_copies:
        copy.wait()
    for tau in range(tg):
        at = slice(tau * hg * rows, (tau + 1) * hg * rows)
        block = t_s[at, :]
        if tau == 0:
            q_s[at, :] = dot(block, w_s[0].astype(jnp.bfloat16)).astype(jnp.bfloat16)
        k_s[at, :] = dot(block, w_s[1].astype(jnp.bfloat16)).astype(jnp.bfloat16)
        v_s[at, :] = dot(block, w_s[2].astype(jnp.bfloat16)).astype(jnp.bfloat16)
    scale = head_dim ** (-0.5) * LOG2E
    lane_head = lax.broadcasted_iota(jnp.int32, (rows, cw), 1) // head_dim
    label = seg_s[1:2, :]
    square_row = lax.broadcasted_iota(jnp.int32, (rows, rows), 0)
    square_col = lax.broadcasted_iota(jnp.int32, (rows, rows), 1)
    column = lax.broadcasted_iota(jnp.int32, (1, keys), 1)
    row_at = lax.broadcasted_iota(jnp.int32, (rows, keys), 0)
    col_at = lax.broadcasted_iota(jnp.int32, (rows, keys), 1)
    slots = p_s.shape[0]

    def p_copy(k):
        slot = k % slots
        return pltpu.make_async_copy(p_s.at[slot], p_out.at[k], sems.at[n * parts + n + slot])

    def chunk(k, carry):
        start = k * rows if isinstance(k, int) else pl.multiple_of(k * rows, rows)
        at = pl.ds(start, rows)
        slot = k % slots
        segment = col_s[k]
        in_block = (column >= start) & (column < start + rows) & (label >= 0.0)
        same_value = jnp.where(in_block, 1.0, 0.0)
        other_value = jnp.where(in_block, 0.0, NEG_BIG)
        bias = jnp.where(segment == label, same_value, other_value)
        bias_s[...] = jnp.where(row_at + start == col_at, 1.0, bias)
        q = q_s[at, :]
        scaled = jnp.zeros((rows, cw), jnp.float32)
        if slots < hg:

            @pl.when(k >= slots)
            def _():
                p_copy(k - slots).wait()

        for h in range(heads):
            qh = jnp.where(lane_head == h, q, jnp.zeros_like(q))
            s = dot_last(qh, k_s[...]) * scale + bias_s[...]
            top = jnp.max(s, axis=1, keepdims=True)
            p = jnp.exp2(s - top)
            total = jnp.sum(p, axis=1, keepdims=True)
            p_s[slot, h] = p.astype(jnp.bfloat16)
            scaled = jnp.where(lane_head == h, 1.0 / total, scaled)
        p_copy(k).start()
        acc = jnp.zeros((rows, cw), jnp.float32)
        for h in range(heads):
            acc = jnp.where(lane_head == h, dot(p_s[slot, h], v_s[...]), acc)
        scaled_out[at, :] = scaled
        o_s[at, :] = (acc * scaled).astype(jnp.bfloat16)
        return carry

    for k in range(hg):
        line = jnp.where(square_row == square_col, seg_s[0:1, k * rows : (k + 1) * rows], 0.0)
        col_s[k] = jnp.sum(line, axis=1, keepdims=True)
    if slots == hg:
        for k in range(hg):
            chunk(k, 0)
    else:
        lax.fori_loop(0, hg, chunk, 0)
    for k in range(hg):
        o_out[k][...] = o_s[k * rows : (k + 1) * rows, :]
    for k in range(hg - slots, hg):
        p_copy(k).wait()


def slot_count(hg, keys):
    return hg if keys <= 2048 else 1


def attention_call(hg, tg, parts, rows, width, wr, cw, head_dim):
    n = hg * tg
    keys = n * rows
    heads = cw // head_dim
    bf16 = jnp.bfloat16
    wide = bf16 if wr % 16 == 0 else jnp.float32
    return pl.pallas_call(
        functools.partial(attention_kernel, hg, tg, parts, rows, wr, head_dim),
        out_shape=[jax.ShapeDtypeStruct((rows, cw), bf16)] * hg
        + [
            jax.ShapeDtypeStruct((hg * rows, cw), jnp.float32),
            jax.ShapeDtypeStruct((hg, heads, rows, keys), bf16),
        ],
        in_specs=[SM] + [ANY] * (n * parts + n),
        out_specs=[VM] * (hg + 1) + [ANY],
        scratch_shapes=[
            pltpu.VMEM((n, 3, wr + 8, cw), bf16),
            pltpu.VMEM((3, width, cw), wide),
            pltpu.VMEM((8, keys), jnp.float32),
            pltpu.VMEM((hg, rows, 1), jnp.float32),
            pltpu.VMEM((hg * rows, cw), bf16),
            pltpu.VMEM((keys, cw), bf16),
            pltpu.VMEM((keys, cw), bf16),
            pltpu.VMEM((keys, width), bf16),
            pltpu.VMEM((rows, keys), jnp.float32),
            pltpu.VMEM((slot_count(hg, keys), heads, rows, keys), bf16),
            pltpu.VMEM((hg * rows, cw), bf16),
            pltpu.SemaphoreType.DMA((n * parts + n + hg,)),
        ],
        compiler_params=pltpu.CompilerParams(vmem_limit_bytes=60 * 1024 * 1024),
    )


def gradient_kernel(hg, tg, parts, rows, wr, head_dim, by_dp, count, *refs):
    n = hg * tg
    refs = list(refs)
    tiles = [[refs.pop(0) for _ in range(parts)] for _ in range(n)]
    p_in = refs.pop(0)
    cots = [refs.pop(0) for _ in range(hg)]
    wout_pieces = [refs.pop(0) for _ in range(tg)]
    scaled_in = refs.pop(0)
    g_out = [refs.pop(0) for _ in range(tg)]
    wout_s, t_s, p_s, gt_s, grad_s, sems = refs
    cw = wout_s.shape[0]
    own = lax.axis_index("seq")
    group = own // tg
    member = own % tg
    heads = cw // head_dim
    size = rows // parts
    slots = p_s.shape[0]
    p_copies = [
        pltpu.make_async_copy(
            p_in.at[k], p_s.at[k % slots], sems.at[n * parts + k % slots]
        )
        for k in range(hg)
    ]
    tile_copies = [
        pltpu.make_async_copy(
            tiles[r][i], t_s.at[pl.ds(r * rows + i * size, size), :], sems.at[r * parts + i]
        )
        for r in range(n)
        for i in range(parts)
    ]
    for copy in p_copies[:slots] + tile_copies:
        copy.start()
    wout = place_rows(wout_s, wout_pieces, member, wr)
    iota = lax.broadcasted_iota(jnp.int32, cots[0].shape, 0)
    for k in range(hg):
        position = ((group ^ k) * tg + member) * rows + iota
        masked = jnp.where(position < count[0], cots[k][...].astype(jnp.float32), 0.0)
        dout = dot_last(masked.astype(jnp.bfloat16), wout).astype(jnp.bfloat16)
        scaled = scaled_in[k * rows : (k + 1) * rows, :]
        d = (dout.astype(jnp.float32) * scaled).T.astype(jnp.bfloat16)
        p_copies[k].wait()
        for h in range(heads):
            at = slice(h * head_dim, (h + 1) * head_dim)
            term = dot(d[at, :], p_s[k % slots, h])
            gt_s[at, :] = term if k == 0 else gt_s[at, :] + term
        if k + slots < hg:
            p_copies[k + slots].start()
    for copy in tile_copies:
        copy.wait()
    grad_s[...] = dot(gt_s[...].astype(jnp.bfloat16), t_s[...]).T
    first = lax.axis_index("dp") if by_dp else 0
    for tau in range(tg):
        for m in range(hg):
            to = ((group ^ m ^ first) * tg + (member ^ tau)) * wr
            to = pl.multiple_of(to, wr)
            g_out[tau][m] = grad_s[pl.ds(to, wr), :].astype(jnp.bfloat16)


def gradient_call(hg, tg, parts, rows, width, wr, cw, head_dim, by_dp):
    n = hg * tg
    keys = n * rows
    heads = cw // head_dim
    bf16 = jnp.bfloat16
    wide = bf16 if wr % 16 == 0 else jnp.float32
    return pl.pallas_call(
        functools.partial(gradient_kernel, hg, tg, parts, rows, wr, head_dim, by_dp),
        out_shape=[jax.ShapeDtypeStruct((hg, wr, cw), bf16)] * tg,
        in_specs=[SM] + [ANY] * (n * parts + 1) + [VM] * (hg + tg + 1),
        out_specs=[VM] * tg,
        scratch_shapes=[
            pltpu.VMEM((cw, width), wide),
            pltpu.VMEM((keys, width), bf16),
            pltpu.VMEM((slot_count(hg, keys), heads, rows, keys), bf16),
            pltpu.VMEM((cw, keys), jnp.float32),
            pltpu.VMEM((width, cw), jnp.float32),
            pltpu.SemaphoreType.DMA((n * parts + hg,)),
        ],
        compiler_params=pltpu.CompilerParams(vmem_limit_bytes=60 * 1024 * 1024),
    )


def local(tiles, cotangent, segment_of, tissue_count, w_query, w_key, w_value, w_out):
    rows, width = tiles.shape[1:]
    wr = w_query.shape[0]
    n = lax.axis_size("seq")
    dp = lax.axis_size("dp")
    hg = math.gcd(HEADS, n)
    tg = n // hg
    cw = width // hg
    head_dim = width // HEADS
    by_dp = dp == hg
    own = lax.axis_index("seq")
    group = own // tg
    bf16 = jnp.bfloat16

    def hop(x, step):
        return lax.ppermute(x, "seq", [(s, s ^ step) for s in range(n)])

    def over_groups(pieces):
        return [pieces[0]] + [hop(pieces[k], k * tg) for k in range(1, hg)]

    def over_members(pieces):
        return [pieces] + [[hop(x, tau) for x in pieces] for tau in range(1, tg)]

    def flat(table):
        return [table[tau][k] for tau in range(tg) for k in range(hg)]

    wide = bf16 if wr % 16 == 0 else jnp.float32
    parts = 2 if hg == 4 and rows % 32 == 0 else 1
    segment_line = segment_of.reshape(1, rows)
    packed = pl.pallas_call(
        functools.partial(pack_kernel, hg, tg, wr, cw),
        out_shape=[jax.ShapeDtypeStruct((3, wr + 8, cw), bf16)] * hg,
        in_specs=[VM] * 4,
        out_specs=[VM] * hg,
    )(w_query, w_key, w_value, segment_line)
    weight_table = over_members(over_groups(packed))
    if parts == 2:
        half = rows // 2
        upper, lower = tiles[0, :half], tiles[0, half:]
        first = [hop(upper, tg), hop(lower, tg)]
        second = [hop(upper, 2 * tg), hop(lower, 2 * tg)]
        third = [hop(first[0], 2 * tg), hop(second[1], tg)]
        tile_pieces = [[upper, lower], first, second, third]
    else:
        tile_pieces = [[x] for x in over_groups([tiles[0]] * hg)]
    tile_pieces = tile_pieces + [
        [hop(x, tau) for x in piece]
        for tau in range(1, tg)
        for piece in tile_pieces
    ]
    flat_tiles = [x for piece in tile_pieces for x in piece]
    cots = over_groups([cotangent[0]] * hg)
    wout_table = over_members(over_groups([w_out] * hg))

    *attention, scaled, weights = attention_call(
        hg, tg, parts, rows, width, wr, cw, head_dim
    )(tissue_count, *flat_tiles, *flat(weight_table))
    attention = over_groups(attention)
    grads = gradient_call(hg, tg, parts, rows, width, wr, cw, head_dim, by_dp)(
        tissue_count,
        *flat_tiles,
        weights,
        *cots,
        *[line[0] for line in wout_table],
        scaled,
    )
    summed = grads[0].astype(jnp.float32)
    for tau in range(1, tg):
        summed = summed + hop(grads[tau], tau).astype(jnp.float32)
    summed = summed.astype(bf16)

    layer_rows = pl.pallas_call(
        functools.partial(proj_kernel, hg, tg, wr),
        out_shape=jax.ShapeDtypeStruct((1, rows, width), bf16),
        in_specs=[VM] * (hg + n),
        out_specs=VM,
        scratch_shapes=[pltpu.VMEM((hg, cw, width), wide)],
    )(*attention, *flat(wout_table))

    if by_dp:
        own_dp = lax.axis_index("dp")
        mine = summed[0].astype(jnp.float32)
        for m in range(1, hg):
            got = lax.ppermute(summed[m], "dp", [(z, z ^ m) for z in range(dp)])
            mine = mine + got.astype(jnp.float32)
        mine = mine.astype(bf16)
        pieces = []
        for m in range(dp):
            pairs = [
                (z * n + s, (z ^ m) * n + (s ^ (z * tg))) for z in range(dp) for s in range(n)
            ]
            pieces.append(lax.ppermute(mine, ("dp", "seq"), pairs))
        index = group ^ own_dp
    else:
        total = lax.psum(summed, "dp")
        pieces = over_groups([total[k] for k in range(hg)])
        index = group
    columns = []
    for p in range(hg):
        piece = pieces[0]
        for m in range(1, hg):
            piece = jnp.where((index ^ p) == m, pieces[m], piece)
        columns.append(piece)
    return (layer_rows, jnp.concatenate(columns, axis=1).astype(jnp.float32))


def solution(mesh):
    placed = (
        P("dp", "seq", None),
        P("dp", "seq", None),
        P("dp", "seq", None),
        P("dp"),
        P("seq", None),
        P("seq", None),
        P("seq", None),
        P("seq", None),
    )
    return jax.shard_map(
        local,
        mesh=mesh,
        in_specs=placed,
        out_specs=(P("dp", "seq", None), P("seq", None)),
        check_vma=False,
    )
```

time: 88 us -> 85.2 us (0.968)
  the two profiles are of different devices: /device:TPU:0 before, /device:TPU:24 now
where the time goes in v1:
time: 85.2 us; the launch traced here: 84.9 us
  starting transfers between devices  35.7 us (42%)
  Pallas kernels  25.7 us (30%)
  waiting for transfers between devices  17 us (20%)
  local copies, waits for them, and re-layouts  2.86 us (3%)
  other arithmetic  1.87 us (2%)
  between operations  1.84 us (2%)
    ppermute x35, starting transfers between devices, hop(): return lax.ppermute(x, 'seq', [(s, s ^ step) for s in range(n)])  23.8 us
    ppermute x35, waiting for transfers between devices, hop(): return lax.ppermute(x, 'seq', [(s, s ^ step) for s in range(n)])  15.8 us
    pallas_call x1, Pallas kernels, local(): attention_call(hg, tg, parts, rows, width, wr, cw, head_dim)  13.3 us
    ppermute x4, starting transfers between devices, local(): pieces.append(lax.ppermute(mine, ('dp', 'seq'), pairs))  9.45 us
    pallas_call x1, Pallas kernels, local(): gradient_call(hg, tg, parts, rows, width, wr, cw, head_dim, by_dp)  7.47 us
    pallas_call x1, Pallas kernels, local(): pl.pallas_call(functools.partial(proj_kernel, hg, tg, wr), out_shape=jax....  2.72 us
    ppermute x3, starting transfers between devices, local(): got = lax.ppermute(summed[m], 'dp', [(z, z ^ m) for z in range(dp)])  2.42 us
    pallas_call x1, Pallas kernels, local(): pl.pallas_call(functools.partial(pack_kernel, hg, tg, wr, cw), out_shape=...  2.17 us
  transfers between devices with their start and end apart: 42, of which 11 were waited for; matrix products, arithmetic and copies ran while one was open for 2% of the time, Pallas kernels for 28%

profile of v1, /device:TPU:24, one launch (start us, length us, event | category | flops | bytes accessed | tf_op | source)
XLA Modules:
  0.0 84.9 jit_solution(6048788274150085578)
XLA Ops:
  0.6 2.2 %shard_map.95 = (bf16[3,104,192]{2,1,0:T(8,128)(2,1)}, bf16[3,104,192]{2,1,0:T(8,128)(2,1)}, bf16[3,104,192]{2,1,0:T(8,128)(2,1)}, bf16[3,104,192]{2,1,0:T(8,128)(2,1)}) custom-call(bf16[96,768]{1,0:T(8,128)(2,1)} %wq.1, bf16[96,768]{1,0:T(8,128)(2,1)} %wk.1, bf16[96,768]{1,0:T(8,128)(2,1)} %wv.1, s32[1,192]{1,0:T(1,128)} %bitcast.21), custom_call_target="tpu_custom_call" | custom-call | tf_op jit(solution)/shard_map/pallas_call | solution.py:323
  2.8 1.5 %collective-permute-start.14 = (bf16[3,104,192]{2,1,0:T(8,128)(2,1)}, bf16[3,104,192]{2,1,0:T(8,128)(2,1)S(1)}, u32[]{:S(2)}, u32[]{:S(2)}) collective-permute-start(bf16[3,104,192]{2,1,0:T(8,128)(2,1)} %get-tuple-element.15), channel_id=1, source_target_pairs={{0,2},{1,3},{2,0},{3,1},{4,6},{5,7},{6,4},{7,5},{8,10},{9,11},{10,... | collective-permute-start | bytes 359432 | tf_op jit(solution)/shard_map/ppermute | solution.py:309
  4.3 1.5 %collective-permute-start.15 = (bf16[3,104,192]{2,1,0:T(8,128)(2,1)}, bf16[3,104,192]{2,1,0:T(8,128)(2,1)S(1)}, u32[]{:S(2)}, u32[]{:S(2)}) collective-permute-start(bf16[3,104,192]{2,1,0:T(8,128)(2,1)} %get-tuple-element.16), channel_id=1, source_target_pairs={{0,4},{1,5},{2,6},{3,7},{4,0},{5,1},{6,2},{7,3},{8,12},{9,13},{10,... | collective-permute-start | bytes 359432 | tf_op jit(solution)/shard_map/ppermute | solution.py:309
  7.3 1.5 %collective-permute-start = (bf16[96,768]{1,0:T(8,128)(2,1)S(1)}, bf16[96,768]{1,0:T(8,128)(2,1)S(1)}, u32[]{:S(2)}, u32[]{:S(2)}) collective-permute-start(bf16[96,768]{1,0:T(8,128)(2,1)S(1)} %get-tuple-element.27.refs_0_), channel_id=1, source_target_pairs={{0,2},{1,3},{2,0},{3,1},{4,6},{5,7},{6,4},{7,5},{8,10},{9,11},{10,... | collective-permute-start | bytes 442376 | tf_op jit(solution)/shard_map/ppermute | solution.py:309
  9.9 1.6 %collective-permute-start.1 = (bf16[96,768]{1,0:T(8,128)(2,1)S(1)}, bf16[96,768]{1,0:T(8,128)(2,1)S(1)}, u32[]{:S(2)}, u32[]{:S(2)}) collective-permute-start(bf16[96,768]{1,0:T(8,128)(2,1)S(1)} %get-tuple-element.26.refs_1_), channel_id=1, source_target_pairs={{0,2},{1,3},{2,0},{3,1},{4,6},{5,7},{6,4},{7,5},{8,10},{9,11},{10,... | collective-permute-start | bytes 442376 | tf_op jit(solution)/shard_map/ppermute | solution.py:309
  11.5 1.6 %collective-permute-done.15.refs_18_ = bf16[3,104,192]{2,1,0:T(8,128)(2,1)S(1)} collective-permute-done((bf16[3,104,192]{2,1,0:T(8,128)(2,1)}, bf16[3,104,192]{2,1,0:T(8,128)(2,1)S(1)}, u32[]{:S(2)}, u32[]{:S(2)}) %collective-permute-start.15) | collective-permute-done | bytes 119840 | tf_op jit(solution)/shard_map/ppermute | solution.py:309
  13.1 2.5 %collective-permute-start.2 = (bf16[96,768]{1,0:T(8,128)(2,1)S(1)}, bf16[96,768]{1,0:T(8,128)(2,1)S(1)}, u32[]{:S(2)}, u32[]{:S(2)}) collective-permute-start(bf16[96,768]{1,0:T(8,128)(2,1)S(1)} %get-tuple-element.27.refs_0_), channel_id=1, source_target_pairs={{0,4},{1,5},{2,6},{3,7},{4,0},{5,1},{6,2},{7,3},{8,12},{9,13},{10,... | collective-permute-start | bytes 442376 | tf_op jit(solution)/shard_map/ppermute | solution.py:309
  16.5 2.1 %collective-permute-done.1.refs_3_ = bf16[96,768]{1,0:T(8,128)(2,1)S(1)} collective-permute-done((bf16[96,768]{1,0:T(8,128)(2,1)S(1)}, bf16[96,768]{1,0:T(8,128)(2,1)S(1)}, u32[]{:S(2)}, u32[]{:S(2)}) %collective-permute-start.1) | collective-permute-done | bytes 147488 | tf_op jit(solution)/shard_map/ppermute | solution.py:309
  19.2 1.6 %collective-permute-done.3.refs_5_ = bf16[96,768]{1,0:T(8,128)(2,1)S(1)} collective-permute-done((bf16[96,768]{1,0:T(8,128)(2,1)S(1)}, bf16[96,768]{1,0:T(8,128)(2,1)S(1)}, u32[]{:S(2)}, u32[]{:S(2)}) %collective-permute-start.3) | collective-permute-done | bytes 147488 | tf_op jit(solution)/shard_map/ppermute | solution.py:309
  20.8 1.6 %collective-permute-start.4 = (bf16[96,768]{1,0:T(8,128)(2,1)S(1)}, bf16[96,768]{1,0:T(8,128)(2,1)S(1)}, u32[]{:S(2)}, u32[]{:S(2)}) collective-permute-start(bf16[96,768]{1,0:T(8,128)(2,1)S(1)} %collective-permute-done.refs_2_), channel_id=1, source_target_pairs={{0,4},{1,5},{2,6},{3,7},{4,0},{5,1},{6,2},{7,3},{8,12},{9,13},{10,... | collective-permute-start | bytes 442376 | tf_op jit(solution)/shard_map/ppermute | solution.py:309
  23.2 3.9 %collective-permute-done.4.refs_6_ = bf16[96,768]{1,0:T(8,128)(2,1)S(1)} collective-permute-done((bf16[96,768]{1,0:T(8,128)(2,1)S(1)}, bf16[96,768]{1,0:T(8,128)(2,1)S(1)}, u32[]{:S(2)}, u32[]{:S(2)}) %collective-permute-start.4) | collective-permute-done | bytes 147488 | tf_op jit(solution)/shard_map/ppermute | solution.py:309
  27.0 1.3 %collective-permute-done.5.refs_7_ = bf16[96,768]{1,0:T(8,128)(2,1)S(1)} collective-permute-done((bf16[96,768]{1,0:T(8,128)(2,1)S(1)}, bf16[96,768]{1,0:T(8,128)(2,1)S(1)}, u32[]{:S(2)}, u32[]{:S(2)}) %collective-permute-start.5) | collective-permute-done | bytes 147488 | tf_op jit(solution)/shard_map/ppermute | solution.py:309
  29.2 2.7 %collective-permute-start.33 = (bf16[192,768]{1,0:T(8,128)(2,1)}, bf16[192,768]{1,0:T(8,128)(2,1)S(1)}, u32[]{:S(2)}, u32[]{:S(2)}) collective-permute-start(bf16[192,768]{1,0:T(8,128)(2,1)} %bitcast.19), channel_id=1, source_target_pairs={{0,6},{1,7},{2,4},{3,5},{4,2},{5,3},{6,0},{7,1},{8,14},{9,15},{10,... | collective-permute-start | bytes 884744 | tf_op jit(solution)/shard_map/ppermute | solution.py:309
  33.9 13.3 %shard_map.96 = (bf16[192,192]{1,0:T(8,128)(2,1)}, bf16[192,192]{1,0:T(8,128)(2,1)}, bf16[192,192]{1,0:T(8,128)(2,1)}, bf16[192,192]{1,0:T(8,128)(2,1)}, f32[768...) custom-call(s32[1]{0:T(128)S(6)} %copy.10.count, bf16[96,768]{1,0:T(8,128)(2,1)} %copy-done.1, bf16[96,768]{1,0:T(8,128)(2,1)} %copy-done, ...), custom_call_target="tpu_custom_call" | custom-call | tf_op jit(solution)/shard_map/pallas_call | solution.py:348
  48.3 7.5 %shard_map.98 = (bf16[4,96,192]{2,1,0:T(8,128)(2,1)}, bf16[4,96,192]{2,1,0:T(8,128)(2,1)}) custom-call(s32[1]{0:T(128)S(6)} %copy.10.count, bf16[96,768]{1,0:T(8,128)(2,1)} %copy-done.1, bf16[96,768]{1,0:T(8,128)(2,1)} %copy-done, bf16[96,768]{1,0:T(8,128)(2,1)} %copy-done.4, bf16[96,768]{1,0:T(8,128)(2,1)} %copy-done.5, bf16[96,768]{1,0:T(8,128)(2,1)} %copy-done.6, ...), custom_call_target="tpu_custom_call" | custom-call | tf_op jit(solution)/shard_map/pallas_call | solution.py:352
  56.7 2.3 %collective-permute-start.26 = (bf16[96,768]{1,0:T(8,128)(2,1)S(1)}, bf16[96,768]{1,0:T(8,128)(2,1)S(1)}, u32[]{:S(2)}, u32[]{:S(2)}) collective-permute-start(bf16[96,768]{1,0:T(8,128)(2,1)S(1)} %copy-done.2), channel_id=1, source_target_pairs={{0,6},{1,7},{2,4},{3,5},{4,2},{5,3},{6,0},{7,1},{8,14},{9,15},{10,... | collective-permute-start | bytes 442376 | tf_op jit(solution)/shard_map/ppermute | solution.py:309
  60.1 1.9 %collective-permute-start.36 = (bf16[96,192]{1,0:T(8,128)(2,1)S(1)}, bf16[96,192]{1,0:T(8,128)(2,1)S(1)}, u32[]{:S(2)}, u32[]{:S(2)}) collective-permute-start(bf16[96,192]{1,0:T(8,128)(2,1)S(1)} %get-tuple-element.34), channel_id=1, source_target_pairs={{0,16},{8,24},{16,0},{24,8},{1,17},{9,25},{17,1},{25,9},{2,18},{10... | collective-permute-start | bytes 110600 | tf_op jit(solution)/shard_map/ppermute | solution.py:377
  62.0 3.3 %collective-permute-done.25.refs_6_ = bf16[96,768]{1,0:T(8,128)(2,1)S(1)} collective-permute-done((bf16[96,768]{1,0:T(8,128)(2,1)S(1)}, bf16[96,768]{1,0:T(8,128)(2,1)S(1)}, u32[]{:S(2)}, u32[]{:S(2)}) %collective-permute-start.25) | collective-permute-done | bytes 147488 | tf_op jit(solution)/shard_map/ppermute | solution.py:309
  66.6 1.3 %collective-permute-start.21 = (bf16[192,192]{1,0:T(8,128)(2,1)S(1)}, bf16[192,192]{1,0:T(8,128)(2,1)S(1)}, u32[]{:S(2)}, u32[]{:S(2)}) collective-permute-start(bf16[192,192]{1,0:T(8,128)(2,1)S(1)} %copy-done.35), channel_id=1, source_target_pairs={{0,2},{1,3},{2,0},{3,1},{4,6},{5,7},{6,4},{7,5},{8,10},{9,11},{10,... | collective-permute-start | bytes 221192 | tf_op jit(solution)/shard_map/ppermute | solution.py:309
  69.4 1.7 %collective-permute-start.23 = (bf16[192,192]{1,0:T(8,128)(2,1)S(1)}, bf16[192,192]{1,0:T(8,128)(2,1)S(1)}, u32[]{:S(2)}, u32[]{:S(2)}) collective-permute-start(bf16[192,192]{1,0:T(8,128)(2,1)S(1)} %copy-done.33), channel_id=1, source_target_pairs={{0,6},{1,7},{2,4},{3,5},{4,2},{5,3},{6,0},{7,1},{8,14},{9,15},{10,... | collective-permute-start | bytes 221192 | tf_op jit(solution)/shard_map/ppermute | solution.py:309
  72.4 2.4 %collective-permute-start.39 = (bf16[96,192]{1,0:T(8,128)(2,1)S(1)}, bf16[96,192]{1,0:T(8,128)(2,1)S(1)}, u32[]{:S(2)}, u32[]{:S(2)}) collective-permute-start(bf16[96,192]{1,0:T(8,128)(2,1)S(1)} %fusion.2), channel_id=1, source_target_pairs={{0,16},{1,17},{2,18},{3,19},{4,20},{5,21},{6,22},{7,23},{8,26},{9,... | collective-permute-start | bytes 110600 | tf_op jit(solution)/shard_map/ppermute | solution.py:385
  74.8 1.6 %collective-permute-start.40 = (bf16[96,192]{1,0:T(8,128)(2,1)S(1)}, bf16[96,192]{1,0:T(8,128)(2,1)S(1)}, u32[]{:S(2)}, u32[]{:S(2)}) collective-permute-start(bf16[96,192]{1,0:T(8,128)(2,1)S(1)} %fusion.2), channel_id=1, source_target_pairs={{0,8},{1,9},{2,10},{3,11},{4,12},{5,13},{6,14},{7,15},{8,2},{9,3},... | collective-permute-start | bytes 110600 | tf_op jit(solution)/shard_map/ppermute | solution.py:385
  76.4 4.2 %collective-permute-start.41 = (bf16[96,192]{1,0:T(8,128)(2,1)S(1)}, bf16[96,192]{1,0:T(8,128)(2,1)S(1)}, u32[]{:S(2)}, u32[]{:S(2)}) collective-permute-start(bf16[96,192]{1,0:T(8,128)(2,1)S(1)} %fusion.2), channel_id=1, source_target_pairs={{0,0},{1,1},{2,2},{3,3},{4,4},{5,5},{6,6},{7,7},{8,10},{9,11},{10,... | collective-permute-start | bytes 110600 | tf_op jit(solution)/shard_map/ppermute | solution.py:385
  81.3 2.7 %shard_map.97 = bf16[1,192,768]{2,1,0:T(8,128)(2,1)} custom-call(bf16[192,192]{1,0:T(8,128)(2,1)} %get-tuple-element.18.refs_0_, bf16[192,192]{1,0:T(8,128)(2,1)} %copy-done.30, bf16[192,192]{1,0:T(8,128)(2,1)} %copy-done.31, bf16[192,192]{1,0:T(8,128)(2,1)} %copy-done.32, bf16[96,768]{1,0:T(8,128)(2,1)} %refs_21_.1, ...), custom_call_target="tpu_custom_call" | custom-call | tf_op jit(solution)/shard_map/pallas_call | solution.py:365
  (142 shorter events, 15.4 us)
Async XLA Ops:
  2.8 7.1 %collective-permute-start.14 = (bf16[3,104,192]{2,1,0:T(8,128)(2,1)}, bf16[3,104,192]{2,1,0:T(8,128)(2,1)S(1)}, u32[]{:S(2)}, u32[]{:S(2)}) collective-permute-start(bf16[3,104,192]{2,1,0:T(8,128)(2,1)} %get-tuple-element.15), channel_id=1, source_target_pairs={{0,2},{1,3},{2,0},{3,1},{4,6},{5,7},{6,4},{7,5},{8,10},{9,11},{10,... | collective-permute-start | bytes 359432 | tf_op jit(solution)/shard_map/ppermute | solution.py:309
  4.3 8.8 %collective-permute-start.15 = (bf16[3,104,192]{2,1,0:T(8,128)(2,1)}, bf16[3,104,192]{2,1,0:T(8,128)(2,1)S(1)}, u32[]{:S(2)}, u32[]{:S(2)}) collective-permute-start(bf16[3,104,192]{2,1,0:T(8,128)(2,1)} %get-tuple-element.16), channel_id=1, source_target_pairs={{0,4},{1,5},{2,6},{3,7},{4,0},{5,1},{6,2},{7,3},{8,12},{9,13},{10,... | collective-permute-start | bytes 359432 | tf_op jit(solution)/shard_map/ppermute | solution.py:309
  5.8 9.8 %collective-permute-start.16 = (bf16[3,104,192]{2,1,0:T(8,128)(2,1)}, bf16[3,104,192]{2,1,0:T(8,128)(2,1)S(1)}, u32[]{:S(2)}, u32[]{:S(2)}) collective-permute-start(bf16[3,104,192]{2,1,0:T(8,128)(2,1)} %get-tuple-element.17), channel_id=1, source_target_pairs={{0,6},{1,7},{2,4},{3,5},{4,2},{5,3},{6,0},{7,1},{8,14},{9,15},{10,... | collective-permute-start | bytes 359432 | tf_op jit(solution)/shard_map/ppermute | solution.py:309
  7.3 9.2 %collective-permute-start = (bf16[96,768]{1,0:T(8,128)(2,1)S(1)}, bf16[96,768]{1,0:T(8,128)(2,1)S(1)}, u32[]{:S(2)}, u32[]{:S(2)}) collective-permute-start(bf16[96,768]{1,0:T(8,128)(2,1)S(1)} %get-tuple-element.27.refs_0_), channel_id=1, source_target_pairs={{0,2},{1,3},{2,0},{3,1},{4,6},{5,7},{6,4},{7,5},{8,10},{9,11},{10,... | collective-permute-start | bytes 442376 | tf_op jit(solution)/shard_map/ppermute | solution.py:309
  8.9 6.8 %collective-permute-start.17 = (bf16[3,104,192]{2,1,0:T(8,128)(2,1)}, bf16[3,104,192]{2,1,0:T(8,128)(2,1)S(1)}, u32[]{:S(2)}, u32[]{:S(2)}) collective-permute-start(bf16[3,104,192]{2,1,0:T(8,128)(2,1)} %get-tuple-element.14.refs_16_), channel_id=1, source_target_pairs={{0,1},{1,0},{2,3},{3,2},{4,5},{5,4},{6,7},{7,6},{8,9},{9,8},{10,11... | collective-permute-start | bytes 359432 | tf_op jit(solution)/shard_map/ppermute | solution.py:309
  9.9 8.8 %collective-permute-start.1 = (bf16[96,768]{1,0:T(8,128)(2,1)S(1)}, bf16[96,768]{1,0:T(8,128)(2,1)S(1)}, u32[]{:S(2)}, u32[]{:S(2)}) collective-permute-start(bf16[96,768]{1,0:T(8,128)(2,1)S(1)} %get-tuple-element.26.refs_1_), channel_id=1, source_target_pairs={{0,2},{1,3},{2,0},{3,1},{4,6},{5,7},{6,4},{7,5},{8,10},{9,11},{10,... | collective-permute-start | bytes 442376 | tf_op jit(solution)/shard_map/ppermute | solution.py:309
  28.3 19.0 %collective-permute-start.31 = (bf16[192,768]{1,0:T(8,128)(2,1)}, bf16[192,768]{1,0:T(8,128)(2,1)S(1)}, u32[]{:S(2)}, u32[]{:S(2)}) collective-permute-start(bf16[192,768]{1,0:T(8,128)(2,1)} %bitcast.17), channel_id=1, source_target_pairs={{0,2},{1,3},{2,0},{3,1},{4,6},{5,7},{6,4},{7,5},{8,10},{9,11},{10,... | collective-permute-start | bytes 884744 | tf_op jit(solution)/shard_map/ppermute | solution.py:309
  28.7 18.7 %collective-permute-start.32 = (bf16[192,768]{1,0:T(8,128)(2,1)}, bf16[192,768]{1,0:T(8,128)(2,1)S(1)}, u32[]{:S(2)}, u32[]{:S(2)}) collective-permute-start(bf16[192,768]{1,0:T(8,128)(2,1)} %bitcast.18), channel_id=1, source_target_pairs={{0,4},{1,5},{2,6},{3,7},{4,0},{5,1},{6,2},{7,3},{8,12},{9,13},{10,... | collective-permute-start | bytes 884744 | tf_op jit(solution)/shard_map/ppermute | solution.py:309
  29.2 18.1 %collective-permute-start.33 = (bf16[192,768]{1,0:T(8,128)(2,1)}, bf16[192,768]{1,0:T(8,128)(2,1)S(1)}, u32[]{:S(2)}, u32[]{:S(2)}) collective-permute-start(bf16[192,768]{1,0:T(8,128)(2,1)} %bitcast.19), channel_id=1, source_target_pairs={{0,6},{1,7},{2,4},{3,5},{4,2},{5,3},{6,0},{7,1},{8,14},{9,15},{10,... | collective-permute-start | bytes 884744 | tf_op jit(solution)/shard_map/ppermute | solution.py:309
  31.9 15.4 %collective-permute-start.27 = (bf16[96,768]{1,0:T(8,128)(2,1)}, bf16[96,768]{1,0:T(8,128)(2,1)S(1)}, u32[]{:S(2)}, u32[]{:S(2)}) collective-permute-start(bf16[96,768]{1,0:T(8,128)(2,1)} %refs_21_.1), channel_id=1, source_target_pairs={{0,1},{1,0},{2,3},{3,2},{4,5},{5,4},{6,7},{7,6},{8,9},{9,8},{10,11... | collective-permute-start | bytes 442376 | tf_op jit(solution)/shard_map/ppermute | solution.py:309
  33.3 25.7 %collective-permute-start.24 = (bf16[96,768]{1,0:T(8,128)(2,1)}, bf16[96,768]{1,0:T(8,128)(2,1)}, u32[]{:S(2)}, u32[]{:S(2)}) collective-permute-start(bf16[96,768]{1,0:T(8,128)(2,1)} %refs_21_.1), channel_id=1, source_target_pairs={{0,2},{1,3},{2,0},{3,1},{4,6},{5,7},{6,4},{7,5},{8,10},{9,11},{10,... | collective-permute-start | bytes 442376 | tf_op jit(solution)/shard_map/ppermute | solution.py:309
  56.0 9.3 %collective-permute-start.25 = (bf16[96,768]{1,0:T(8,128)(2,1)S(1)}, bf16[96,768]{1,0:T(8,128)(2,1)S(1)}, u32[]{:S(2)}, u32[]{:S(2)}) collective-permute-start(bf16[96,768]{1,0:T(8,128)(2,1)S(1)} %copy-done.2), channel_id=1, source_target_pairs={{0,4},{1,5},{2,6},{3,7},{4,0},{5,1},{6,2},{7,3},{8,12},{9,13},{10,... | collective-permute-start | bytes 442376 | tf_op jit(solution)/shard_map/ppermute | solution.py:309
  56.7 9.0 %collective-permute-start.26 = (bf16[96,768]{1,0:T(8,128)(2,1)S(1)}, bf16[96,768]{1,0:T(8,128)(2,1)S(1)}, u32[]{:S(2)}, u32[]{:S(2)}) collective-permute-start(bf16[96,768]{1,0:T(8,128)(2,1)S(1)} %copy-done.2), channel_id=1, source_target_pairs={{0,6},{1,7},{2,4},{3,5},{4,2},{5,3},{6,0},{7,1},{8,14},{9,15},{10,... | collective-permute-start | bytes 442376 | tf_op jit(solution)/shard_map/ppermute | solution.py:309
  59.0 6.8 %collective-permute-start.28 = (bf16[96,768]{1,0:T(8,128)(2,1)}, bf16[96,768]{1,0:T(8,128)(2,1)S(1)}, u32[]{:S(2)}, u32[]{:S(2)}) collective-permute-start(bf16[96,768]{1,0:T(8,128)(2,1)} %collective-permute-done.24.refs_5_), channel_id=1, source_target_pairs={{0,1},{1,0},{2,3},{3,2},{4,5},{5,4},{6,7},{7,6},{8,9},{9,8},{10,11... | collective-permute-start | bytes 442376 | tf_op jit(solution)/shard_map/ppermute | solution.py:309
  60.0 6.6 %collective-permute-start.37 = (bf16[96,192]{1,0:T(8,128)(2,1)S(1)}, bf16[96,192]{1,0:T(8,128)(2,1)S(1)}, u32[]{:S(2)}, u32[]{:S(2)}) collective-permute-start(bf16[96,192]{1,0:T(8,128)(2,1)S(1)} %get-tuple-element.33), channel_id=1, source_target_pairs={{0,24},{8,16},{16,8},{24,0},{1,25},{9,17},{17,9},{25,1},{2,26},{10... | collective-permute-start | bytes 110600 | tf_op jit(solution)/shard_map/ppermute | solution.py:377
  60.1 7.8 %collective-permute-start.36 = (bf16[96,192]{1,0:T(8,128)(2,1)S(1)}, bf16[96,192]{1,0:T(8,128)(2,1)S(1)}, u32[]{:S(2)}, u32[]{:S(2)}) collective-permute-start(bf16[96,192]{1,0:T(8,128)(2,1)S(1)} %get-tuple-element.34), channel_id=1, source_target_pairs={{0,16},{8,24},{16,0},{24,8},{1,17},{9,25},{17,1},{25,9},{2,18},{10... | collective-permute-start | bytes 110600 | tf_op jit(solution)/shard_map/ppermute | solution.py:377
  65.8 6.6 %collective-permute-start.30 = (bf16[96,768]{1,0:T(8,128)(2,1)S(1)}, bf16[96,768]{1,0:T(8,128)(2,1)S(1)}, u32[]{:S(2)}, u32[]{:S(2)}) collective-permute-start(bf16[96,768]{1,0:T(8,128)(2,1)S(1)} %collective-permute-done.26.refs_7_), channel_id=1, source_target_pairs={{0,1},{1,0},{2,3},{3,2},{4,5},{5,4},{6,7},{7,6},{8,9},{9,8},{10,11... | collective-permute-start | bytes 442376 | tf_op jit(solution)/shard_map/ppermute | solution.py:309
  66.6 8.2 %collective-permute-start.21 = (bf16[192,192]{1,0:T(8,128)(2,1)S(1)}, bf16[192,192]{1,0:T(8,128)(2,1)S(1)}, u32[]{:S(2)}, u32[]{:S(2)}) collective-permute-start(bf16[192,192]{1,0:T(8,128)(2,1)S(1)} %copy-done.35), channel_id=1, source_target_pairs={{0,2},{1,3},{2,0},{3,1},{4,6},{5,7},{6,4},{7,5},{8,10},{9,11},{10,... | collective-permute-start | bytes 221192 | tf_op jit(solution)/shard_map/ppermute | solution.py:309
  67.8 8.6 %collective-permute-start.22 = (bf16[192,192]{1,0:T(8,128)(2,1)S(1)}, bf16[192,192]{1,0:T(8,128)(2,1)S(1)}, u32[]{:S(2)}, u32[]{:S(2)}) collective-permute-start(bf16[192,192]{1,0:T(8,128)(2,1)S(1)} %copy-done.34), channel_id=1, source_target_pairs={{0,4},{1,5},{2,6},{3,7},{4,0},{5,1},{6,2},{7,3},{8,12},{9,13},{10,... | collective-permute-start | bytes 221192 | tf_op jit(solution)/shard_map/ppermute | solution.py:309
  69.4 11.3 %collective-permute-start.23 = (bf16[192,192]{1,0:T(8,128)(2,1)S(1)}, bf16[192,192]{1,0:T(8,128)(2,1)S(1)}, u32[]{:S(2)}, u32[]{:S(2)}) collective-permute-start(bf16[192,192]{1,0:T(8,128)(2,1)S(1)} %copy-done.33), channel_id=1, source_target_pairs={{0,6},{1,7},{2,4},{3,5},{4,2},{5,3},{6,0},{7,1},{8,14},{9,15},{10,... | collective-permute-start | bytes 221192 | tf_op jit(solution)/shard_map/ppermute | solution.py:309
  71.1 12.9 %collective-permute-start.38 = (bf16[96,192]{1,0:T(8,128)(2,1)S(1)}, bf16[96,192]{1,0:T(8,128)(2,1)S(1)}, u32[]{:S(2)}, u32[]{:S(2)}) collective-permute-start(bf16[96,192]{1,0:T(8,128)(2,1)S(1)} %fusion.2), channel_id=1, source_target_pairs={{0,24},{1,25},{2,26},{3,27},{4,28},{5,29},{6,30},{7,31},{8,18},{9,... | collective-permute-start | bytes 110600 | tf_op jit(solution)/shard_map/ppermute | solution.py:385
  72.4 11.7 %collective-permute-start.39 = (bf16[96,192]{1,0:T(8,128)(2,1)S(1)}, bf16[96,192]{1,0:T(8,128)(2,1)S(1)}, u32[]{:S(2)}, u32[]{:S(2)}) collective-permute-start(bf16[96,192]{1,0:T(8,128)(2,1)S(1)} %fusion.2), channel_id=1, source_target_pairs={{0,16},{1,17},{2,18},{3,19},{4,20},{5,21},{6,22},{7,23},{8,26},{9,... | collective-permute-start | bytes 110600 | tf_op jit(solution)/shard_map/ppermute | solution.py:385
  74.8 9.3 %collective-permute-start.40 = (bf16[96,192]{1,0:T(8,128)(2,1)S(1)}, bf16[96,192]{1,0:T(8,128)(2,1)S(1)}, u32[]{:S(2)}, u32[]{:S(2)}) collective-permute-start(bf16[96,192]{1,0:T(8,128)(2,1)S(1)} %fusion.2), channel_id=1, source_target_pairs={{0,8},{1,9},{2,10},{3,11},{4,12},{5,13},{6,14},{7,15},{8,2},{9,3},... | collective-permute-start | bytes 110600 | tf_op jit(solution)/shard_map/ppermute | solution.py:385
  76.4 7.7 %collective-permute-start.41 = (bf16[96,192]{1,0:T(8,128)(2,1)S(1)}, bf16[96,192]{1,0:T(8,128)(2,1)S(1)}, u32[]{:S(2)}, u32[]{:S(2)}) collective-permute-start(bf16[96,192]{1,0:T(8,128)(2,1)S(1)} %fusion.2), channel_id=1, source_target_pairs={{0,0},{1,1},{2,2},{3,3},{4,4},{5,5},{6,6},{7,7},{8,10},{9,11},{10,... | collective-permute-start | bytes 110600 | tf_op jit(solution)/shard_map/ppermute | solution.py:385
  (54 other events, 491.2 us)

commit v2 on v1

--- a/solution.py
+++ b/solution.py
@@ -62,14 +62,18 @@
     out[0] = total.astype(jnp.bfloat16)
 
 
-def attention_kernel(hg, tg, parts, rows, wr, head_dim, count, *refs):
+def attention_kernel(hg, tg, parts, rows, wr, head_dim, resident, count, *refs):
     n = hg * tg
     refs = list(refs)
     tiles = [[refs.pop(0) for _ in range(parts)] for _ in range(n)]
     packed = [refs.pop(0) for _ in range(n)]
     o_out = [refs.pop(0) for _ in range(hg)]
     scaled_out, p_out = refs.pop(0), refs.pop(0)
-    wp_s, w_s, seg_s, col_s, q_s, k_s, v_s, t_s, bias_s, p_s, o_s, sems = refs
+    if resident:
+        p_s, t_s = p_out, refs.pop(0)
+    else:
+        p_s, t_s = refs.pop(0), refs.pop(0)
+    wp_s, w_s, seg_s, col_s, q_s, k_s, v_s, bias_s, o_s, sems = refs
     cw = q_s.shape[1]
     own = lax.axis_index("seq")
     group = own // tg
@@ -151,7 +155,8 @@
             total = jnp.sum(p, axis=1, keepdims=True)
             p_s[slot, h] = p.astype(jnp.bfloat16)
             scaled = jnp.where(lane_head == h, 1.0 / total, scaled)
-        p_copy(k).start()
+        if not resident:
+            p_copy(k).start()
         acc = jnp.zeros((rows, cw), jnp.float32)
         for h in range(heads):
             acc = jnp.where(lane_head == h, dot(p_s[slot, h], v_s[...]), acc)
@@ -170,11 +175,12 @@
     for k in range(hg):
         o_out[k][...] = o_s[k * rows : (k + 1) * rows, :]
     for k in range(hg - slots, hg):
-        p_copy(k).wait()
-
-
-def slot_count(hg, keys):
-    return hg if keys <= 2048 else 1
+        if not resident:
+            p_copy(k).wait()
+
+
+def fits(keys):
+    return keys <= 2048
 
 
 def attention_call(hg, tg, parts, rows, width, wr, cw, head_dim):
@@ -183,16 +189,22 @@
     heads = cw // head_dim
     bf16 = jnp.bfloat16
     wide = bf16 if wr % 16 == 0 else jnp.float32
+    resident = fits(keys)
+    if resident:
+        kept = [pltpu.VMEM((hg, heads, rows, keys), bf16), pltpu.VMEM((keys, width), bf16)]
+        local = []
+    else:
+        kept = [jax.ShapeDtypeStruct((hg, heads, rows, keys), bf16)]
+        local = [pltpu.VMEM((1, heads, rows, keys), bf16), pltpu.VMEM((keys, width), bf16)]
     return pl.pallas_call(
-        functools.partial(attention_kernel, hg, tg, parts, rows, wr, head_dim),
+        functools.partial(attention_kernel, hg, tg, parts, rows, wr, head_dim, resident),
         out_shape=[jax.ShapeDtypeStruct((rows, cw), bf16)] * hg
+        + [jax.ShapeDtypeStruct((hg * rows, cw), jnp.float32)]
+        + kept,
+        in_specs=[SM] + [ANY] * (n * parts + n),
+        out_specs=[VM] * (hg + 1) + [VM if resident else ANY] * len(kept),
+        scratch_shapes=local
         + [
-            jax.ShapeDtypeStruct((hg * rows, cw), jnp.float32),
-            jax.ShapeDtypeStruct((hg, heads, rows, keys), bf16),
-        ],
-        in_specs=[SM] + [ANY] * (n * parts + n),
-        out_specs=[VM] * (hg + 1) + [ANY],
-        scratch_shapes=[
             pltpu.VMEM((n, 3, wr + 8, cw), bf16),
             pltpu.VMEM((3, width, cw), wide),
             pltpu.VMEM((8, keys), jnp.float32),
@@ -200,26 +212,29 @@
             pltpu.VMEM((hg * rows, cw), bf16),
             pltpu.VMEM((keys, cw), bf16),
             pltpu.VMEM((keys, cw), bf16),
-            pltpu.VMEM((keys, width), bf16),
             pltpu.VMEM((rows, keys), jnp.float32),
-            pltpu.VMEM((slot_count(hg, keys), heads, rows, keys), bf16),
             pltpu.VMEM((hg * rows, cw), bf16),
             pltpu.SemaphoreType.DMA((n * parts + n + hg,)),
         ],
-        compiler_params=pltpu.CompilerParams(vmem_limit_bytes=60 * 1024 * 1024),
-    )
-
-
-def gradient_kernel(hg, tg, parts, rows, wr, head_dim, by_dp, count, *refs):
+        compiler_params=pltpu.CompilerParams(vmem_limit_bytes=(40 if resident else 60) * 1024 * 1024),
+    )
+
+
+def gradient_kernel(hg, tg, parts, rows, wr, head_dim, by_dp, resident, count, *refs):
     n = hg * tg
     refs = list(refs)
-    tiles = [[refs.pop(0) for _ in range(parts)] for _ in range(n)]
-    p_in = refs.pop(0)
+    if resident:
+        p_s, t_s = refs.pop(0), refs.pop(0)
+    else:
+        tiles = [[refs.pop(0) for _ in range(parts)] for _ in range(n)]
+        p_in = refs.pop(0)
     cots = [refs.pop(0) for _ in range(hg)]
     wout_pieces = [refs.pop(0) for _ in range(tg)]
     scaled_in = refs.pop(0)
     g_out = [refs.pop(0) for _ in range(tg)]
-    wout_s, t_s, p_s, gt_s, grad_s, sems = refs
+    if not resident:
+        p_s, t_s = refs.pop(0), refs.pop(0)
+    wout_s, gt_s, grad_s, sems = refs
     cw = wout_s.shape[0]
     own = lax.axis_index("seq")
     group = own // tg
@@ -227,19 +242,21 @@
     heads = cw // head_dim
     size = rows // parts
     slots = p_s.shape[0]
-    p_copies = [
-        pltpu.make_async_copy(
-            p_in.at[k], p_s.at[k % slots], sems.at[n * parts + k % slots]
-        )
-        for k in range(hg)
-    ]
-    tile_copies = [
-        pltpu.make_async_copy(
-            tiles[r][i], t_s.at[pl.ds(r * rows + i * size, size), :], sems.at[r * parts + i]
-        )
-        for r in range(n)
-        for i in range(parts)
-    ]
+    p_copies, tile_copies = [], []
+    if not resident:
+        p_copies = [
+            pltpu.make_async_copy(
+                p_in.at[k], p_s.at[k % slots], sems.at[n * parts + k % slots]
+            )
+            for k in range(hg)
+        ]
+        tile_copies = [
+            pltpu.make_async_copy(
+                tiles[r][i], t_s.at[pl.ds(r * rows + i * size, size), :], sems.at[r * parts + i]
+            )
+            for r in range(n)
+            for i in range(parts)
+        ]
     for copy in p_copies[:slots] + tile_copies:
         copy.start()
     wout = place_rows(wout_s, wout_pieces, member, wr)
@@ -250,7 +267,8 @@
         dout = dot_last(masked.astype(jnp.bfloat16), wout).astype(jnp.bfloat16)
         scaled = scaled_in[k * rows : (k + 1) * rows, :]
         d = (dout.astype(jnp.float32) * scaled).T.astype(jnp.bfloat16)
-        p_copies[k].wait()
+        if not resident:
+            p_copies[k].wait()
         for h in range(heads):
             at = slice(h * head_dim, (h + 1) * head_dim)
             term = dot(d[at, :], p_s[k % slots, h])
@@ -274,20 +292,25 @@
     heads = cw // head_dim
     bf16 = jnp.bfloat16
     wide = bf16 if wr % 16 == 0 else jnp.float32
+    resident = fits(keys)
+    local = []
+    if not resident:
+        local = [pltpu.VMEM((1, heads, rows, keys), bf16), pltpu.VMEM((keys, width), bf16)]
     return pl.pallas_call(
-        functools.partial(gradient_kernel, hg, tg, parts, rows, wr, head_dim, by_dp),
+        functools.partial(gradient_kernel, hg, tg, parts, rows, wr, head_dim, by_dp, resident),
         out_shape=[jax.ShapeDtypeStruct((hg, wr, cw), bf16)] * tg,
-        in_specs=[SM] + [ANY] * (n * parts + 1) + [VM] * (hg + tg + 1),
+        in_specs=[SM]
+        + ([VM] * 2 if resident else [ANY] * (n * parts + 1))
+        + [VM] * (hg + tg + 1),
         out_specs=[VM] * tg,
-        scratch_shapes=[
+        scratch_shapes=local
+        + [
             pltpu.VMEM((cw, width), wide),
-            pltpu.VMEM((keys, width), bf16),
-            pltpu.VMEM((slot_count(hg, keys), heads, rows, keys), bf16),
             pltpu.VMEM((cw, keys), jnp.float32),
             pltpu.VMEM((width, cw), jnp.float32),
             pltpu.SemaphoreType.DMA((n * parts + hg,)),
         ],
-        compiler_params=pltpu.CompilerParams(vmem_limit_bytes=60 * 1024 * 1024),
+        compiler_params=pltpu.CompilerParams(vmem_limit_bytes=(40 if resident else 60) * 1024 * 1024),
     )
 
 
@@ -345,14 +368,18 @@
     cots = over_groups([cotangent[0]] * hg)
     wout_table = over_members(over_groups([w_out] * hg))
 
-    *attention, scaled, weights = attention_call(
-        hg, tg, parts, rows, width, wr, cw, head_dim
-    )(tissue_count, *flat_tiles, *flat(weight_table))
+    results = attention_call(hg, tg, parts, rows, width, wr, cw, head_dim)(
+        tissue_count, *flat_tiles, *flat(weight_table)
+    )
+    attention, scaled, kept = results[:hg], results[hg], results[hg + 1 :]
+    if fits(n * rows):
+        kept = [pltpu.with_memory_space_constraint(x, pltpu.VMEM) for x in kept]
+    else:
+        kept = [*flat_tiles, *kept]
     attention = over_groups(attention)
     grads = gradient_call(hg, tg, parts, rows, width, wr, cw, head_dim, by_dp)(
         tissue_count,
-        *flat_tiles,
-        weights,
+        *kept,
         *cots,
         *[line[0] for line in wout_table],
         scaled,

time: 85.2 us -> 85.8 us (level)
  the two profiles are of different devices: /device:TPU:24 before, /device:TPU:0 now
where the time goes in v2:
time: 85.8 us; the launch traced here: 84.5 us
  starting transfers between devices  40 us (47%)
  Pallas kernels  23.5 us (27%)
  waiting for transfers between devices  14 us (16%)
  local copies, waits for them, and re-layouts  4.41 us (5%)
  between operations  1.67 us (2%)
  other arithmetic  0.94 us (1%)
    ppermute x35, starting transfers between devices, hop(): return lax.ppermute(x, 'seq', [(s, s ^ step) for s in range(n)])  26.3 us
    pallas_call x1, Pallas kernels, local(): attention_call(hg, tg, parts, rows, width, wr, cw, head_dim)  14.9 us
    ppermute x35, waiting for transfers between devices, hop(): return lax.ppermute(x, 'seq', [(s, s ^ step) for s in range(n)])  14 us
    ppermute x3, starting transfers between devices, local(): got = lax.ppermute(summed[m], 'dp', [(z, z ^ m) for z in range(dp)])  7.54 us
    ppermute x4, starting transfers between devices, local(): pieces.append(lax.ppermute(mine, ('dp', 'seq'), pairs))  6.19 us
    pallas_call x1, Pallas kernels, local(): gradient_call(hg, tg, parts, rows, width, wr, cw, head_dim, by_dp)  3.63 us
    unnamed x28, local copies, waits for them, and re-layouts  3.4 us
    pallas_call x1, Pallas kernels, local(): pl.pallas_call(functools.partial(proj_kernel, hg, tg, wr), out_shape=jax....  2.72 us
  transfers between devices with their start and end apart: 42, of which 9 were waited for; matrix products, arithmetic and copies ran while one was open for 1% of the time, Pallas kernels for 25%

profile of v2, /device:TPU:0, one launch (start us, length us, event | category | flops | bytes accessed | tf_op | source)
XLA Modules:
  0.0 84.5 jit_solution(670567700821632051)
XLA Ops:
  0.6 2.2 %shard_map.95 = (bf16[3,104,192]{2,1,0:T(8,128)(2,1)}, bf16[3,104,192]{2,1,0:T(8,128)(2,1)}, bf16[3,104,192]{2,1,0:T(8,128)(2,1)}, bf16[3,104,192]{2,1,0:T(8,128)(2,1)}) custom-call(bf16[96,768]{1,0:T(8,128)(2,1)} %wq.1, bf16[96,768]{1,0:T(8,128)(2,1)} %wk.1, bf16[96,768]{1,0:T(8,128)(2,1)} %wv.1, s32[1,192]{1,0:T(1,128)} %bitcast.21), custom_call_target="tpu_custom_call" | custom-call | tf_op jit(solution)/shard_map/pallas_call | solution.py:346
  2.8 3.0 %collective-permute-start.14 = (bf16[3,104,192]{2,1,0:T(8,128)(2,1)}, bf16[3,104,192]{2,1,0:T(8,128)(2,1)S(1)}, u32[]{:S(2)}, u32[]{:S(2)}) collective-permute-start(bf16[3,104,192]{2,1,0:T(8,128)(2,1)} %get-tuple-element.16), channel_id=1, source_target_pairs={{0,2},{1,3},{2,0},{3,1},{4,6},{5,7},{6,4},{7,5},{8,10},{9,11},{10,... | collective-permute-start | bytes 359432 | tf_op jit(solution)/shard_map/ppermute | solution.py:332
  5.8 1.5 %collective-permute-start.15 = (bf16[3,104,192]{2,1,0:T(8,128)(2,1)}, bf16[3,104,192]{2,1,0:T(8,128)(2,1)S(1)}, u32[]{:S(2)}, u32[]{:S(2)}) collective-permute-start(bf16[3,104,192]{2,1,0:T(8,128)(2,1)} %get-tuple-element.17), channel_id=1, source_target_pairs={{0,4},{1,5},{2,6},{3,7},{4,0},{5,1},{6,2},{7,3},{8,12},{9,13},{10,... | collective-permute-start | bytes 359432 | tf_op jit(solution)/shard_map/ppermute | solution.py:332
  8.3 2.0 %collective-permute-start = (bf16[96,768]{1,0:T(8,128)(2,1)S(1)}, bf16[96,768]{1,0:T(8,128)(2,1)S(1)}, u32[]{:S(2)}, u32[]{:S(2)}) collective-permute-start(bf16[96,768]{1,0:T(8,128)(2,1)S(1)} %get-tuple-element.29.refs_0_), channel_id=1, source_target_pairs={{0,2},{1,3},{2,0},{3,1},{4,6},{5,7},{6,4},{7,5},{8,10},{9,11},{10,... | collective-permute-start | bytes 442376 | tf_op jit(solution)/shard_map/ppermute | solution.py:332
  10.9 2.0 %collective-permute-start.3 = (bf16[96,768]{1,0:T(8,128)(2,1)S(1)}, bf16[96,768]{1,0:T(8,128)(2,1)S(1)}, u32[]{:S(2)}, u32[]{:S(2)}) collective-permute-start(bf16[96,768]{1,0:T(8,128)(2,1)S(1)} %get-tuple-element.28.refs_1_), channel_id=1, source_target_pairs={{0,4},{1,5},{2,6},{3,7},{4,0},{5,1},{6,2},{7,3},{8,12},{9,13},{10,... | collective-permute-start | bytes 442376 | tf_op jit(solution)/shard_map/ppermute | solution.py:332
  12.9 2.3 %collective-permute-done.15.refs_18_ = bf16[3,104,192]{2,1,0:T(8,128)(2,1)S(1)} collective-permute-done((bf16[3,104,192]{2,1,0:T(8,128)(2,1)}, bf16[3,104,192]{2,1,0:T(8,128)(2,1)S(1)}, u32[]{:S(2)}, u32[]{:S(2)}) %collective-permute-start.15) | collective-permute-done | bytes 119840 | tf_op jit(solution)/shard_map/ppermute | solution.py:332
  15.1 2.4 %collective-permute-start.2 = (bf16[96,768]{1,0:T(8,128)(2,1)S(1)}, bf16[96,768]{1,0:T(8,128)(2,1)S(1)}, u32[]{:S(2)}, u32[]{:S(2)}) collective-permute-start(bf16[96,768]{1,0:T(8,128)(2,1)S(1)} %get-tuple-element.29.refs_0_), channel_id=1, source_target_pairs={{0,4},{1,5},{2,6},{3,7},{4,0},{5,1},{6,2},{7,3},{8,12},{9,13},{10,... | collective-permute-start | bytes 442376 | tf_op jit(solution)/shard_map/ppermute | solution.py:332
  18.3 3.0 %collective-permute-done.2.refs_4_ = bf16[96,768]{1,0:T(8,128)(2,1)S(1)} collective-permute-done((bf16[96,768]{1,0:T(8,128)(2,1)S(1)}, bf16[96,768]{1,0:T(8,128)(2,1)S(1)}, u32[]{:S(2)}, u32[]{:S(2)}) %collective-permute-start.2) | collective-permute-done | bytes 147488 | tf_op jit(solution)/shard_map/ppermute | solution.py:332
  21.3 1.4 %collective-permute-done.1.refs_3_ = bf16[96,768]{1,0:T(8,128)(2,1)S(1)} collective-permute-done((bf16[96,768]{1,0:T(8,128)(2,1)S(1)}, bf16[96,768]{1,0:T(8,128)(2,1)S(1)}, u32[]{:S(2)}, u32[]{:S(2)}) %collective-permute-start.1) | collective-permute-done | bytes 147488 | tf_op jit(solution)/shard_map/ppermute | solution.py:332
  24.5 4.5 %collective-permute-done.4.refs_6_ = bf16[96,768]{1,0:T(8,128)(2,1)S(1)} collective-permute-done((bf16[96,768]{1,0:T(8,128)(2,1)S(1)}, bf16[96,768]{1,0:T(8,128)(2,1)S(1)}, u32[]{:S(2)}, u32[]{:S(2)}) %collective-permute-start.4) | collective-permute-done | bytes 147488 | tf_op jit(solution)/shard_map/ppermute | solution.py:332
  29.5 1.5 %collective-permute-start.32 = (bf16[192,768]{1,0:T(8,128)(2,1)}, bf16[192,768]{1,0:T(8,128)(2,1)S(1)}, u32[]{:S(2)}, u32[]{:S(2)}) collective-permute-start(bf16[192,768]{1,0:T(8,128)(2,1)} %bitcast.18), channel_id=1, source_target_pairs={{0,4},{1,5},{2,6},{3,7},{4,0},{5,1},{6,2},{7,3},{8,12},{9,13},{10,... | collective-permute-start | bytes 884744 | tf_op jit(solution)/shard_map/ppermute | solution.py:332
  31.0 2.0 %collective-permute-start.33 = (bf16[192,768]{1,0:T(8,128)(2,1)}, bf16[192,768]{1,0:T(8,128)(2,1)S(1)}, u32[]{:S(2)}, u32[]{:S(2)}) collective-permute-start(bf16[192,768]{1,0:T(8,128)(2,1)} %bitcast.19), channel_id=1, source_target_pairs={{0,6},{1,7},{2,4},{3,5},{4,2},{5,3},{6,0},{7,1},{8,14},{9,15},{10,... | collective-permute-start | bytes 884744 | tf_op jit(solution)/shard_map/ppermute | solution.py:332
  35.3 14.9 %shard_map.96 = (bf16[192,192]{1,0:T(8,128)(2,1)S(1)}, bf16[192,192]{1,0:T(8,128)(2,1)S(1)}, bf16[192,192]{1,0:T(8,128)(2,1)S(1)}, bf16[192,192]{1,0:T(8,128)(2,...) custom-call(s32[1]{0:T(128)S(6)} %copy.10.count, ...), custom_call_target="tpu_custom_call" | custom-call | tf_op jit(solution)/shard_map/pallas_call | solution.py:371
  52.2 3.6 %shard_map.98 = (bf16[4,96,192]{2,1,0:T(8,128)(2,1)S(1)}, bf16[4,96,192]{2,1,0:T(8,128)(2,1)S(1)}) custom-call(s32[1]{0:T(128)S(6)} %copy.10.count, bf16[4,3,192,1536]{3,2,1,0:T(8,128)(2,1)S(1)} %get-tuple-element.23.refs_0_, bf16[1536,768]{1,0:T(8,128)(2,1)S(1)} %get-tuple-element.24.refs_1_, bf16[192,768]{1,0:T(8,128)(2,1)S(1)} %bitcast.20, ...), custom_call_target="tpu_custom_call" | custom-call | tf_op jit(solution)/shard_map/pallas_call | solution.py:380
  56.0 1.5 %collective-permute-start.25 = (bf16[96,768]{1,0:T(8,128)(2,1)S(1)}, bf16[96,768]{1,0:T(8,128)(2,1)S(1)}, u32[]{:S(2)}, u32[]{:S(2)}) collective-permute-start(bf16[96,768]{1,0:T(8,128)(2,1)S(1)} %copy-done), channel_id=1, source_target_pairs={{0,4},{1,5},{2,6},{3,7},{4,0},{5,1},{6,2},{7,3},{8,12},{9,13},{10,... | collective-permute-start | bytes 442376 | tf_op jit(solution)/shard_map/ppermute | solution.py:332
  57.5 2.0 %collective-permute-start.26 = (bf16[96,768]{1,0:T(8,128)(2,1)S(1)}, bf16[96,768]{1,0:T(8,128)(2,1)S(1)}, u32[]{:S(2)}, u32[]{:S(2)}) collective-permute-start(bf16[96,768]{1,0:T(8,128)(2,1)S(1)} %copy-done), channel_id=1, source_target_pairs={{0,6},{1,7},{2,4},{3,5},{4,2},{5,3},{6,0},{7,1},{8,14},{9,15},{10,... | collective-permute-start | bytes 442376 | tf_op jit(solution)/shard_map/ppermute | solution.py:332
  59.5 1.5 %collective-permute-start.35 = (bf16[96,192]{1,0:T(8,128)(2,1)S(1)}, bf16[96,192]{1,0:T(8,128)(2,1)S(1)}, u32[]{:S(2)}, u32[]{:S(2)}) collective-permute-start(bf16[96,192]{1,0:T(8,128)(2,1)S(1)} %get-tuple-element.34), channel_id=1, source_target_pairs={{0,8},{8,0},{16,24},{24,16},{1,9},{9,1},{17,25},{25,17},{2,10},{10... | collective-permute-start | bytes 110600 | tf_op jit(solution)/shard_map/ppermute | solution.py:404
  61.0 2.6 %collective-permute-start.36 = (bf16[96,192]{1,0:T(8,128)(2,1)S(1)}, bf16[96,192]{1,0:T(8,128)(2,1)S(1)}, u32[]{:S(2)}, u32[]{:S(2)}) collective-permute-start(bf16[96,192]{1,0:T(8,128)(2,1)S(1)} %get-tuple-element.36), channel_id=1, source_target_pairs={{0,16},{8,24},{16,0},{24,8},{1,17},{9,25},{17,1},{25,9},{2,18},{10... | collective-permute-start | bytes 110600 | tf_op jit(solution)/shard_map/ppermute | solution.py:404
  63.6 1.8 %collective-permute-done.25.refs_6_ = bf16[96,768]{1,0:T(8,128)(2,1)S(1)} collective-permute-done((bf16[96,768]{1,0:T(8,128)(2,1)S(1)}, bf16[96,768]{1,0:T(8,128)(2,1)S(1)}, u32[]{:S(2)}, u32[]{:S(2)}) %collective-permute-start.25) | collective-permute-done | bytes 147488 | tf_op jit(solution)/shard_map/ppermute | solution.py:332
  65.4 3.5 %collective-permute-start.37 = (bf16[96,192]{1,0:T(8,128)(2,1)S(1)}, bf16[96,192]{1,0:T(8,128)(2,1)S(1)}, u32[]{:S(2)}, u32[]{:S(2)}) collective-permute-start(bf16[96,192]{1,0:T(8,128)(2,1)S(1)} %get-tuple-element.35), channel_id=1, source_target_pairs={{0,24},{8,16},{16,8},{24,0},{1,25},{9,17},{17,9},{25,1},{2,26},{10... | collective-permute-start | bytes 110600 | tf_op jit(solution)/shard_map/ppermute | solution.py:404
  69.4 1.9 %collective-permute-start.21 = (bf16[192,192]{1,0:T(8,128)(2,1)S(1)}, bf16[192,192]{1,0:T(8,128)(2,1)S(1)}, u32[]{:S(2)}, u32[]{:S(2)}) collective-permute-start(bf16[192,192]{1,0:T(8,128)(2,1)S(1)} %get-tuple-element.20), channel_id=1, source_target_pairs={{0,2},{1,3},{2,0},{3,1},{4,6},{5,7},{6,4},{7,5},{8,10},{9,11},{10,... | collective-permute-start | bytes 221192 | tf_op jit(solution)/shard_map/ppermute | solution.py:332
  73.9 3.5 %collective-permute-start.38 = (bf16[96,192]{1,0:T(8,128)(2,1)S(1)}, bf16[96,192]{1,0:T(8,128)(2,1)S(1)}, u32[]{:S(2)}, u32[]{:S(2)}) collective-permute-start(bf16[96,192]{1,0:T(8,128)(2,1)S(1)} %fusion.2), channel_id=1, source_target_pairs={{0,24},{1,25},{2,26},{3,27},{4,28},{5,29},{6,30},{7,31},{8,18},{9,... | collective-permute-start | bytes 110600 | tf_op jit(solution)/shard_map/ppermute | solution.py:412
  77.4 2.1 %collective-permute-start.40 = (bf16[96,192]{1,0:T(8,128)(2,1)S(1)}, bf16[96,192]{1,0:T(8,128)(2,1)S(1)}, u32[]{:S(2)}, u32[]{:S(2)}) collective-permute-start(bf16[96,192]{1,0:T(8,128)(2,1)S(1)} %fusion.2), channel_id=1, source_target_pairs={{0,8},{1,9},{2,10},{3,11},{4,12},{5,13},{6,14},{7,15},{8,2},{9,3},... | collective-permute-start | bytes 110600 | tf_op jit(solution)/shard_map/ppermute | solution.py:412
  80.9 2.7 %shard_map.97 = bf16[1,192,768]{2,1,0:T(8,128)(2,1)} custom-call(bf16[192,192]{1,0:T(8,128)(2,1)} %copy-done.4, bf16[192,192]{1,0:T(8,128)(2,1)} %copy-done.11, bf16[192,192]{1,0:T(8,128)(2,1)} %copy-done.12, bf16[192,192]{1,0:T(8,128)(2,1)} %copy-done.13, bf16[96,768]{1,0:T(8,128)(2,1)} %refs_6_.1, bf16[96,768]{1,0:T(8,128)(2,1)} %copy-done.5, ...), custom_call_target="tpu_custom_call" | custom-call | tf_op jit(solution)/shard_map/pallas_call | solution.py:392
  (98 shorter events, 13.7 us)
Async XLA Ops:
  2.8 8.1 %collective-permute-start.14 = (bf16[3,104,192]{2,1,0:T(8,128)(2,1)}, bf16[3,104,192]{2,1,0:T(8,128)(2,1)S(1)}, u32[]{:S(2)}, u32[]{:S(2)}) collective-permute-start(bf16[3,104,192]{2,1,0:T(8,128)(2,1)} %get-tuple-element.16), channel_id=1, source_target_pairs={{0,2},{1,3},{2,0},{3,1},{4,6},{5,7},{6,4},{7,5},{8,10},{9,11},{10,... | collective-permute-start | bytes 359432 | tf_op jit(solution)/shard_map/ppermute | solution.py:332
  5.8 9.4 %collective-permute-start.15 = (bf16[3,104,192]{2,1,0:T(8,128)(2,1)}, bf16[3,104,192]{2,1,0:T(8,128)(2,1)S(1)}, u32[]{:S(2)}, u32[]{:S(2)}) collective-permute-start(bf16[3,104,192]{2,1,0:T(8,128)(2,1)} %get-tuple-element.17), channel_id=1, source_target_pairs={{0,4},{1,5},{2,6},{3,7},{4,0},{5,1},{6,2},{7,3},{8,12},{9,13},{10,... | collective-permute-start | bytes 359432 | tf_op jit(solution)/shard_map/ppermute | solution.py:332
  7.3 10.3 %collective-permute-start.16 = (bf16[3,104,192]{2,1,0:T(8,128)(2,1)}, bf16[3,104,192]{2,1,0:T(8,128)(2,1)S(1)}, u32[]{:S(2)}, u32[]{:S(2)}) collective-permute-start(bf16[3,104,192]{2,1,0:T(8,128)(2,1)} %get-tuple-element.18), channel_id=1, source_target_pairs={{0,6},{1,7},{2,4},{3,5},{4,2},{5,3},{6,0},{7,1},{8,14},{9,15},{10,... | collective-permute-start | bytes 359432 | tf_op jit(solution)/shard_map/ppermute | solution.py:332
  8.3 9.3 %collective-permute-start = (bf16[96,768]{1,0:T(8,128)(2,1)S(1)}, bf16[96,768]{1,0:T(8,128)(2,1)S(1)}, u32[]{:S(2)}, u32[]{:S(2)}) collective-permute-start(bf16[96,768]{1,0:T(8,128)(2,1)S(1)} %get-tuple-element.29.refs_0_), channel_id=1, source_target_pairs={{0,2},{1,3},{2,0},{3,1},{4,6},{5,7},{6,4},{7,5},{8,10},{9,11},{10,... | collective-permute-start | bytes 442376 | tf_op jit(solution)/shard_map/ppermute | solution.py:332
  10.3 7.2 %collective-permute-start.17 = (bf16[3,104,192]{2,1,0:T(8,128)(2,1)}, bf16[3,104,192]{2,1,0:T(8,128)(2,1)S(1)}, u32[]{:S(2)}, u32[]{:S(2)}) collective-permute-start(bf16[3,104,192]{2,1,0:T(8,128)(2,1)} %get-tuple-element.15.refs_16_), channel_id=1, source_target_pairs={{0,1},{1,0},{2,3},{3,2},{4,5},{5,4},{6,7},{7,6},{8,9},{9,8},{10,11... | collective-permute-start | bytes 359432 | tf_op jit(solution)/shard_map/ppermute | solution.py:332
  10.9 7.4 %collective-permute-start.3 = (bf16[96,768]{1,0:T(8,128)(2,1)S(1)}, bf16[96,768]{1,0:T(8,128)(2,1)S(1)}, u32[]{:S(2)}, u32[]{:S(2)}) collective-permute-start(bf16[96,768]{1,0:T(8,128)(2,1)S(1)} %get-tuple-element.28.refs_1_), channel_id=1, source_target_pairs={{0,4},{1,5},{2,6},{3,7},{4,0},{5,1},{6,2},{7,3},{8,12},{9,13},{10,... | collective-permute-start | bytes 442376 | tf_op jit(solution)/shard_map/ppermute | solution.py:332
  22.7 6.3 %collective-permute-start.4 = (bf16[96,768]{1,0:T(8,128)(2,1)S(1)}, bf16[96,768]{1,0:T(8,128)(2,1)S(1)}, u32[]{:S(2)}, u32[]{:S(2)}) collective-permute-start(bf16[96,768]{1,0:T(8,128)(2,1)S(1)} %collective-permute-done.refs_2_), channel_id=1, source_target_pairs={{0,4},{1,5},{2,6},{3,7},{4,0},{5,1},{6,2},{7,3},{8,12},{9,13},{10,... | collective-permute-start | bytes 442376 | tf_op jit(solution)/shard_map/ppermute | solution.py:332
  24.4 6.6 %collective-permute-start.10 = (bf16[96,768]{1,0:T(8,128)(2,1)S(1)}, bf16[96,768]{1,0:T(8,128)(2,1)S(1)}, u32[]{:S(2)}, u32[]{:S(2)}) collective-permute-start(bf16[96,768]{1,0:T(8,128)(2,1)S(1)} %collective-permute-done.2.refs_4_), channel_id=1, source_target_pairs={{0,1},{1,0},{2,3},{3,2},{4,5},{5,4},{6,7},{7,6},{8,9},{9,8},{10,11... | collective-permute-start | bytes 442376 | tf_op jit(solution)/shard_map/ppermute | solution.py:332
  29.5 20.8 %collective-permute-start.31 = (bf16[192,768]{1,0:T(8,128)(2,1)}, bf16[192,768]{1,0:T(8,128)(2,1)S(1)}, u32[]{:S(2)}, u32[]{:S(2)}) collective-permute-start(bf16[192,768]{1,0:T(8,128)(2,1)} %bitcast.17), channel_id=1, source_target_pairs={{0,2},{1,3},{2,0},{3,1},{4,6},{5,7},{6,4},{7,5},{8,10},{9,11},{10,... | collective-permute-start | bytes 884744 | tf_op jit(solution)/shard_map/ppermute | solution.py:332
  29.5 20.8 %collective-permute-start.32 = (bf16[192,768]{1,0:T(8,128)(2,1)}, bf16[192,768]{1,0:T(8,128)(2,1)S(1)}, u32[]{:S(2)}, u32[]{:S(2)}) collective-permute-start(bf16[192,768]{1,0:T(8,128)(2,1)} %bitcast.18), channel_id=1, source_target_pairs={{0,4},{1,5},{2,6},{3,7},{4,0},{5,1},{6,2},{7,3},{8,12},{9,13},{10,... | collective-permute-start | bytes 884744 | tf_op jit(solution)/shard_map/ppermute | solution.py:332
  31.0 19.3 %collective-permute-start.33 = (bf16[192,768]{1,0:T(8,128)(2,1)}, bf16[192,768]{1,0:T(8,128)(2,1)S(1)}, u32[]{:S(2)}, u32[]{:S(2)}) collective-permute-start(bf16[192,768]{1,0:T(8,128)(2,1)} %bitcast.19), channel_id=1, source_target_pairs={{0,6},{1,7},{2,4},{3,5},{4,2},{5,3},{6,0},{7,1},{8,14},{9,15},{10,... | collective-permute-start | bytes 884744 | tf_op jit(solution)/shard_map/ppermute | solution.py:332
  33.0 17.3 %collective-permute-start.27 = (bf16[96,768]{1,0:T(8,128)(2,1)}, bf16[96,768]{1,0:T(8,128)(2,1)S(1)}, u32[]{:S(2)}, u32[]{:S(2)}) collective-permute-start(bf16[96,768]{1,0:T(8,128)(2,1)} %refs_6_.1), channel_id=1, source_target_pairs={{0,1},{1,0},{2,3},{3,2},{4,5},{5,4},{6,7},{7,6},{8,9},{9,8},{10,11... | collective-permute-start | bytes 442376 | tf_op jit(solution)/shard_map/ppermute | solution.py:332
  34.3 25.1 %collective-permute-start.24 = (bf16[96,768]{1,0:T(8,128)(2,1)}, bf16[96,768]{1,0:T(8,128)(2,1)S(1)}, u32[]{:S(2)}, u32[]{:S(2)}) collective-permute-start(bf16[96,768]{1,0:T(8,128)(2,1)} %refs_6_.1), channel_id=1, source_target_pairs={{0,2},{1,3},{2,0},{3,1},{4,6},{5,7},{6,4},{7,5},{8,10},{9,11},{10,... | collective-permute-start | bytes 442376 | tf_op jit(solution)/shard_map/ppermute | solution.py:332
  56.0 9.3 %collective-permute-start.25 = (bf16[96,768]{1,0:T(8,128)(2,1)S(1)}, bf16[96,768]{1,0:T(8,128)(2,1)S(1)}, u32[]{:S(2)}, u32[]{:S(2)}) collective-permute-start(bf16[96,768]{1,0:T(8,128)(2,1)S(1)} %copy-done), channel_id=1, source_target_pairs={{0,4},{1,5},{2,6},{3,7},{4,0},{5,1},{6,2},{7,3},{8,12},{9,13},{10,... | collective-permute-start | bytes 442376 | tf_op jit(solution)/shard_map/ppermute | solution.py:332
  57.5 11.4 %collective-permute-start.26 = (bf16[96,768]{1,0:T(8,128)(2,1)S(1)}, bf16[96,768]{1,0:T(8,128)(2,1)S(1)}, u32[]{:S(2)}, u32[]{:S(2)}) collective-permute-start(bf16[96,768]{1,0:T(8,128)(2,1)S(1)} %copy-done), channel_id=1, source_target_pairs={{0,6},{1,7},{2,4},{3,5},{4,2},{5,3},{6,0},{7,1},{8,14},{9,15},{10,... | collective-permute-start | bytes 442376 | tf_op jit(solution)/shard_map/ppermute | solution.py:332
  59.4 9.5 %collective-permute-start.28 = (bf16[96,768]{1,0:T(8,128)(2,1)S(1)}, bf16[96,768]{1,0:T(8,128)(2,1)S(1)}, u32[]{:S(2)}, u32[]{:S(2)}) collective-permute-start(bf16[96,768]{1,0:T(8,128)(2,1)S(1)} %collective-permute-done.24.refs_5_), channel_id=1, source_target_pairs={{0,1},{1,0},{2,3},{3,2},{4,5},{5,4},{6,7},{7,6},{8,9},{9,8},{10,11... | collective-permute-start | bytes 442376 | tf_op jit(solution)/shard_map/ppermute | solution.py:332
  59.5 9.9 %collective-permute-start.35 = (bf16[96,192]{1,0:T(8,128)(2,1)S(1)}, bf16[96,192]{1,0:T(8,128)(2,1)S(1)}, u32[]{:S(2)}, u32[]{:S(2)}) collective-permute-start(bf16[96,192]{1,0:T(8,128)(2,1)S(1)} %get-tuple-element.34), channel_id=1, source_target_pairs={{0,8},{8,0},{16,24},{24,16},{1,9},{9,1},{17,25},{25,17},{2,10},{10... | collective-permute-start | bytes 110600 | tf_op jit(solution)/shard_map/ppermute | solution.py:404
  61.0 10.3 %collective-permute-start.36 = (bf16[96,192]{1,0:T(8,128)(2,1)S(1)}, bf16[96,192]{1,0:T(8,128)(2,1)S(1)}, u32[]{:S(2)}, u32[]{:S(2)}) collective-permute-start(bf16[96,192]{1,0:T(8,128)(2,1)S(1)} %get-tuple-element.36), channel_id=1, source_target_pairs={{0,16},{8,24},{16,0},{24,8},{1,17},{9,25},{17,1},{25,9},{2,18},{10... | collective-permute-start | bytes 110600 | tf_op jit(solution)/shard_map/ppermute | solution.py:404
  65.4 7.2 %collective-permute-start.37 = (bf16[96,192]{1,0:T(8,128)(2,1)S(1)}, bf16[96,192]{1,0:T(8,128)(2,1)S(1)}, u32[]{:S(2)}, u32[]{:S(2)}) collective-permute-start(bf16[96,192]{1,0:T(8,128)(2,1)S(1)} %get-tuple-element.35), channel_id=1, source_target_pairs={{0,24},{8,16},{16,8},{24,0},{1,25},{9,17},{17,9},{25,1},{2,26},{10... | collective-permute-start | bytes 110600 | tf_op jit(solution)/shard_map/ppermute | solution.py:404
  69.0 8.5 %collective-permute-start.30 = (bf16[96,768]{1,0:T(8,128)(2,1)S(1)}, bf16[96,768]{1,0:T(8,128)(2,1)S(1)}, u32[]{:S(2)}, u32[]{:S(2)}) collective-permute-start(bf16[96,768]{1,0:T(8,128)(2,1)S(1)} %collective-permute-done.26.refs_7_), channel_id=1, source_target_pairs={{0,1},{1,0},{2,3},{3,2},{4,5},{5,4},{6,7},{7,6},{8,9},{9,8},{10,11... | collective-permute-start | bytes 442376 | tf_op jit(solution)/shard_map/ppermute | solution.py:332
  69.4 8.0 %collective-permute-start.21 = (bf16[192,192]{1,0:T(8,128)(2,1)S(1)}, bf16[192,192]{1,0:T(8,128)(2,1)S(1)}, u32[]{:S(2)}, u32[]{:S(2)}) collective-permute-start(bf16[192,192]{1,0:T(8,128)(2,1)S(1)} %get-tuple-element.20), channel_id=1, source_target_pairs={{0,2},{1,3},{2,0},{3,1},{4,6},{5,7},{6,4},{7,5},{8,10},{9,11},{10,... | collective-permute-start | bytes 221192 | tf_op jit(solution)/shard_map/ppermute | solution.py:332
  71.3 8.2 %collective-permute-start.22 = (bf16[192,192]{1,0:T(8,128)(2,1)S(1)}, bf16[192,192]{1,0:T(8,128)(2,1)S(1)}, u32[]{:S(2)}, u32[]{:S(2)}) collective-permute-start(bf16[192,192]{1,0:T(8,128)(2,1)S(1)} %get-tuple-element.21), channel_id=1, source_target_pairs={{0,4},{1,5},{2,6},{3,7},{4,0},{5,1},{6,2},{7,3},{8,12},{9,13},{10,... | collective-permute-start | bytes 221192 | tf_op jit(solution)/shard_map/ppermute | solution.py:332
  72.6 7.6 %collective-permute-start.23 = (bf16[192,192]{1,0:T(8,128)(2,1)S(1)}, bf16[192,192]{1,0:T(8,128)(2,1)S(1)}, u32[]{:S(2)}, u32[]{:S(2)}) collective-permute-start(bf16[192,192]{1,0:T(8,128)(2,1)S(1)} %get-tuple-element.22), channel_id=1, source_target_pairs={{0,6},{1,7},{2,4},{3,5},{4,2},{5,3},{6,0},{7,1},{8,14},{9,15},{10,... | collective-permute-start | bytes 221192 | tf_op jit(solution)/shard_map/ppermute | solution.py:332
  73.9 9.7 %collective-permute-start.38 = (bf16[96,192]{1,0:T(8,128)(2,1)S(1)}, bf16[96,192]{1,0:T(8,128)(2,1)S(1)}, u32[]{:S(2)}, u32[]{:S(2)}) collective-permute-start(bf16[96,192]{1,0:T(8,128)(2,1)S(1)} %fusion.2), channel_id=1, source_target_pairs={{0,24},{1,25},{2,26},{3,27},{4,28},{5,29},{6,30},{7,31},{8,18},{9,... | collective-permute-start | bytes 110600 | tf_op jit(solution)/shard_map/ppermute | solution.py:412
  (32 other events, 206.7 us)

commit v3 on v2

--- a/solution.py
+++ b/solution.py
@@ -73,41 +73,51 @@
         p_s, t_s = p_out, refs.pop(0)
     else:
         p_s, t_s = refs.pop(0), refs.pop(0)
-    wp_s, w_s, seg_s, col_s, q_s, k_s, v_s, bias_s, o_s, sems = refs
+    if not resident:
+        wp_s = refs.pop(0)
+    w_s, seg_s, col_s, q_s, k_s, v_s, bias_s, o_s, sems = refs
     cw = q_s.shape[1]
     own = lax.axis_index("seq")
     group = own // tg
     member = own % tg
     keys = n * rows
     heads = cw // head_dim
-    packed_copies = [
-        pltpu.make_async_copy(packed[r], wp_s.at[r], sems.at[n * parts + r]) for r in range(n)
-    ]
     size = rows // parts
-    tile_copies = [
-        pltpu.make_async_copy(
-            tiles[r][i], t_s.at[pl.ds(r * rows + i * size, size), :], sems.at[r * parts + i]
-        )
-        for r in range(n)
-        for i in range(parts)
-    ]
-    for copy in packed_copies + tile_copies:
-        copy.start()
+    if not resident:
+        packed_copies = [
+            pltpu.make_async_copy(packed[r], wp_s.at[r], sems.at[n * parts + r]) for r in range(n)
+        ]
+        tile_copies = [
+            pltpu.make_async_copy(
+                tiles[r][i], t_s.at[pl.ds(r * rows + i * size, size), :], sems.at[r * parts + i]
+            )
+            for r in range(n)
+            for i in range(parts)
+        ]
+        for copy in packed_copies + tile_copies:
+            copy.start()
     for tau in range(tg):
         for k in range(hg):
             r = tau * hg + k
-            packed_copies[r].wait()
+            piece = packed[r]
+            if not resident:
+                packed_copies[r].wait()
+                piece = wp_s.at[r]
             source = (group ^ k) * tg + (member ^ tau)
             to = pl.multiple_of(source * wr, wr)
             for i in range(3):
-                w_s[i, pl.ds(to, wr), :] = wp_s[r, i, :wr].astype(w_s.dtype)
-            line = wp_s[r, 0, wr : wr + 8, :].astype(jnp.float32)[:1]
+                w_s[i, pl.ds(to, wr), :] = piece[i, :wr].astype(w_s.dtype)
+            line = piece[0, wr : wr + 8, :].astype(jnp.float32)[:1]
             at = source * rows + lax.broadcasted_iota(jnp.int32, (1, rows), 1)
             columns = slice(r * rows, (r + 1) * rows)
             seg_s[0:1, columns] = line
             seg_s[1:2, columns] = jnp.where(at < count[0], line, -1.0)
-    for copy in tile_copies:
-        copy.wait()
+    for r in range(n):
+        for i in range(parts):
+            if resident:
+                t_s[r * rows + i * size : r * rows + (i + 1) * size, :] = tiles[r][i][...]
+            else:
+                tile_copies[r * parts + i].wait()
     for tau in range(tg):
         at = slice(tau * hg * rows, (tau + 1) * hg * rows)
         block = t_s[at, :]
@@ -195,17 +205,20 @@
         local = []
     else:
         kept = [jax.ShapeDtypeStruct((hg, heads, rows, keys), bf16)]
-        local = [pltpu.VMEM((1, heads, rows, keys), bf16), pltpu.VMEM((keys, width), bf16)]
+        local = [
+            pltpu.VMEM((1, heads, rows, keys), bf16),
+            pltpu.VMEM((keys, width), bf16),
+            pltpu.VMEM((n, 3, wr + 8, cw), bf16),
+        ]
     return pl.pallas_call(
         functools.partial(attention_kernel, hg, tg, parts, rows, wr, head_dim, resident),
         out_shape=[jax.ShapeDtypeStruct((rows, cw), bf16)] * hg
         + [jax.ShapeDtypeStruct((hg * rows, cw), jnp.float32)]
         + kept,
-        in_specs=[SM] + [ANY] * (n * parts + n),
+        in_specs=[SM] + [VM if resident else ANY] * (n * parts + n),
         out_specs=[VM] * (hg + 1) + [VM if resident else ANY] * len(kept),
         scratch_shapes=local
         + [
-            pltpu.VMEM((n, 3, wr + 8, cw), bf16),
             pltpu.VMEM((3, width, cw), wide),
             pltpu.VMEM((8, keys), jnp.float32),
             pltpu.VMEM((hg, rows, 1), jnp.float32),
@@ -368,21 +381,24 @@
     cots = over_groups([cotangent[0]] * hg)
     wout_table = over_members(over_groups([w_out] * hg))
 
+    def near_core(arrays):
+        if not fits(n * rows):
+            return arrays
+        return [pltpu.with_memory_space_constraint(x, pltpu.VMEM) for x in arrays]
+
     results = attention_call(hg, tg, parts, rows, width, wr, cw, head_dim)(
-        tissue_count, *flat_tiles, *flat(weight_table)
+        tissue_count, *near_core(flat_tiles), *near_core(flat(weight_table))
     )
     attention, scaled, kept = results[:hg], results[hg], results[hg + 1 :]
-    if fits(n * rows):
-        kept = [pltpu.with_memory_space_constraint(x, pltpu.VMEM) for x in kept]
-    else:
+    if not fits(n * rows):
         kept = [*flat_tiles, *kept]
     attention = over_groups(attention)
     grads = gradient_call(hg, tg, parts, rows, width, wr, cw, head_dim, by_dp)(
         tissue_count,
-        *kept,
-        *cots,
-        *[line[0] for line in wout_table],
-        scaled,
+        *near_core(kept),
+        *near_core(cots),
+        *near_core([line[0] for line in wout_table]),
+        *near_core([scaled]),
     )
     summed = grads[0].astype(jnp.float32)
     for tau in range(1, tg):
@@ -395,7 +411,7 @@
         in_specs=[VM] * (hg + n),
         out_specs=VM,
         scratch_shapes=[pltpu.VMEM((hg, cw, width), wide)],
-    )(*attention, *flat(wout_table))
+    )(*near_core(attention), *near_core(flat(wout_table)))
 
     if by_dp:
         own_dp = lax.axis_index("dp")

time: 85.8 us -> 81 us (0.944)
  the two profiles are of different devices: /device:TPU:0 before, /device:TPU:24 now
where the time goes in v3:
time: 81 us; the launch traced here: 80.8 us
  starting transfers between devices  31.6 us (39%)
  waiting for transfers between devices  26.4 us (33%)
  Pallas kernels  16.6 us (20%)
  local copies, waits for them, and re-layouts  3.8 us (5%)
  between operations  1.5 us (2%)
  other arithmetic  0.93 us (1%)
    ppermute x35, starting transfers between devices, hop(): return lax.ppermute(x, 'seq', [(s, s ^ step) for s in range(n)])  21.5 us
    ppermute x35, waiting for transfers between devices, hop(): return lax.ppermute(x, 'seq', [(s, s ^ step) for s in range(n)])  20.6 us
    pallas_call x1, Pallas kernels, local(): attention_call(hg, tg, parts, rows, width, wr, cw, head_dim)  9.37 us
    ppermute x4, starting transfers between devices, local(): pieces.append(lax.ppermute(mine, ('dp', 'seq'), pairs))  8.62 us
    pallas_call x1, Pallas kernels, local(): gradient_call(hg, tg, parts, rows, width, wr, cw, head_dim, by_dp)  3.81 us
    ppermute x3, waiting for transfers between devices, local(): got = lax.ppermute(summed[m], 'dp', [(z, z ^ m) for z in range(dp)])  3.1 us
    unnamed x8, local copies, waits for them, and re-layouts  2.79 us
    ppermute x4, waiting for transfers between devices, local(): pieces.append(lax.ppermute(mine, ('dp', 'seq'), pairs))  2.65 us
  transfers between devices with their start and end apart: 42, of which 13 were waited for; matrix products, arithmetic and copies ran while one was open for 1% of the time, Pallas kernels for 18%

profile of v3, /device:TPU:24, one launch (start us, length us, event | category | flops | bytes accessed | tf_op | source)
XLA Modules:
  0.0 80.8 jit_solution(3994188172247736008)
XLA Ops:
  0.6 2.2 %shard_map.95 = (bf16[3,104,192]{2,1,0:T(8,128)(2,1)}, bf16[3,104,192]{2,1,0:T(8,128)(2,1)}, bf16[3,104,192]{2,1,0:T(8,128)(2,1)}, bf16[3,104,192]{2,1,0:T(8,128)(2,1)}) custom-call(bf16[96,768]{1,0:T(8,128)(2,1)} %wq.1, bf16[96,768]{1,0:T(8,128)(2,1)} %wk.1, bf16[96,768]{1,0:T(8,128)(2,1)} %wv.1, s32[1,192]{1,0:T(1,128)} %bitcast.21), custom_call_target="tpu_custom_call" | custom-call | tf_op jit(solution)/shard_map/pallas_call | solution.py:359
  2.8 1.5 %collective-permute-start.14 = (bf16[3,104,192]{2,1,0:T(8,128)(2,1)}, bf16[3,104,192]{2,1,0:T(8,128)(2,1)S(1)}, u32[]{:S(2)}, u32[]{:S(2)}) collective-permute-start(bf16[3,104,192]{2,1,0:T(8,128)(2,1)} %get-tuple-element.16), channel_id=1, source_target_pairs={{0,2},{1,3},{2,0},{3,1},{4,6},{5,7},{6,4},{7,5},{8,10},{9,11},{10,... | collective-permute-start | bytes 359432 | tf_op jit(solution)/shard_map/ppermute | solution.py:345
  4.3 1.5 %collective-permute-start.15 = (bf16[3,104,192]{2,1,0:T(8,128)(2,1)}, bf16[3,104,192]{2,1,0:T(8,128)(2,1)S(1)}, u32[]{:S(2)}, u32[]{:S(2)}) collective-permute-start(bf16[3,104,192]{2,1,0:T(8,128)(2,1)} %get-tuple-element.17), channel_id=1, source_target_pairs={{0,4},{1,5},{2,6},{3,7},{4,0},{5,1},{6,2},{7,3},{8,12},{9,13},{10,... | collective-permute-start | bytes 359432 | tf_op jit(solution)/shard_map/ppermute | solution.py:345
  7.3 1.5 %collective-permute-start = (bf16[96,768]{1,0:T(8,128)(2,1)S(1)}, bf16[96,768]{1,0:T(8,128)(2,1)S(1)}, u32[]{:S(2)}, u32[]{:S(2)}) collective-permute-start(bf16[96,768]{1,0:T(8,128)(2,1)S(1)} %get-tuple-element.29.refs_0_), channel_id=1, source_target_pairs={{0,2},{1,3},{2,0},{3,1},{4,6},{5,7},{6,4},{7,5},{8,10},{9,11},{10,... | collective-permute-start | bytes 442376 | tf_op jit(solution)/shard_map/ppermute | solution.py:345
  9.9 1.5 %collective-permute-start.3 = (bf16[96,768]{1,0:T(8,128)(2,1)S(1)}, bf16[96,768]{1,0:T(8,128)(2,1)S(1)}, u32[]{:S(2)}, u32[]{:S(2)}) collective-permute-start(bf16[96,768]{1,0:T(8,128)(2,1)S(1)} %get-tuple-element.28.refs_1_), channel_id=1, source_target_pairs={{0,4},{1,5},{2,6},{3,7},{4,0},{5,1},{6,2},{7,3},{8,12},{9,13},{10,... | collective-permute-start | bytes 442376 | tf_op jit(solution)/shard_map/ppermute | solution.py:345
  11.4 2.1 %collective-permute-done.15.refs_18_ = bf16[3,104,192]{2,1,0:T(8,128)(2,1)S(1)} collective-permute-done((bf16[3,104,192]{2,1,0:T(8,128)(2,1)}, bf16[3,104,192]{2,1,0:T(8,128)(2,1)S(1)}, u32[]{:S(2)}, u32[]{:S(2)}) %collective-permute-start.15) | collective-permute-done | bytes 119840 | tf_op jit(solution)/shard_map/ppermute | solution.py:345
  13.5 2.4 %collective-permute-start.2 = (bf16[96,768]{1,0:T(8,128)(2,1)S(1)}, bf16[96,768]{1,0:T(8,128)(2,1)S(1)}, u32[]{:S(2)}, u32[]{:S(2)}) collective-permute-start(bf16[96,768]{1,0:T(8,128)(2,1)S(1)} %get-tuple-element.29.refs_0_), channel_id=1, source_target_pairs={{0,4},{1,5},{2,6},{3,7},{4,0},{5,1},{6,2},{7,3},{8,12},{9,13},{10,... | collective-permute-start | bytes 442376 | tf_op jit(solution)/shard_map/ppermute | solution.py:345
  17.0 2.8 %collective-permute-done.2.refs_4_ = bf16[96,768]{1,0:T(8,128)(2,1)S(1)} collective-permute-done((bf16[96,768]{1,0:T(8,128)(2,1)S(1)}, bf16[96,768]{1,0:T(8,128)(2,1)S(1)}, u32[]{:S(2)}, u32[]{:S(2)}) %collective-permute-start.2) | collective-permute-done | bytes 147488 | tf_op jit(solution)/shard_map/ppermute | solution.py:345
  19.8 1.2 %collective-permute-done.1.refs_3_ = bf16[96,768]{1,0:T(8,128)(2,1)S(1)} collective-permute-done((bf16[96,768]{1,0:T(8,128)(2,1)S(1)}, bf16[96,768]{1,0:T(8,128)(2,1)S(1)}, u32[]{:S(2)}, u32[]{:S(2)}) %collective-permute-start.1) | collective-permute-done | bytes 147488 | tf_op jit(solution)/shard_map/ppermute | solution.py:345
  23.0 4.3 %collective-permute-done.4.refs_6_ = bf16[96,768]{1,0:T(8,128)(2,1)S(1)} collective-permute-done((bf16[96,768]{1,0:T(8,128)(2,1)S(1)}, bf16[96,768]{1,0:T(8,128)(2,1)S(1)}, u32[]{:S(2)}, u32[]{:S(2)}) %collective-permute-start.4) | collective-permute-done | bytes 147488 | tf_op jit(solution)/shard_map/ppermute | solution.py:345
  27.9 1.4 %collective-permute-start.32 = (bf16[192,768]{1,0:T(8,128)(2,1)}, bf16[192,768]{1,0:T(8,128)(2,1)S(1)}, u32[]{:S(2)}, u32[]{:S(2)}) collective-permute-start(bf16[192,768]{1,0:T(8,128)(2,1)} %bitcast.18), channel_id=1, source_target_pairs={{0,4},{1,5},{2,6},{3,7},{4,0},{5,1},{6,2},{7,3},{8,12},{9,13},{10,... | collective-permute-start | bytes 884744 | tf_op jit(solution)/shard_map/ppermute | solution.py:345
  29.3 2.0 %collective-permute-start.33 = (bf16[192,768]{1,0:T(8,128)(2,1)}, bf16[192,768]{1,0:T(8,128)(2,1)S(1)}, u32[]{:S(2)}, u32[]{:S(2)}) collective-permute-start(bf16[192,768]{1,0:T(8,128)(2,1)} %bitcast.19), channel_id=1, source_target_pairs={{0,6},{1,7},{2,4},{3,5},{4,2},{5,3},{6,0},{7,1},{8,14},{9,15},{10,... | collective-permute-start | bytes 884744 | tf_op jit(solution)/shard_map/ppermute | solution.py:345
  33.7 9.4 %shard_map.96 = (bf16[192,192]{1,0:T(8,128)(2,1)S(1)}, bf16[192,192]{1,0:T(8,128)(2,1)S(1)}, bf16[192,192]{1,0:T(8,128)(2,1)S(1)}, bf16[192,192]{1,0:T(8,128)(2,...) custom-call(s32[1]{0:T(128)S(6)} %copy.10.count, ...), custom_call_target="tpu_custom_call" | custom-call | tf_op jit(solution)/shard_map/pallas_call | solution.py:389
  43.1 1.7 %collective-permute-done.33.refs_5_ = bf16[192,768]{1,0:T(8,128)(2,1)S(1)} collective-permute-done((bf16[192,768]{1,0:T(8,128)(2,1)}, bf16[192,768]{1,0:T(8,128)(2,1)S(1)}, u32[]{:S(2)}, u32[]{:S(2)}) %collective-permute-start.33) | collective-permute-done | bytes 294944 | tf_op jit(solution)/shard_map/ppermute | solution.py:345
  46.7 3.8 %shard_map.98 = (bf16[4,96,192]{2,1,0:T(8,128)(2,1)S(1)}, bf16[4,96,192]{2,1,0:T(8,128)(2,1)S(1)}) custom-call(s32[1]{0:T(128)S(6)} %copy.10.count, bf16[4,3,192,1536]{3,2,1,0:T(8,128)(2,1)S(1)} %get-tuple-element.23.refs_0_, bf16[1536,768]{1,0:T(8,128)(2,1)S(1)} %get-tuple-element.24.refs_1_, bf16[192,768]{1,0:T(8,128)(2,1)S(1)} %bitcast.20, ...), custom_call_target="tpu_custom_call" | custom-call | tf_op jit(solution)/shard_map/pallas_call | solution.py:396
  53.6 6.4 %collective-permute-done.25.refs_6_ = bf16[96,768]{1,0:T(8,128)(2,1)S(1)} collective-permute-done((bf16[96,768]{1,0:T(8,128)(2,1)S(1)}, bf16[96,768]{1,0:T(8,128)(2,1)S(1)}, u32[]{:S(2)}, u32[]{:S(2)}) %collective-permute-start.25) | collective-permute-done | bytes 147488 | tf_op jit(solution)/shard_map/ppermute | solution.py:345
  61.3 1.5 %collective-permute-start.22 = (bf16[192,192]{1,0:T(8,128)(2,1)S(1)}, bf16[192,192]{1,0:T(8,128)(2,1)S(1)}, u32[]{:S(2)}, u32[]{:S(2)}) collective-permute-start(bf16[192,192]{1,0:T(8,128)(2,1)S(1)} %get-tuple-element.21), channel_id=1, source_target_pairs={{0,4},{1,5},{2,6},{3,7},{4,0},{5,1},{6,2},{7,3},{8,12},{9,13},{10,... | collective-permute-start | bytes 221192 | tf_op jit(solution)/shard_map/ppermute | solution.py:345
  62.8 3.1 %collective-permute-done.37 = bf16[96,192]{1,0:T(8,128)(2,1)S(1)} collective-permute-done((bf16[96,192]{1,0:T(8,128)(2,1)S(1)}, bf16[96,192]{1,0:T(8,128)(2,1)S(1)}, u32[]{:S(2)}, u32[]{:S(2)}) %collective-permute-start.37) | collective-permute-done | bytes 36896 | tf_op jit(solution)/shard_map/ppermute | solution.py:420
  65.9 1.3 %collective-permute-start.23 = (bf16[192,192]{1,0:T(8,128)(2,1)S(1)}, bf16[192,192]{1,0:T(8,128)(2,1)S(1)}, u32[]{:S(2)}, u32[]{:S(2)}) collective-permute-start(bf16[192,192]{1,0:T(8,128)(2,1)S(1)} %get-tuple-element.22), channel_id=1, source_target_pairs={{0,6},{1,7},{2,4},{3,5},{4,2},{5,3},{6,0},{7,1},{8,14},{9,15},{10,... | collective-permute-start | bytes 221192 | tf_op jit(solution)/shard_map/ppermute | solution.py:345
  67.3 1.5 %collective-permute-start.38 = (bf16[96,192]{1,0:T(8,128)(2,1)S(1)}, bf16[96,192]{1,0:T(8,128)(2,1)S(1)}, u32[]{:S(2)}, u32[]{:S(2)}) collective-permute-start(bf16[96,192]{1,0:T(8,128)(2,1)S(1)} %fusion.2), channel_id=1, source_target_pairs={{0,24},{1,25},{2,26},{3,27},{4,28},{5,29},{6,30},{7,31},{8,18},{9,... | collective-permute-start | bytes 110600 | tf_op jit(solution)/shard_map/ppermute | solution.py:428
  68.8 4.2 %collective-permute-start.40 = (bf16[96,192]{1,0:T(8,128)(2,1)S(1)}, bf16[96,192]{1,0:T(8,128)(2,1)S(1)}, u32[]{:S(2)}, u32[]{:S(2)}) collective-permute-start(bf16[96,192]{1,0:T(8,128)(2,1)S(1)} %fusion.2), channel_id=1, source_target_pairs={{0,8},{1,9},{2,10},{3,11},{4,12},{5,13},{6,14},{7,15},{8,2},{9,3},... | collective-permute-start | bytes 110600 | tf_op jit(solution)/shard_map/ppermute | solution.py:428
  73.0 2.9 %collective-permute-start.41 = (bf16[96,192]{1,0:T(8,128)(2,1)S(1)}, bf16[96,192]{1,0:T(8,128)(2,1)S(1)}, u32[]{:S(2)}, u32[]{:S(2)}) collective-permute-start(bf16[96,192]{1,0:T(8,128)(2,1)S(1)} %fusion.2), channel_id=1, source_target_pairs={{0,0},{1,1},{2,2},{3,3},{4,4},{5,5},{6,6},{7,7},{8,10},{9,11},{10,... | collective-permute-start | bytes 110600 | tf_op jit(solution)/shard_map/ppermute | solution.py:428
  76.0 1.3 %shard_map.97 = bf16[1,192,768]{2,1,0:T(8,128)(2,1)} custom-call(bf16[192,192]{1,0:T(8,128)(2,1)S(1)} %get-tuple-element.19.refs_0_, bf16[192,192]{1,0:T(8,128)(2,1)S(1)} %collective-permute-done.21.refs_1_, bf16[192,192]{1,0:T(8,128)(2,1)S(1)} %collective-permute-done.22.refs_2_, bf16[192,192]{1,0:T(8,128)(2,1)S(1)} %collective-permute-done.23.refs_3_, ...), custom_call_target="tpu_custom_call" | custom-call | tf_op jit(solution)/shard_map/pallas_call | solution.py:408
  77.3 2.6 %collective-permute-done.41 = bf16[96,192]{1,0:T(8,128)(2,1)S(1)} collective-permute-done((bf16[96,192]{1,0:T(8,128)(2,1)S(1)}, bf16[96,192]{1,0:T(8,128)(2,1)S(1)}, u32[]{:S(2)}, u32[]{:S(2)}) %collective-permute-start.41) | collective-permute-done | bytes 36896 | tf_op jit(solution)/shard_map/ppermute | solution.py:428
  (78 shorter events, 15.2 us)
Async XLA Ops:
  2.8 7.1 %collective-permute-start.14 = (bf16[3,104,192]{2,1,0:T(8,128)(2,1)}, bf16[3,104,192]{2,1,0:T(8,128)(2,1)S(1)}, u32[]{:S(2)}, u32[]{:S(2)}) collective-permute-start(bf16[3,104,192]{2,1,0:T(8,128)(2,1)} %get-tuple-element.16), channel_id=1, source_target_pairs={{0,2},{1,3},{2,0},{3,1},{4,6},{5,7},{6,4},{7,5},{8,10},{9,11},{10,... | collective-permute-start | bytes 359432 | tf_op jit(solution)/shard_map/ppermute | solution.py:345
  4.3 9.2 %collective-permute-start.15 = (bf16[3,104,192]{2,1,0:T(8,128)(2,1)}, bf16[3,104,192]{2,1,0:T(8,128)(2,1)S(1)}, u32[]{:S(2)}, u32[]{:S(2)}) collective-permute-start(bf16[3,104,192]{2,1,0:T(8,128)(2,1)} %get-tuple-element.17), channel_id=1, source_target_pairs={{0,4},{1,5},{2,6},{3,7},{4,0},{5,1},{6,2},{7,3},{8,12},{9,13},{10,... | collective-permute-start | bytes 359432 | tf_op jit(solution)/shard_map/ppermute | solution.py:345
  5.8 10.1 %collective-permute-start.16 = (bf16[3,104,192]{2,1,0:T(8,128)(2,1)}, bf16[3,104,192]{2,1,0:T(8,128)(2,1)S(1)}, u32[]{:S(2)}, u32[]{:S(2)}) collective-permute-start(bf16[3,104,192]{2,1,0:T(8,128)(2,1)} %get-tuple-element.18), channel_id=1, source_target_pairs={{0,6},{1,7},{2,4},{3,5},{4,2},{5,3},{6,0},{7,1},{8,14},{9,15},{10,... | collective-permute-start | bytes 359432 | tf_op jit(solution)/shard_map/ppermute | solution.py:345
  7.3 8.7 %collective-permute-start = (bf16[96,768]{1,0:T(8,128)(2,1)S(1)}, bf16[96,768]{1,0:T(8,128)(2,1)S(1)}, u32[]{:S(2)}, u32[]{:S(2)}) collective-permute-start(bf16[96,768]{1,0:T(8,128)(2,1)S(1)} %get-tuple-element.29.refs_0_), channel_id=1, source_target_pairs={{0,2},{1,3},{2,0},{3,1},{4,6},{5,7},{6,4},{7,5},{8,10},{9,11},{10,... | collective-permute-start | bytes 442376 | tf_op jit(solution)/shard_map/ppermute | solution.py:345
  8.8 7.0 %collective-permute-start.17 = (bf16[3,104,192]{2,1,0:T(8,128)(2,1)}, bf16[3,104,192]{2,1,0:T(8,128)(2,1)S(1)}, u32[]{:S(2)}, u32[]{:S(2)}) collective-permute-start(bf16[3,104,192]{2,1,0:T(8,128)(2,1)} %get-tuple-element.15.refs_16_), channel_id=1, source_target_pairs={{0,1},{1,0},{2,3},{3,2},{4,5},{5,4},{6,7},{7,6},{8,9},{9,8},{10,11... | collective-permute-start | bytes 359432 | tf_op jit(solution)/shard_map/ppermute | solution.py:345
  9.9 7.1 %collective-permute-start.3 = (bf16[96,768]{1,0:T(8,128)(2,1)S(1)}, bf16[96,768]{1,0:T(8,128)(2,1)S(1)}, u32[]{:S(2)}, u32[]{:S(2)}) collective-permute-start(bf16[96,768]{1,0:T(8,128)(2,1)S(1)} %get-tuple-element.28.refs_1_), channel_id=1, source_target_pairs={{0,4},{1,5},{2,6},{3,7},{4,0},{5,1},{6,2},{7,3},{8,12},{9,13},{10,... | collective-permute-start | bytes 442376 | tf_op jit(solution)/shard_map/ppermute | solution.py:345
  27.8 15.3 %collective-permute-start.31 = (bf16[192,768]{1,0:T(8,128)(2,1)}, bf16[192,768]{1,0:T(8,128)(2,1)S(1)}, u32[]{:S(2)}, u32[]{:S(2)}) collective-permute-start(bf16[192,768]{1,0:T(8,128)(2,1)} %bitcast.17), channel_id=1, source_target_pairs={{0,2},{1,3},{2,0},{3,1},{4,6},{5,7},{6,4},{7,5},{8,10},{9,11},{10,... | collective-permute-start | bytes 884744 | tf_op jit(solution)/shard_map/ppermute | solution.py:345
  27.9 15.2 %collective-permute-start.32 = (bf16[192,768]{1,0:T(8,128)(2,1)}, bf16[192,768]{1,0:T(8,128)(2,1)S(1)}, u32[]{:S(2)}, u32[]{:S(2)}) collective-permute-start(bf16[192,768]{1,0:T(8,128)(2,1)} %bitcast.18), channel_id=1, source_target_pairs={{0,4},{1,5},{2,6},{3,7},{4,0},{5,1},{6,2},{7,3},{8,12},{9,13},{10,... | collective-permute-start | bytes 884744 | tf_op jit(solution)/shard_map/ppermute | solution.py:345
  29.3 15.6 %collective-permute-start.33 = (bf16[192,768]{1,0:T(8,128)(2,1)}, bf16[192,768]{1,0:T(8,128)(2,1)S(1)}, u32[]{:S(2)}, u32[]{:S(2)}) collective-permute-start(bf16[192,768]{1,0:T(8,128)(2,1)} %bitcast.19), channel_id=1, source_target_pairs={{0,6},{1,7},{2,4},{3,5},{4,2},{5,3},{6,0},{7,1},{8,14},{9,15},{10,... | collective-permute-start | bytes 884744 | tf_op jit(solution)/shard_map/ppermute | solution.py:345
  31.3 11.8 %collective-permute-start.27 = (bf16[96,768]{1,0:T(8,128)(2,1)}, bf16[96,768]{1,0:T(8,128)(2,1)S(1)}, u32[]{:S(2)}, u32[]{:S(2)}) collective-permute-start(bf16[96,768]{1,0:T(8,128)(2,1)} %refs_6_.1), channel_id=1, source_target_pairs={{0,1},{1,0},{2,3},{3,2},{4,5},{5,4},{6,7},{7,6},{8,9},{9,8},{10,11... | collective-permute-start | bytes 442376 | tf_op jit(solution)/shard_map/ppermute | solution.py:345
  32.7 19.8 %collective-permute-start.24 = (bf16[96,768]{1,0:T(8,128)(2,1)}, bf16[96,768]{1,0:T(8,128)(2,1)S(1)}, u32[]{:S(2)}, u32[]{:S(2)}) collective-permute-start(bf16[96,768]{1,0:T(8,128)(2,1)} %refs_6_.1), channel_id=1, source_target_pairs={{0,2},{1,3},{2,0},{3,1},{4,6},{5,7},{6,4},{7,5},{8,10},{9,11},{10,... | collective-permute-start | bytes 442376 | tf_op jit(solution)/shard_map/ppermute | solution.py:345
  50.6 9.4 %collective-permute-start.25 = (bf16[96,768]{1,0:T(8,128)(2,1)S(1)}, bf16[96,768]{1,0:T(8,128)(2,1)S(1)}, u32[]{:S(2)}, u32[]{:S(2)}) collective-permute-start(bf16[96,768]{1,0:T(8,128)(2,1)S(1)} %copy-done), channel_id=1, source_target_pairs={{0,4},{1,5},{2,6},{3,7},{4,0},{5,1},{6,2},{7,3},{8,12},{9,13},{10,... | collective-permute-start | bytes 442376 | tf_op jit(solution)/shard_map/ppermute | solution.py:345
  51.5 8.9 %collective-permute-start.26 = (bf16[96,768]{1,0:T(8,128)(2,1)S(1)}, bf16[96,768]{1,0:T(8,128)(2,1)S(1)}, u32[]{:S(2)}, u32[]{:S(2)}) collective-permute-start(bf16[96,768]{1,0:T(8,128)(2,1)S(1)} %copy-done), channel_id=1, source_target_pairs={{0,6},{1,7},{2,4},{3,5},{4,2},{5,3},{6,0},{7,1},{8,14},{9,15},{10,... | collective-permute-start | bytes 442376 | tf_op jit(solution)/shard_map/ppermute | solution.py:345
  52.5 8.0 %collective-permute-start.28 = (bf16[96,768]{1,0:T(8,128)(2,1)S(1)}, bf16[96,768]{1,0:T(8,128)(2,1)S(1)}, u32[]{:S(2)}, u32[]{:S(2)}) collective-permute-start(bf16[96,768]{1,0:T(8,128)(2,1)S(1)} %collective-permute-done.24.refs_5_), channel_id=1, source_target_pairs={{0,1},{1,0},{2,3},{3,2},{4,5},{5,4},{6,7},{7,6},{8,9},{9,8},{10,11... | collective-permute-start | bytes 442376 | tf_op jit(solution)/shard_map/ppermute | solution.py:345
  52.6 8.4 %collective-permute-start.35 = (bf16[96,192]{1,0:T(8,128)(2,1)S(1)}, bf16[96,192]{1,0:T(8,128)(2,1)S(1)}, u32[]{:S(2)}, u32[]{:S(2)}) collective-permute-start(bf16[96,192]{1,0:T(8,128)(2,1)S(1)} %get-tuple-element.34), channel_id=1, source_target_pairs={{0,8},{8,0},{16,24},{24,16},{1,9},{9,1},{17,25},{25,17},{2,10},{10... | collective-permute-start | bytes 110600 | tf_op jit(solution)/shard_map/ppermute | solution.py:420
  53.1 8.2 %collective-permute-start.36 = (bf16[96,192]{1,0:T(8,128)(2,1)S(1)}, bf16[96,192]{1,0:T(8,128)(2,1)S(1)}, u32[]{:S(2)}, u32[]{:S(2)}) collective-permute-start(bf16[96,192]{1,0:T(8,128)(2,1)S(1)} %get-tuple-element.36), channel_id=1, source_target_pairs={{0,16},{8,24},{16,0},{24,8},{1,17},{9,25},{17,1},{25,9},{2,18},{10... | collective-permute-start | bytes 110600 | tf_op jit(solution)/shard_map/ppermute | solution.py:420
  60.5 8.3 %collective-permute-start.30 = (bf16[96,768]{1,0:T(8,128)(2,1)S(1)}, bf16[96,768]{1,0:T(8,128)(2,1)S(1)}, u32[]{:S(2)}, u32[]{:S(2)}) collective-permute-start(bf16[96,768]{1,0:T(8,128)(2,1)S(1)} %collective-permute-done.26.refs_7_), channel_id=1, source_target_pairs={{0,1},{1,0},{2,3},{3,2},{4,5},{5,4},{6,7},{7,6},{8,9},{9,8},{10,11... | collective-permute-start | bytes 442376 | tf_op jit(solution)/shard_map/ppermute | solution.py:345
  61.0 7.8 %collective-permute-start.21 = (bf16[192,192]{1,0:T(8,128)(2,1)S(1)}, bf16[192,192]{1,0:T(8,128)(2,1)S(1)}, u32[]{:S(2)}, u32[]{:S(2)}) collective-permute-start(bf16[192,192]{1,0:T(8,128)(2,1)S(1)} %get-tuple-element.20), channel_id=1, source_target_pairs={{0,2},{1,3},{2,0},{3,1},{4,6},{5,7},{6,4},{7,5},{8,10},{9,11},{10,... | collective-permute-start | bytes 221192 | tf_op jit(solution)/shard_map/ppermute | solution.py:345
  61.3 11.7 %collective-permute-start.22 = (bf16[192,192]{1,0:T(8,128)(2,1)S(1)}, bf16[192,192]{1,0:T(8,128)(2,1)S(1)}, u32[]{:S(2)}, u32[]{:S(2)}) collective-permute-start(bf16[192,192]{1,0:T(8,128)(2,1)S(1)} %get-tuple-element.21), channel_id=1, source_target_pairs={{0,4},{1,5},{2,6},{3,7},{4,0},{5,1},{6,2},{7,3},{8,12},{9,13},{10,... | collective-permute-start | bytes 221192 | tf_op jit(solution)/shard_map/ppermute | solution.py:345
  65.9 10.0 %collective-permute-start.23 = (bf16[192,192]{1,0:T(8,128)(2,1)S(1)}, bf16[192,192]{1,0:T(8,128)(2,1)S(1)}, u32[]{:S(2)}, u32[]{:S(2)}) collective-permute-start(bf16[192,192]{1,0:T(8,128)(2,1)S(1)} %get-tuple-element.22), channel_id=1, source_target_pairs={{0,6},{1,7},{2,4},{3,5},{4,2},{5,3},{6,0},{7,1},{8,14},{9,15},{10,... | collective-permute-start | bytes 221192 | tf_op jit(solution)/shard_map/ppermute | solution.py:345
  67.3 10.0 %collective-permute-start.38 = (bf16[96,192]{1,0:T(8,128)(2,1)S(1)}, bf16[96,192]{1,0:T(8,128)(2,1)S(1)}, u32[]{:S(2)}, u32[]{:S(2)}) collective-permute-start(bf16[96,192]{1,0:T(8,128)(2,1)S(1)} %fusion.2), channel_id=1, source_target_pairs={{0,24},{1,25},{2,26},{3,27},{4,28},{5,29},{6,30},{7,31},{8,18},{9,... | collective-permute-start | bytes 110600 | tf_op jit(solution)/shard_map/ppermute | solution.py:428
  68.8 8.5 %collective-permute-start.39 = (bf16[96,192]{1,0:T(8,128)(2,1)S(1)}, bf16[96,192]{1,0:T(8,128)(2,1)S(1)}, u32[]{:S(2)}, u32[]{:S(2)}) collective-permute-start(bf16[96,192]{1,0:T(8,128)(2,1)S(1)} %fusion.2), channel_id=1, source_target_pairs={{0,16},{1,17},{2,18},{3,19},{4,20},{5,21},{6,22},{7,23},{8,26},{9,... | collective-permute-start | bytes 110600 | tf_op jit(solution)/shard_map/ppermute | solution.py:428
  68.8 8.5 %collective-permute-start.40 = (bf16[96,192]{1,0:T(8,128)(2,1)S(1)}, bf16[96,192]{1,0:T(8,128)(2,1)S(1)}, u32[]{:S(2)}, u32[]{:S(2)}) collective-permute-start(bf16[96,192]{1,0:T(8,128)(2,1)S(1)} %fusion.2), channel_id=1, source_target_pairs={{0,8},{1,9},{2,10},{3,11},{4,12},{5,13},{6,14},{7,15},{8,2},{9,3},... | collective-permute-start | bytes 110600 | tf_op jit(solution)/shard_map/ppermute | solution.py:428
  73.0 6.9 %collective-permute-start.41 = (bf16[96,192]{1,0:T(8,128)(2,1)S(1)}, bf16[96,192]{1,0:T(8,128)(2,1)S(1)}, u32[]{:S(2)}, u32[]{:S(2)}) collective-permute-start(bf16[96,192]{1,0:T(8,128)(2,1)S(1)} %fusion.2), channel_id=1, source_target_pairs={{0,0},{1,1},{2,2},{3,3},{4,4},{5,5},{6,6},{7,7},{8,10},{9,11},{10,... | collective-permute-start | bytes 110600 | tf_op jit(solution)/shard_map/ppermute | solution.py:428
  (22 other events, 130.4 us)

commit v4 on v3

--- a/solution.py
+++ b/solution.py
@@ -14,6 +14,7 @@
 LOG2E = 1.4426950408889634
 
 
+SMALL = pltpu.CompilerParams(vmem_limit_bytes=16 * 1024 * 1024)
 VM = pl.BlockSpec(memory_space=pltpu.VMEM)
 ANY = pl.BlockSpec(memory_space=pl.ANY)
 SM = pl.BlockSpec(memory_space=pltpu.SMEM)
@@ -43,10 +44,20 @@
             outs[k][i, wr:] = jnp.broadcast_to(seg[...], (8, cw)).astype(jnp.bfloat16)
 
 
+def merge_kernel(rows, count, cot, *refs):
+    merged = refs[-1]
+    position = lax.axis_index("seq") * rows + lax.broadcasted_iota(jnp.int32, cot.shape, 0)
+    masked = jnp.where(position < count[0], cot[...].astype(jnp.float32), 0.0)
+    merged[:rows, :] = masked.astype(jnp.bfloat16)
+    if len(refs) == 2:
+        merged[rows:, :] = refs[0][...]
+
+
 def place_rows(scratch, pieces, member, wr):
     for tau, piece in enumerate(pieces):
         to = pl.multiple_of((member ^ tau) * wr, wr)
-        scratch[pl.ds(to, wr), :] = piece[...].astype(scratch.dtype)
+        last = piece.shape[0]
+        scratch[pl.ds(to, wr), :] = piece[last - wr : last, :].astype(scratch.dtype)
     return scratch[...].astype(jnp.bfloat16)
 
 
@@ -229,11 +240,11 @@
             pltpu.VMEM((hg * rows, cw), bf16),
             pltpu.SemaphoreType.DMA((n * parts + n + hg,)),
         ],
-        compiler_params=pltpu.CompilerParams(vmem_limit_bytes=(40 if resident else 60) * 1024 * 1024),
-    )
-
-
-def gradient_kernel(hg, tg, parts, rows, wr, head_dim, by_dp, resident, count, *refs):
+        compiler_params=pltpu.CompilerParams(vmem_limit_bytes=(30 if resident else 60) * 1024 * 1024),
+    )
+
+
+def gradient_kernel(hg, tg, parts, rows, wr, head_dim, by_dp, resident, *refs):
     n = hg * tg
     refs = list(refs)
     if resident:
@@ -273,11 +284,8 @@
     for copy in p_copies[:slots] + tile_copies:
         copy.start()
     wout = place_rows(wout_s, wout_pieces, member, wr)
-    iota = lax.broadcasted_iota(jnp.int32, cots[0].shape, 0)
     for k in range(hg):
-        position = ((group ^ k) * tg + member) * rows + iota
-        masked = jnp.where(position < count[0], cots[k][...].astype(jnp.float32), 0.0)
-        dout = dot_last(masked.astype(jnp.bfloat16), wout).astype(jnp.bfloat16)
+        dout = dot_last(cots[k][:rows, :], wout).astype(jnp.bfloat16)
         scaled = scaled_in[k * rows : (k + 1) * rows, :]
         d = (dout.astype(jnp.float32) * scaled).T.astype(jnp.bfloat16)
         if not resident:
@@ -312,8 +320,7 @@
     return pl.pallas_call(
         functools.partial(gradient_kernel, hg, tg, parts, rows, wr, head_dim, by_dp, resident),
         out_shape=[jax.ShapeDtypeStruct((hg, wr, cw), bf16)] * tg,
-        in_specs=[SM]
-        + ([VM] * 2 if resident else [ANY] * (n * parts + 1))
+        in_specs=([VM] * 2 if resident else [ANY] * (n * parts + 1))
         + [VM] * (hg + tg + 1),
         out_specs=[VM] * tg,
         scratch_shapes=local
@@ -323,7 +330,7 @@
             pltpu.VMEM((width, cw), jnp.float32),
             pltpu.SemaphoreType.DMA((n * parts + hg,)),
         ],
-        compiler_params=pltpu.CompilerParams(vmem_limit_bytes=(40 if resident else 60) * 1024 * 1024),
+        compiler_params=pltpu.CompilerParams(vmem_limit_bytes=(30 if resident else 60) * 1024 * 1024),
     )
 
 
@@ -378,8 +385,18 @@
         for piece in tile_pieces
     ]
     flat_tiles = [x for piece in tile_pieces for x in piece]
-    cots = over_groups([cotangent[0]] * hg)
-    wout_table = over_members(over_groups([w_out] * hg))
+    joined = fits(n * rows)
+    merged = pl.pallas_call(
+        functools.partial(merge_kernel, rows),
+        out_shape=jax.ShapeDtypeStruct((rows + wr if joined else rows, width), bf16),
+        in_specs=[SM] + [VM] * (2 if joined else 1),
+        out_specs=VM,
+    )(tissue_count, cotangent[0], *([w_out] if joined else []))
+    cots = over_groups([merged] * hg)
+    if joined:
+        wout_table = over_members(cots)
+    else:
+        wout_table = over_members(over_groups([w_out] * hg))
 
     def near_core(arrays):
         if not fits(n * rows):
@@ -394,7 +411,6 @@
         kept = [*flat_tiles, *kept]
     attention = over_groups(attention)
     grads = gradient_call(hg, tg, parts, rows, width, wr, cw, head_dim, by_dp)(
-        tissue_count,
         *near_core(kept),
         *near_core(cots),
         *near_core([line[0] for line in wout_table]),
@@ -411,6 +427,7 @@
         in_specs=[VM] * (hg + n),
         out_specs=VM,
         scratch_shapes=[pltpu.VMEM((hg, cw, width), wide)],
+        compiler_params=SMALL,
     )(*near_core(attention), *near_core(flat(wout_table)))
 
     if by_dp:

time: 81 us -> 98.3 us (1.21)
  the two profiles are of different devices: /device:TPU:24 before, /device:TPU:0 now
where the time goes in v4:
time: 98.3 us; the launch traced here: 97.8 us
  waiting for transfers between devices  35.2 us (36%)
  starting transfers between devices  29.3 us (30%)
  Pallas kernels  19.6 us (20%)
  local copies, waits for them, and re-layouts  9.8 us (10%)
  other arithmetic  2.41 us (2%)
  between operations  1.52 us (2%)
    ppermute x32, starting transfers between devices, hop(): return lax.ppermute(x, 'seq', [(s, s ^ step) for s in range(n)])  21.5 us
    ppermute x32, waiting for transfers between devices, hop(): return lax.ppermute(x, 'seq', [(s, s ^ step) for s in range(n)])  20.1 us
    pallas_call x1, Pallas kernels, local(): attention_call(hg, tg, parts, rows, width, wr, cw, head_dim)  10.5 us
    ppermute x4, waiting for transfers between devices, local(): pieces.append(lax.ppermute(mine, ('dp', 'seq'), pairs))  10.2 us
    unnamed x36, local copies, waits for them, and re-layouts  8.79 us
    ppermute x3, waiting for transfers between devices, local(): got = lax.ppermute(summed[m], 'dp', [(z, z ^ m) for z in range(dp)])  4.87 us
    ppermute x3, starting transfers between devices, local(): got = lax.ppermute(summed[m], 'dp', [(z, z ^ m) for z in range(dp)])  4.45 us
    pallas_call x1, Pallas kernels, local(): gradient_call(hg, tg, parts, rows, width, wr, cw, head_dim, by_dp)  3.81 us
  transfers between devices with their start and end apart: 39, of which 16 were waited for; matrix products, arithmetic and copies ran while one was open for 3% of the time, Pallas kernels for 13%

profile of v4, /device:TPU:0, one launch (start us, length us, event | category | flops | bytes accessed | tf_op | source)
XLA Modules:
  0.0 97.8 jit_solution(18377515867328335755)
XLA Ops:
  0.6 2.2 %shard_map.95 = (bf16[3,104,192]{2,1,0:T(8,128)(2,1)}, bf16[3,104,192]{2,1,0:T(8,128)(2,1)}, bf16[3,104,192]{2,1,0:T(8,128)(2,1)}, bf16[3,104,192]{2,1,0:T(8,128)(2,1)}) custom-call(bf16[96,768]{1,0:T(8,128)(2,1)} %wq.1, bf16[96,768]{1,0:T(8,128)(2,1)} %wk.1, bf16[96,768]{1,0:T(8,128)(2,1)} %wv.1, s32[1,192]{1,0:T(1,128)} %bitcast.18), custom_call_target="tpu_custom_call" | custom-call | tf_op jit(solution)/shard_map/pallas_call | solution.py:366
  2.8 3.0 %collective-permute-start.14 = (bf16[3,104,192]{2,1,0:T(8,128)(2,1)}, bf16[3,104,192]{2,1,0:T(8,128)(2,1)S(1)}, u32[]{:S(2)}, u32[]{:S(2)}) collective-permute-start(bf16[3,104,192]{2,1,0:T(8,128)(2,1)} %get-tuple-element.16), channel_id=1, source_target_pairs={{0,2},{1,3},{2,0},{3,1},{4,6},{5,7},{6,4},{7,5},{8,10},{9,11},{10,... | collective-permute-start | bytes 359432 | tf_op jit(solution)/shard_map/ppermute | solution.py:352
  5.8 1.5 %collective-permute-start.15 = (bf16[3,104,192]{2,1,0:T(8,128)(2,1)}, bf16[3,104,192]{2,1,0:T(8,128)(2,1)S(1)}, u32[]{:S(2)}, u32[]{:S(2)}) collective-permute-start(bf16[3,104,192]{2,1,0:T(8,128)(2,1)} %get-tuple-element.17), channel_id=1, source_target_pairs={{0,4},{1,5},{2,6},{3,7},{4,0},{5,1},{6,2},{7,3},{8,12},{9,13},{10,... | collective-permute-start | bytes 359432 | tf_op jit(solution)/shard_map/ppermute | solution.py:352
  8.3 2.0 %collective-permute-start = (bf16[96,768]{1,0:T(8,128)(2,1)S(1)}, bf16[96,768]{1,0:T(8,128)(2,1)S(1)}, u32[]{:S(2)}, u32[]{:S(2)}) collective-permute-start(bf16[96,768]{1,0:T(8,128)(2,1)S(1)} %get-tuple-element.29.refs_0_), channel_id=1, source_target_pairs={{0,2},{1,3},{2,0},{3,1},{4,6},{5,7},{6,4},{7,5},{8,10},{9,11},{10,... | collective-permute-start | bytes 442376 | tf_op jit(solution)/shard_map/ppermute | solution.py:352
  10.8 2.0 %collective-permute-start.3 = (bf16[96,768]{1,0:T(8,128)(2,1)S(1)}, bf16[96,768]{1,0:T(8,128)(2,1)S(1)}, u32[]{:S(2)}, u32[]{:S(2)}) collective-permute-start(bf16[96,768]{1,0:T(8,128)(2,1)S(1)} %get-tuple-element.28.refs_1_), channel_id=1, source_target_pairs={{0,4},{1,5},{2,6},{3,7},{4,0},{5,1},{6,2},{7,3},{8,12},{9,13},{10,... | collective-permute-start | bytes 442376 | tf_op jit(solution)/shard_map/ppermute | solution.py:352
  12.9 2.3 %collective-permute-done.15.refs_18_ = bf16[3,104,192]{2,1,0:T(8,128)(2,1)S(1)} collective-permute-done((bf16[3,104,192]{2,1,0:T(8,128)(2,1)}, bf16[3,104,192]{2,1,0:T(8,128)(2,1)S(1)}, u32[]{:S(2)}, u32[]{:S(2)}) %collective-permute-start.15) | collective-permute-done | bytes 119840 | tf_op jit(solution)/shard_map/ppermute | solution.py:352
  15.1 2.4 %collective-permute-start.2 = (bf16[96,768]{1,0:T(8,128)(2,1)S(1)}, bf16[96,768]{1,0:T(8,128)(2,1)S(1)}, u32[]{:S(2)}, u32[]{:S(2)}) collective-permute-start(bf16[96,768]{1,0:T(8,128)(2,1)S(1)} %get-tuple-element.29.refs_0_), channel_id=1, source_target_pairs={{0,4},{1,5},{2,6},{3,7},{4,0},{5,1},{6,2},{7,3},{8,12},{9,13},{10,... | collective-permute-start | bytes 442376 | tf_op jit(solution)/shard_map/ppermute | solution.py:352
  18.3 3.0 %collective-permute-done.2.refs_4_ = bf16[96,768]{1,0:T(8,128)(2,1)S(1)} collective-permute-done((bf16[96,768]{1,0:T(8,128)(2,1)S(1)}, bf16[96,768]{1,0:T(8,128)(2,1)S(1)}, u32[]{:S(2)}, u32[]{:S(2)}) %collective-permute-start.2) | collective-permute-done | bytes 147488 | tf_op jit(solution)/shard_map/ppermute | solution.py:352
  25.1 1.8 %shard_map.97.refs_4_.refs_2_.refs_6_ = bf16[288,768]{1,0:T(8,128)(2,1)} custom-call(s32[1]{0:T(128)S(6)} %copy.10.count, bf16[192,768]{1,0:T(8,128)(2,1)} %bitcast.17, bf16[96,768]{1,0:T(8,128)(2,1)} %refs_0_.1), custom_call_target="tpu_custom_call" | custom-call | tf_op jit(solution)/shard_map/pallas_call | solution.py:389
  26.9 2.2 %collective-permute-done.4.refs_6_ = bf16[96,768]{1,0:T(8,128)(2,1)} collective-permute-done((bf16[96,768]{1,0:T(8,128)(2,1)S(1)}, bf16[96,768]{1,0:T(8,128)(2,1)}, u32[]{:S(2)}, u32[]{:S(2)}) %collective-permute-start.4) | collective-permute-done | bytes 147488 | tf_op jit(solution)/shard_map/ppermute | solution.py:352
  30.2 1.7 %collective-permute-start.25 = (bf16[288,768]{1,0:T(8,128)(2,1)}, bf16[288,768]{1,0:T(8,128)(2,1)S(1)}, u32[]{:S(2)}, u32[]{:S(2)}) collective-permute-start(bf16[288,768]{1,0:T(8,128)(2,1)} %shard_map.97.refs_4_.refs_2_.refs_6_), channel_id=1, source_target_pairs={{0,4},{1,5},{2,6},{3,7},{4,0},{5,1},{6,2},{7,3},{8,12},{9,13},{10,... | collective-permute-start | bytes 1327112 | tf_op jit(solution)/shard_map/ppermute | solution.py:352
  32.5 1.5 %collective-permute-start.26 = (bf16[288,768]{1,0:T(8,128)(2,1)}, bf16[288,768]{1,0:T(8,128)(2,1)S(1)}, u32[]{:S(2)}, u32[]{:S(2)}) collective-permute-start(bf16[288,768]{1,0:T(8,128)(2,1)} %shard_map.97.refs_4_.refs_2_.refs_6_), channel_id=1, source_target_pairs={{0,6},{1,7},{2,4},{3,5},{4,2},{5,3},{6,0},{7,1},{8,14},{9,15},{10,... | collective-permute-start | bytes 1327112 | tf_op jit(solution)/shard_map/ppermute | solution.py:352
  34.6 1.7 %collective-permute-done.12.refs_14_ = bf16[96,768]{1,0:T(8,128)(2,1)S(1)} collective-permute-done((bf16[96,768]{1,0:T(8,128)(2,1)}, bf16[96,768]{1,0:T(8,128)(2,1)S(1)}, u32[]{:S(2)}, u32[]{:S(2)}) %collective-permute-start.12) | collective-permute-done | bytes 147488 | tf_op jit(solution)/shard_map/ppermute | solution.py:352
  43.4 10.5 %shard_map.96 = (bf16[192,192]{1,0:T(8,128)(2,1)S(1)}, bf16[192,192]{1,0:T(8,128)(2,1)S(1)}, bf16[192,192]{1,0:T(8,128)(2,1)S(1)}, bf16[192,192]{1,0:T(8,128)(2,...) custom-call(s32[1]{0:T(128)S(6)} %copy.10.count, ...), custom_call_target="tpu_custom_call" | custom-call | tf_op jit(solution)/shard_map/pallas_call | solution.py:406
  55.1 3.8 %shard_map.99 = (bf16[4,96,192]{2,1,0:T(8,128)(2,1)S(1)}, bf16[4,96,192]{2,1,0:T(8,128)(2,1)S(1)}) custom-call(bf16[4,3,192,1536]{3,2,1,0:T(8,128)(2,1)S(1)} %get-tuple-element.23.refs_0_, bf16[1536,768]{1,0:T(8,128)(2,1)S(1)} %get-tuple-element.24.refs_1_, bf16[288,768]{1,0:T(8,128)(2,1)S(1)} %copy-done, ...), custom_call_target="tpu_custom_call" | custom-call | tf_op jit(solution)/shard_map/pallas_call | solution.py:413
  61.9 2.6 %collective-permute-start.33 = (bf16[96,192]{1,0:T(8,128)(2,1)S(1)}, bf16[96,192]{1,0:T(8,128)(2,1)S(1)}, u32[]{:S(2)}, u32[]{:S(2)}) collective-permute-start(bf16[96,192]{1,0:T(8,128)(2,1)S(1)} %get-tuple-element.36), channel_id=1, source_target_pairs={{0,16},{8,24},{16,0},{24,8},{1,17},{9,25},{17,1},{25,9},{2,18},{10... | collective-permute-start | bytes 110600 | tf_op jit(solution)/shard_map/ppermute | solution.py:437
  65.5 2.2 %collective-permute-done.33 = bf16[96,192]{1,0:T(8,128)(2,1)S(1)} collective-permute-done((bf16[96,192]{1,0:T(8,128)(2,1)S(1)}, bf16[96,192]{1,0:T(8,128)(2,1)S(1)}, u32[]{:S(2)}, u32[]{:S(2)}) %collective-permute-start.33) | collective-permute-done | bytes 36896 | tf_op jit(solution)/shard_map/ppermute | solution.py:437
  67.8 2.6 %collective-permute-done.34 = bf16[96,192]{1,0:T(8,128)(2,1)S(1)} collective-permute-done((bf16[96,192]{1,0:T(8,128)(2,1)S(1)}, bf16[96,192]{1,0:T(8,128)(2,1)S(1)}, u32[]{:S(2)}, u32[]{:S(2)}) %collective-permute-start.34) | collective-permute-done | bytes 36896 | tf_op jit(solution)/shard_map/ppermute | solution.py:437
  72.4 6.8 %collective-permute-done.35 = bf16[96,192]{1,0:T(8,128)(2,1)} collective-permute-done((bf16[96,192]{1,0:T(8,128)(2,1)}, bf16[96,192]{1,0:T(8,128)(2,1)}, u32[]{:S(2)}, u32[]{:S(2)}) %collective-permute-start.35) | collective-permute-done | bytes 36896 | tf_op jit(solution)/shard_map/ppermute | solution.py:445
  79.2 2.1 %collective-permute-start.38 = (bf16[96,192]{1,0:T(8,128)(2,1)}, bf16[96,192]{1,0:T(8,128)(2,1)}, u32[]{:S(2)}, u32[]{:S(2)}) collective-permute-start(bf16[96,192]{1,0:T(8,128)(2,1)} %fusion.2), channel_id=1, source_target_pairs={{0,0},{1,1},{2,2},{3,3},{4,4},{5,5},{6,6},{7,7},{8,10},{9,11},{10,... | collective-permute-start | bytes 110600 | tf_op jit(solution)/shard_map/ppermute | solution.py:445
  81.3 3.3 %collective-permute-done.37 = bf16[96,192]{1,0:T(8,128)(2,1)} collective-permute-done((bf16[96,192]{1,0:T(8,128)(2,1)}, bf16[96,192]{1,0:T(8,128)(2,1)}, u32[]{:S(2)}, u32[]{:S(2)}) %collective-permute-start.37) | collective-permute-done | bytes 36896 | tf_op jit(solution)/shard_map/ppermute | solution.py:445
  87.3 2.5 %collective-permute-done.21.refs_1_ = bf16[192,192]{1,0:T(8,128)(2,1)S(1)} collective-permute-done((bf16[192,192]{1,0:T(8,128)(2,1)}, bf16[192,192]{1,0:T(8,128)(2,1)S(1)}, u32[]{:S(2)}, u32[]{:S(2)}) %collective-permute-start.21) | collective-permute-done | bytes 73760 | tf_op jit(solution)/shard_map/ppermute | solution.py:352
  89.9 1.5 %collective-permute-start.23 = (bf16[192,192]{1,0:T(8,128)(2,1)}, bf16[192,192]{1,0:T(8,128)(2,1)S(1)}, u32[]{:S(2)}, u32[]{:S(2)}) collective-permute-start(bf16[192,192]{1,0:T(8,128)(2,1)} %copy-done.15), channel_id=1, source_target_pairs={{0,6},{1,7},{2,4},{3,5},{4,2},{5,3},{6,0},{7,1},{8,14},{9,15},{10,... | collective-permute-start | bytes 221192 | tf_op jit(solution)/shard_map/ppermute | solution.py:352
  92.2 3.4 %collective-permute-done.23.refs_3_ = bf16[192,192]{1,0:T(8,128)(2,1)S(1)} collective-permute-done((bf16[192,192]{1,0:T(8,128)(2,1)}, bf16[192,192]{1,0:T(8,128)(2,1)S(1)}, u32[]{:S(2)}, u32[]{:S(2)}) %collective-permute-start.23) | collective-permute-done | bytes 73760 | tf_op jit(solution)/shard_map/ppermute | solution.py:352
  (101 shorter events, 27.5 us)
Async XLA Ops:
  2.8 8.1 %collective-permute-start.14 = (bf16[3,104,192]{2,1,0:T(8,128)(2,1)}, bf16[3,104,192]{2,1,0:T(8,128)(2,1)S(1)}, u32[]{:S(2)}, u32[]{:S(2)}) collective-permute-start(bf16[3,104,192]{2,1,0:T(8,128)(2,1)} %get-tuple-element.16), channel_id=1, source_target_pairs={{0,2},{1,3},{2,0},{3,1},{4,6},{5,7},{6,4},{7,5},{8,10},{9,11},{10,... | collective-permute-start | bytes 359432 | tf_op jit(solution)/shard_map/ppermute | solution.py:352
  5.8 9.4 %collective-permute-start.15 = (bf16[3,104,192]{2,1,0:T(8,128)(2,1)}, bf16[3,104,192]{2,1,0:T(8,128)(2,1)S(1)}, u32[]{:S(2)}, u32[]{:S(2)}) collective-permute-start(bf16[3,104,192]{2,1,0:T(8,128)(2,1)} %get-tuple-element.17), channel_id=1, source_target_pairs={{0,4},{1,5},{2,6},{3,7},{4,0},{5,1},{6,2},{7,3},{8,12},{9,13},{10,... | collective-permute-start | bytes 359432 | tf_op jit(solution)/shard_map/ppermute | solution.py:352
  7.3 10.3 %collective-permute-start.16 = (bf16[3,104,192]{2,1,0:T(8,128)(2,1)}, bf16[3,104,192]{2,1,0:T(8,128)(2,1)S(1)}, u32[]{:S(2)}, u32[]{:S(2)}) collective-permute-start(bf16[3,104,192]{2,1,0:T(8,128)(2,1)} %get-tuple-element.18), channel_id=1, source_target_pairs={{0,6},{1,7},{2,4},{3,5},{4,2},{5,3},{6,0},{7,1},{8,14},{9,15},{10,... | collective-permute-start | bytes 359432 | tf_op jit(solution)/shard_map/ppermute | solution.py:352
  8.3 9.3 %collective-permute-start = (bf16[96,768]{1,0:T(8,128)(2,1)S(1)}, bf16[96,768]{1,0:T(8,128)(2,1)S(1)}, u32[]{:S(2)}, u32[]{:S(2)}) collective-permute-start(bf16[96,768]{1,0:T(8,128)(2,1)S(1)} %get-tuple-element.29.refs_0_), channel_id=1, source_target_pairs={{0,2},{1,3},{2,0},{3,1},{4,6},{5,7},{6,4},{7,5},{8,10},{9,11},{10,... | collective-permute-start | bytes 442376 | tf_op jit(solution)/shard_map/ppermute | solution.py:352
  10.3 7.2 %collective-permute-start.17 = (bf16[3,104,192]{2,1,0:T(8,128)(2,1)}, bf16[3,104,192]{2,1,0:T(8,128)(2,1)S(1)}, u32[]{:S(2)}, u32[]{:S(2)}) collective-permute-start(bf16[3,104,192]{2,1,0:T(8,128)(2,1)} %get-tuple-element.15.refs_16_), channel_id=1, source_target_pairs={{0,1},{1,0},{2,3},{3,2},{4,5},{5,4},{6,7},{7,6},{8,9},{9,8},{10,11... | collective-permute-start | bytes 359432 | tf_op jit(solution)/shard_map/ppermute | solution.py:352
  10.8 7.4 %collective-permute-start.3 = (bf16[96,768]{1,0:T(8,128)(2,1)S(1)}, bf16[96,768]{1,0:T(8,128)(2,1)S(1)}, u32[]{:S(2)}, u32[]{:S(2)}) collective-permute-start(bf16[96,768]{1,0:T(8,128)(2,1)S(1)} %get-tuple-element.28.refs_1_), channel_id=1, source_target_pairs={{0,4},{1,5},{2,6},{3,7},{4,0},{5,1},{6,2},{7,3},{8,12},{9,13},{10,... | collective-permute-start | bytes 442376 | tf_op jit(solution)/shard_map/ppermute | solution.py:352
  15.1 6.1 %collective-permute-start.2 = (bf16[96,768]{1,0:T(8,128)(2,1)S(1)}, bf16[96,768]{1,0:T(8,128)(2,1)S(1)}, u32[]{:S(2)}, u32[]{:S(2)}) collective-permute-start(bf16[96,768]{1,0:T(8,128)(2,1)S(1)} %get-tuple-element.29.refs_0_), channel_id=1, source_target_pairs={{0,4},{1,5},{2,6},{3,7},{4,0},{5,1},{6,2},{7,3},{8,12},{9,13},{10,... | collective-permute-start | bytes 442376 | tf_op jit(solution)/shard_map/ppermute | solution.py:352
  22.8 6.4 %collective-permute-start.4 = (bf16[96,768]{1,0:T(8,128)(2,1)S(1)}, bf16[96,768]{1,0:T(8,128)(2,1)}, u32[]{:S(2)}, u32[]{:S(2)}) collective-permute-start(bf16[96,768]{1,0:T(8,128)(2,1)S(1)} %collective-permute-done.refs_2_), channel_id=1, source_target_pairs={{0,4},{1,5},{2,6},{3,7},{4,0},{5,1},{6,2},{7,3},{8,12},{9,13},{10,... | collective-permute-start | bytes 442376 | tf_op jit(solution)/shard_map/ppermute | solution.py:352
  23.3 5.9 %collective-permute-start.5 = (bf16[96,768]{1,0:T(8,128)(2,1)S(1)}, bf16[96,768]{1,0:T(8,128)(2,1)}, u32[]{:S(2)}, u32[]{:S(2)}) collective-permute-start(bf16[96,768]{1,0:T(8,128)(2,1)S(1)} %collective-permute-done.3.refs_5_), channel_id=1, source_target_pairs={{0,2},{1,3},{2,0},{3,1},{4,6},{5,7},{6,4},{7,5},{8,10},{9,11},{10,... | collective-permute-start | bytes 442376 | tf_op jit(solution)/shard_map/ppermute | solution.py:352
  23.9 8.0 %collective-permute-start.8 = (bf16[96,768]{1,0:T(8,128)(2,1)S(1)}, bf16[96,768]{1,0:T(8,128)(2,1)S(1)}, u32[]{:S(2)}, u32[]{:S(2)}) collective-permute-start(bf16[96,768]{1,0:T(8,128)(2,1)S(1)} %collective-permute-done.refs_2_), channel_id=1, source_target_pairs={{0,1},{1,0},{2,3},{3,2},{4,5},{5,4},{6,7},{7,6},{8,9},{9,8},{10,11... | collective-permute-start | bytes 442376 | tf_op jit(solution)/shard_map/ppermute | solution.py:352
  24.4 9.7 %collective-permute-start.10 = (bf16[96,768]{1,0:T(8,128)(2,1)S(1)}, bf16[96,768]{1,0:T(8,128)(2,1)}, u32[]{:S(2)}, u32[]{:S(2)}) collective-permute-start(bf16[96,768]{1,0:T(8,128)(2,1)S(1)} %collective-permute-done.2.refs_4_), channel_id=1, source_target_pairs={{0,1},{1,0},{2,3},{3,2},{4,5},{5,4},{6,7},{7,6},{8,9},{9,8},{10,11... | collective-permute-start | bytes 442376 | tf_op jit(solution)/shard_map/ppermute | solution.py:352
  29.2 24.7 %collective-permute-start.24 = (bf16[288,768]{1,0:T(8,128)(2,1)}, bf16[288,768]{1,0:T(8,128)(2,1)S(1)}, u32[]{:S(2)}, u32[]{:S(2)}) collective-permute-start(bf16[288,768]{1,0:T(8,128)(2,1)} %shard_map.97.refs_4_.refs_2_.refs_6_), channel_id=1, source_target_pairs={{0,2},{1,3},{2,0},{3,1},{4,6},{5,7},{6,4},{7,5},{8,10},{9,11},{10,... | collective-permute-start | bytes 1327112 | tf_op jit(solution)/shard_map/ppermute | solution.py:352
  30.2 23.8 %collective-permute-start.25 = (bf16[288,768]{1,0:T(8,128)(2,1)}, bf16[288,768]{1,0:T(8,128)(2,1)S(1)}, u32[]{:S(2)}, u32[]{:S(2)}) collective-permute-start(bf16[288,768]{1,0:T(8,128)(2,1)} %shard_map.97.refs_4_.refs_2_.refs_6_), channel_id=1, source_target_pairs={{0,4},{1,5},{2,6},{3,7},{4,0},{5,1},{6,2},{7,3},{8,12},{9,13},{10,... | collective-permute-start | bytes 1327112 | tf_op jit(solution)/shard_map/ppermute | solution.py:352
  32.5 21.5 %collective-permute-start.26 = (bf16[288,768]{1,0:T(8,128)(2,1)}, bf16[288,768]{1,0:T(8,128)(2,1)S(1)}, u32[]{:S(2)}, u32[]{:S(2)}) collective-permute-start(bf16[288,768]{1,0:T(8,128)(2,1)} %shard_map.97.refs_4_.refs_2_.refs_6_), channel_id=1, source_target_pairs={{0,6},{1,7},{2,4},{3,5},{4,2},{5,3},{6,0},{7,1},{8,14},{9,15},{10,... | collective-permute-start | bytes 1327112 | tf_op jit(solution)/shard_map/ppermute | solution.py:352
  34.1 19.9 %collective-permute-start.27 = (bf16[288,768]{1,0:T(8,128)(2,1)}, bf16[288,768]{1,0:T(8,128)(2,1)S(1)}, u32[]{:S(2)}, u32[]{:S(2)}) collective-permute-start(bf16[288,768]{1,0:T(8,128)(2,1)} %shard_map.97.refs_4_.refs_2_.refs_6_), channel_id=1, source_target_pairs={{0,1},{1,0},{2,3},{3,2},{4,5},{5,4},{6,7},{7,6},{8,9},{9,8},{10,11... | collective-permute-start | bytes 1327112 | tf_op jit(solution)/shard_map/ppermute | solution.py:352
  61.9 5.9 %collective-permute-start.33 = (bf16[96,192]{1,0:T(8,128)(2,1)S(1)}, bf16[96,192]{1,0:T(8,128)(2,1)S(1)}, u32[]{:S(2)}, u32[]{:S(2)}) collective-permute-start(bf16[96,192]{1,0:T(8,128)(2,1)S(1)} %get-tuple-element.36), channel_id=1, source_target_pairs={{0,16},{8,24},{16,0},{24,8},{1,17},{9,25},{17,1},{25,9},{2,18},{10... | collective-permute-start | bytes 110600 | tf_op jit(solution)/shard_map/ppermute | solution.py:437
  64.5 5.9 %collective-permute-start.34 = (bf16[96,192]{1,0:T(8,128)(2,1)S(1)}, bf16[96,192]{1,0:T(8,128)(2,1)S(1)}, u32[]{:S(2)}, u32[]{:S(2)}) collective-permute-start(bf16[96,192]{1,0:T(8,128)(2,1)S(1)} %get-tuple-element.35), channel_id=1, source_target_pairs={{0,24},{8,16},{16,8},{24,0},{1,25},{9,17},{17,9},{25,1},{2,26},{10... | collective-permute-start | bytes 110600 | tf_op jit(solution)/shard_map/ppermute | solution.py:437
  64.9 30.7 %collective-permute-start.28 = (bf16[288,768]{1,0:T(8,128)(2,1)S(1)}, bf16[288,768]{1,0:T(8,128)(2,1)S(1)}, u32[]{:S(2)}, u32[]{:S(2)}) collective-permute-start(bf16[288,768]{1,0:T(8,128)(2,1)S(1)} %collective-permute-done.24.refs_5_.refs_3_), channel_id=1, source_target_pairs={{0,1},{1,0},{2,3},{3,2},{4,5},{5,4},{6,7},{7,6},{8,9},{9,8},{10,11... | collective-permute-start | bytes 1327112 | tf_op jit(solution)/shard_map/ppermute | solution.py:352
  64.9 30.7 %collective-permute-start.29 = (bf16[288,768]{1,0:T(8,128)(2,1)S(1)}, bf16[288,768]{1,0:T(8,128)(2,1)S(1)}, u32[]{:S(2)}, u32[]{:S(2)}) collective-permute-start(bf16[288,768]{1,0:T(8,128)(2,1)S(1)} %collective-permute-done.25.refs_6_.refs_4_), channel_id=1, source_target_pairs={{0,1},{1,0},{2,3},{3,2},{4,5},{5,4},{6,7},{7,6},{8,9},{9,8},{10,11... | collective-permute-start | bytes 1327112 | tf_op jit(solution)/shard_map/ppermute | solution.py:352
  65.4 30.2 %collective-permute-start.30 = (bf16[288,768]{1,0:T(8,128)(2,1)S(1)}, bf16[288,768]{1,0:T(8,128)(2,1)S(1)}, u32[]{:S(2)}, u32[]{:S(2)}) collective-permute-start(bf16[288,768]{1,0:T(8,128)(2,1)S(1)} %collective-permute-done.26.refs_7_.refs_5_), channel_id=1, source_target_pairs={{0,1},{1,0},{2,3},{3,2},{4,5},{5,4},{6,7},{7,6},{8,9},{9,8},{10,11... | collective-permute-start | bytes 1327112 | tf_op jit(solution)/shard_map/ppermute | solution.py:352
  71.0 8.2 %collective-permute-start.35 = (bf16[96,192]{1,0:T(8,128)(2,1)}, bf16[96,192]{1,0:T(8,128)(2,1)}, u32[]{:S(2)}, u32[]{:S(2)}) collective-permute-start(bf16[96,192]{1,0:T(8,128)(2,1)} %fusion.2), channel_id=1, source_target_pairs={{0,24},{1,25},{2,26},{3,27},{4,28},{5,29},{6,30},{7,31},{8,18},{9,... | collective-permute-start | bytes 110600 | tf_op jit(solution)/shard_map/ppermute | solution.py:445
  72.1 7.1 %collective-permute-start.36 = (bf16[96,192]{1,0:T(8,128)(2,1)}, bf16[96,192]{1,0:T(8,128)(2,1)}, u32[]{:S(2)}, u32[]{:S(2)}) collective-permute-start(bf16[96,192]{1,0:T(8,128)(2,1)} %fusion.2), channel_id=1, source_target_pairs={{0,16},{1,17},{2,18},{3,19},{4,20},{5,21},{6,22},{7,23},{8,26},{9,... | collective-permute-start | bytes 110600 | tf_op jit(solution)/shard_map/ppermute | solution.py:445
  79.2 6.1 %collective-permute-start.38 = (bf16[96,192]{1,0:T(8,128)(2,1)}, bf16[96,192]{1,0:T(8,128)(2,1)}, u32[]{:S(2)}, u32[]{:S(2)}) collective-permute-start(bf16[96,192]{1,0:T(8,128)(2,1)} %fusion.2), channel_id=1, source_target_pairs={{0,0},{1,1},{2,2},{3,3},{4,4},{5,5},{6,6},{7,7},{8,10},{9,11},{10,... | collective-permute-start | bytes 110600 | tf_op jit(solution)/shard_map/ppermute | solution.py:445
  85.3 6.9 %collective-permute-start.22 = (bf16[192,192]{1,0:T(8,128)(2,1)}, bf16[192,192]{1,0:T(8,128)(2,1)S(1)}, u32[]{:S(2)}, u32[]{:S(2)}) collective-permute-start(bf16[192,192]{1,0:T(8,128)(2,1)} %copy-done.16), channel_id=1, source_target_pairs={{0,4},{1,5},{2,6},{3,7},{4,0},{5,1},{6,2},{7,3},{8,12},{9,13},{10,... | collective-permute-start | bytes 221192 | tf_op jit(solution)/shard_map/ppermute | solution.py:352
  (33 other events, 195.9 us)

commit v5 on v4

--- a/solution.py
+++ b/solution.py
@@ -28,8 +28,10 @@
     return lax.dot_general(a, b, (((1,), (0,)), ((), ())), preferred_element_type=jnp.float32)
 
 
-def pack_kernel(hg, tg, wr, cw, wq, wk, wv, seg, *outs):
+def pack_kernel(hg, tg, wr, cw, count, wq, wk, wv, seg, cot, wout, *outs):
     group = lax.axis_index("seq") // tg
+    rows = cot.shape[0]
+    merged = outs[hg]
     for k in range(hg):
         for part in range(hg):
 
@@ -42,15 +44,11 @@
 
         for i in range(3):
             outs[k][i, wr:] = jnp.broadcast_to(seg[...], (8, cw)).astype(jnp.bfloat16)
-
-
-def merge_kernel(rows, count, cot, *refs):
-    merged = refs[-1]
     position = lax.axis_index("seq") * rows + lax.broadcasted_iota(jnp.int32, cot.shape, 0)
     masked = jnp.where(position < count[0], cot[...].astype(jnp.float32), 0.0)
     merged[:rows, :] = masked.astype(jnp.bfloat16)
-    if len(refs) == 2:
-        merged[rows:, :] = refs[0][...]
+    if merged.shape[0] > rows:
+        merged[rows:, :] = wout[...]
 
 
 def place_rows(scratch, pieces, member, wr):
@@ -211,6 +209,7 @@
     bf16 = jnp.bfloat16
     wide = bf16 if wr % 16 == 0 else jnp.float32
     resident = fits(keys)
+    own = pltpu.VMEM if resident else jax.ShapeDtypeStruct
     if resident:
         kept = [pltpu.VMEM((hg, heads, rows, keys), bf16), pltpu.VMEM((keys, width), bf16)]
         local = []
@@ -223,9 +222,7 @@
         ]
     return pl.pallas_call(
         functools.partial(attention_kernel, hg, tg, parts, rows, wr, head_dim, resident),
-        out_shape=[jax.ShapeDtypeStruct((rows, cw), bf16)] * hg
-        + [jax.ShapeDtypeStruct((hg * rows, cw), jnp.float32)]
-        + kept,
+        out_shape=[own((rows, cw), bf16)] * hg + [own((hg * rows, cw), jnp.float32)] + kept,
         in_specs=[SM] + [VM if resident else ANY] * (n * parts + n),
         out_specs=[VM] * (hg + 1) + [VM if resident else ANY] * len(kept),
         scratch_shapes=local
@@ -363,12 +360,16 @@
     wide = bf16 if wr % 16 == 0 else jnp.float32
     parts = 2 if hg == 4 and rows % 32 == 0 else 1
     segment_line = segment_of.reshape(1, rows)
-    packed = pl.pallas_call(
+    joined = fits(n * rows)
+    own_shape = pltpu.VMEM if joined else jax.ShapeDtypeStruct
+    *packed, merged = pl.pallas_call(
         functools.partial(pack_kernel, hg, tg, wr, cw),
-        out_shape=[jax.ShapeDtypeStruct((3, wr + 8, cw), bf16)] * hg,
-        in_specs=[VM] * 4,
-        out_specs=[VM] * hg,
-    )(w_query, w_key, w_value, segment_line)
+        out_shape=[own_shape((3, wr + 8, cw), bf16)]
+        + [jax.ShapeDtypeStruct((3, wr + 8, cw), bf16)] * (hg - 1)
+        + [own_shape((rows + wr if joined else rows, width), bf16)],
+        in_specs=[SM] + [VM] * 6,
+        out_specs=[VM] * (hg + 1),
+    )(tissue_count, w_query, w_key, w_value, segment_line, cotangent[0], w_out)
     weight_table = over_members(over_groups(packed))
     if parts == 2:
         half = rows // 2
@@ -385,13 +386,6 @@
         for piece in tile_pieces
     ]
     flat_tiles = [x for piece in tile_pieces for x in piece]
-    joined = fits(n * rows)
-    merged = pl.pallas_call(
-        functools.partial(merge_kernel, rows),
-        out_shape=jax.ShapeDtypeStruct((rows + wr if joined else rows, width), bf16),
-        in_specs=[SM] + [VM] * (2 if joined else 1),
-        out_specs=VM,
-    )(tissue_count, cotangent[0], *([w_out] if joined else []))
     cots = over_groups([merged] * hg)
     if joined:
         wout_table = over_members(cots)

time: 98.3 us -> 94.9 us (0.965)
  local copies, waits for them, and re-layouts: 9.8 us -> 1.02 us
  waiting for transfers between devices: 35.2 us -> 42.3 us
  Pallas kernels: 19.6 us -> 17.8 us
    unnamed x36 -> x2, local copies, waits for them, and re-layouts: 8.79 us -> 0.01 us
    ppermute x32, waiting for transfers between devices: 20.1 us -> 27.4 us  [hop(): return lax.ppermute(x, 'seq', [(s, s ^ step) for s in range(n)])]
    pallas_call x1 -> x0, Pallas kernels: 1.83 us -> none  [local(): pl.pallas_call(functools.partial(merge_kernel, rows), out_shape=jax.Shape...]
    pallas_call x1, Pallas kernels: 10.5 us -> 9.37 us  [local(): attention_call(hg, tg, parts, rows, width, wr, cw, head_dim)]
    pallas_call x1, Pallas kernels: 1.28 us -> 2.27 us  [local(): pl.pallas_call(functools.partial(proj_kernel, hg, tg, wr), out_shape=jax....]
  transfers between devices with their start and end apart: 39 -> 39, of which waited for: 16 -> 17; matrix products, arithmetic and copies ran while one was open for 3% -> 3% of each run, Pallas kernels for 13% -> 10%
where the time goes in v5:
time: 94.9 us; the launch traced here: 94.6 us
  waiting for transfers between devices  42.3 us (45%)
  starting transfers between devices  29.7 us (31%)
  Pallas kernels  17.8 us (19%)
  other arithmetic  2.35 us (2%)
  between operations  1.41 us (1%)
  local copies, waits for them, and re-layouts  1.02 us (1%)
    ppermute x32, waiting for transfers between devices, hop(): return lax.ppermute(x, 'seq', [(s, s ^ step) for s in range(n)])  27.4 us
    ppermute x32, starting transfers between devices, hop(): return lax.ppermute(x, 'seq', [(s, s ^ step) for s in range(n)])  22.2 us
    ppermute x4, waiting for transfers between devices, local(): pieces.append(lax.ppermute(mine, ('dp', 'seq'), pairs))  10.1 us
    pallas_call x1, Pallas kernels, local(): attention_call(hg, tg, parts, rows, width, wr, cw, head_dim)  9.37 us
    ppermute x3, waiting for transfers between devices, local(): got = lax.ppermute(summed[m], 'dp', [(z, z ^ m) for z in range(dp)])  4.89 us
    ppermute x3, starting transfers between devices, local(): got = lax.ppermute(summed[m], 'dp', [(z, z ^ m) for z in range(dp)])  4.45 us
    pallas_call x1, Pallas kernels, local(): gradient_call(hg, tg, parts, rows, width, wr, cw, head_dim, by_dp)  3.82 us
    ppermute x4, starting transfers between devices, local(): pieces.append(lax.ppermute(mine, ('dp', 'seq'), pairs))  3.11 us
  transfers between devices with their start and end apart: 39, of which 17 were waited for; matrix products, arithmetic and copies ran while one was open for 3% of the time, Pallas kernels for 10%

profile of v5, /device:TPU:0, one launch (start us, length us, event | category | flops | bytes accessed | tf_op | source)
XLA Modules:
  0.0 94.6 jit_solution(4711849379738064907)
XLA Ops:
  1.3 2.3 %shard_map.95 = (bf16[3,104,192]{2,1,0:T(8,128)(2,1)S(1)}, bf16[3,104,192]{2,1,0:T(8,128)(2,1)}, bf16[3,104,192]{2,1,0:T(8,128)(2,1)}, bf16[3,104,192]{2,1,0:T(8,128)(2,1)}, bf16[288,768]{1,0:T(8,128)(2,1)S(1)}) custom-call(s32[1]{0:T(128)S(6)} %copy.10.count, bf16[96,768]{1,0:T(8,128)(2,1)} %wq.1, bf16[96,768]{1,0:T(8,128)(2,1)} %wk.1, bf16[96,768]{1,0:T(8,128)(2,1)} %wv.1, ...), custom_call_target="tpu_custom_call" | custom-call | tf_op jit(solution)/shard_map/pallas_call | solution.py:365
  3.6 3.0 %collective-permute-start.14 = (bf16[3,104,192]{2,1,0:T(8,128)(2,1)}, bf16[3,104,192]{2,1,0:T(8,128)(2,1)S(1)}, u32[]{:S(2)}, u32[]{:S(2)}) collective-permute-start(bf16[3,104,192]{2,1,0:T(8,128)(2,1)} %get-tuple-element.17), channel_id=1, source_target_pairs={{0,2},{1,3},{2,0},{3,1},{4,6},{5,7},{6,4},{7,5},{8,10},{9,11},{10,... | collective-permute-start | bytes 359432 | tf_op jit(solution)/shard_map/ppermute | solution.py:349
  9.0 2.0 %collective-permute-start = (bf16[96,768]{1,0:T(8,128)(2,1)S(1)}, bf16[96,768]{1,0:T(8,128)(2,1)S(1)}, u32[]{:S(2)}, u32[]{:S(2)}) collective-permute-start(bf16[96,768]{1,0:T(8,128)(2,1)S(1)} %get-tuple-element.31.refs_0_), channel_id=1, source_target_pairs={{0,2},{1,3},{2,0},{3,1},{4,6},{5,7},{6,4},{7,5},{8,10},{9,11},{10,... | collective-permute-start | bytes 442376 | tf_op jit(solution)/shard_map/ppermute | solution.py:349
  11.6 2.0 %collective-permute-start.3 = (bf16[96,768]{1,0:T(8,128)(2,1)S(1)}, bf16[96,768]{1,0:T(8,128)(2,1)S(1)}, u32[]{:S(2)}, u32[]{:S(2)}) collective-permute-start(bf16[96,768]{1,0:T(8,128)(2,1)S(1)} %get-tuple-element.30.refs_1_), channel_id=1, source_target_pairs={{0,4},{1,5},{2,6},{3,7},{4,0},{5,1},{6,2},{7,3},{8,12},{9,13},{10,... | collective-permute-start | bytes 442376 | tf_op jit(solution)/shard_map/ppermute | solution.py:349
  13.6 2.3 %collective-permute-done.15.refs_18_ = bf16[3,104,192]{2,1,0:T(8,128)(2,1)S(1)} collective-permute-done((bf16[3,104,192]{2,1,0:T(8,128)(2,1)}, bf16[3,104,192]{2,1,0:T(8,128)(2,1)S(1)}, u32[]{:S(2)}, u32[]{:S(2)}) %collective-permute-start.15) | collective-permute-done | bytes 119840 | tf_op jit(solution)/shard_map/ppermute | solution.py:349
  15.9 2.4 %collective-permute-start.2 = (bf16[96,768]{1,0:T(8,128)(2,1)S(1)}, bf16[96,768]{1,0:T(8,128)(2,1)S(1)}, u32[]{:S(2)}, u32[]{:S(2)}) collective-permute-start(bf16[96,768]{1,0:T(8,128)(2,1)S(1)} %get-tuple-element.31.refs_0_), channel_id=1, source_target_pairs={{0,4},{1,5},{2,6},{3,7},{4,0},{5,1},{6,2},{7,3},{8,12},{9,13},{10,... | collective-permute-start | bytes 442376 | tf_op jit(solution)/shard_map/ppermute | solution.py:349
  19.1 3.0 %collective-permute-done.2.refs_4_ = bf16[96,768]{1,0:T(8,128)(2,1)S(1)} collective-permute-done((bf16[96,768]{1,0:T(8,128)(2,1)S(1)}, bf16[96,768]{1,0:T(8,128)(2,1)S(1)}, u32[]{:S(2)}, u32[]{:S(2)}) %collective-permute-start.2) | collective-permute-done | bytes 147488 | tf_op jit(solution)/shard_map/ppermute | solution.py:349
  25.2 4.5 %collective-permute-done.4.refs_6_ = bf16[96,768]{1,0:T(8,128)(2,1)S(1)} collective-permute-done((bf16[96,768]{1,0:T(8,128)(2,1)S(1)}, bf16[96,768]{1,0:T(8,128)(2,1)S(1)}, u32[]{:S(2)}, u32[]{:S(2)}) %collective-permute-start.4) | collective-permute-done | bytes 147488 | tf_op jit(solution)/shard_map/ppermute | solution.py:349
  30.2 1.6 %collective-permute-start.25 = (bf16[288,768]{1,0:T(8,128)(2,1)S(1)}, bf16[288,768]{1,0:T(8,128)(2,1)S(1)}, u32[]{:S(2)}, u32[]{:S(2)}) collective-permute-start(bf16[288,768]{1,0:T(8,128)(2,1)S(1)} %get-tuple-element.24.refs_4_.refs_2_.refs_6_), channel_id=1, source_target_pairs={{0,4},{1,5},{2,6},{3,7},{4,0},{5,1},{6,2},{7,3},{8,12},{9,13},{10,... | collective-permute-start | bytes 1327112 | tf_op jit(solution)/shard_map/ppermute | solution.py:349
  31.7 1.5 %collective-permute-start.26 = (bf16[288,768]{1,0:T(8,128)(2,1)S(1)}, bf16[288,768]{1,0:T(8,128)(2,1)S(1)}, u32[]{:S(2)}, u32[]{:S(2)}) collective-permute-start(bf16[288,768]{1,0:T(8,128)(2,1)S(1)} %get-tuple-element.24.refs_4_.refs_2_.refs_6_), channel_id=1, source_target_pairs={{0,6},{1,7},{2,4},{3,5},{4,2},{5,3},{6,0},{7,1},{8,14},{9,15},{10,... | collective-permute-start | bytes 1327112 | tf_op jit(solution)/shard_map/ppermute | solution.py:349
  36.7 9.4 %shard_map.96 = (bf16[192,192]{1,0:T(8,128)(2,1)S(1)}, bf16[192,192]{1,0:T(8,128)(2,1)S(1)}, bf16[192,192]{1,0:T(8,128)(2,1)S(1)}, bf16[192,192]{1,0:T(8,128)(2,...) custom-call(s32[1]{0:T(128)S(6)} %copy.10.count, ...), custom_call_target="tpu_custom_call" | custom-call | tf_op jit(solution)/shard_map/pallas_call | solution.py:400
  46.1 5.8 %collective-permute-done.26.refs_7_.refs_5_ = bf16[288,768]{1,0:T(8,128)(2,1)S(1)} collective-permute-done((bf16[288,768]{1,0:T(8,128)(2,1)S(1)}, bf16[288,768]{1,0:T(8,128)(2,1)S(1)}, u32[]{:S(2)}, u32[]{:S(2)}) %collective-permute-start.26) | collective-permute-done | bytes 442400 | tf_op jit(solution)/shard_map/ppermute | solution.py:349
  51.8 3.8 %shard_map.98 = (bf16[4,96,192]{2,1,0:T(8,128)(2,1)S(1)}, bf16[4,96,192]{2,1,0:T(8,128)(2,1)S(1)}) custom-call(bf16[4,3,192,1536]{3,2,1,0:T(8,128)(2,1)S(1)} %get-tuple-element.25.refs_0_, bf16[1536,768]{1,0:T(8,128)(2,1)S(1)} %get-tuple-element.26.refs_1_, bf16[288,768]{1,0:T(8,128)(2,1)S(1)} %get-tuple-element.24.refs_4_.refs_2_.refs_6_, ...), custom_call_target="tpu_custom_call" | custom-call | tf_op jit(solution)/shard_map/pallas_call | solution.py:407
  58.7 2.6 %collective-permute-start.33 = (bf16[96,192]{1,0:T(8,128)(2,1)S(1)}, bf16[96,192]{1,0:T(8,128)(2,1)S(1)}, u32[]{:S(2)}, u32[]{:S(2)}) collective-permute-start(bf16[96,192]{1,0:T(8,128)(2,1)S(1)} %get-tuple-element.38), channel_id=1, source_target_pairs={{0,16},{8,24},{16,0},{24,8},{1,17},{9,25},{17,1},{25,9},{2,18},{10... | collective-permute-start | bytes 110600 | tf_op jit(solution)/shard_map/ppermute | solution.py:431
  62.3 2.3 %collective-permute-done.33 = bf16[96,192]{1,0:T(8,128)(2,1)S(1)} collective-permute-done((bf16[96,192]{1,0:T(8,128)(2,1)S(1)}, bf16[96,192]{1,0:T(8,128)(2,1)S(1)}, u32[]{:S(2)}, u32[]{:S(2)}) %collective-permute-start.33) | collective-permute-done | bytes 36896 | tf_op jit(solution)/shard_map/ppermute | solution.py:431
  64.6 2.6 %collective-permute-done.34 = bf16[96,192]{1,0:T(8,128)(2,1)S(1)} collective-permute-done((bf16[96,192]{1,0:T(8,128)(2,1)S(1)}, bf16[96,192]{1,0:T(8,128)(2,1)S(1)}, u32[]{:S(2)}, u32[]{:S(2)}) %collective-permute-start.34) | collective-permute-done | bytes 36896 | tf_op jit(solution)/shard_map/ppermute | solution.py:431
  68.9 6.9 %collective-permute-done.35 = bf16[96,192]{1,0:T(8,128)(2,1)S(1)} collective-permute-done((bf16[96,192]{1,0:T(8,128)(2,1)}, bf16[96,192]{1,0:T(8,128)(2,1)S(1)}, u32[]{:S(2)}, u32[]{:S(2)}) %collective-permute-start.35) | collective-permute-done | bytes 36896 | tf_op jit(solution)/shard_map/ppermute | solution.py:439
  75.8 2.1 %collective-permute-start.38 = (bf16[96,192]{1,0:T(8,128)(2,1)}, bf16[96,192]{1,0:T(8,128)(2,1)}, u32[]{:S(2)}, u32[]{:S(2)}) collective-permute-start(bf16[96,192]{1,0:T(8,128)(2,1)} %fusion.2), channel_id=1, source_target_pairs={{0,0},{1,1},{2,2},{3,3},{4,4},{5,5},{6,6},{7,7},{8,10},{9,11},{10,... | collective-permute-start | bytes 110600 | tf_op jit(solution)/shard_map/ppermute | solution.py:439
  77.8 3.2 %collective-permute-done.37 = bf16[96,192]{1,0:T(8,128)(2,1)S(1)} collective-permute-done((bf16[96,192]{1,0:T(8,128)(2,1)}, bf16[96,192]{1,0:T(8,128)(2,1)S(1)}, u32[]{:S(2)}, u32[]{:S(2)}) %collective-permute-start.37) | collective-permute-done | bytes 36896 | tf_op jit(solution)/shard_map/ppermute | solution.py:439
  81.1 1.8 %collective-permute-start.21 = (bf16[192,192]{1,0:T(8,128)(2,1)}, bf16[192,192]{1,0:T(8,128)(2,1)S(1)}, u32[]{:S(2)}, u32[]{:S(2)}) collective-permute-start(bf16[192,192]{1,0:T(8,128)(2,1)} %copy-done), channel_id=1, source_target_pairs={{0,2},{1,3},{2,0},{3,1},{4,6},{5,7},{6,4},{7,5},{8,10},{9,11},{10,... | collective-permute-start | bytes 221192 | tf_op jit(solution)/shard_map/ppermute | solution.py:349
  84.3 2.5 %collective-permute-done.21.refs_1_ = bf16[192,192]{1,0:T(8,128)(2,1)S(1)} collective-permute-done((bf16[192,192]{1,0:T(8,128)(2,1)}, bf16[192,192]{1,0:T(8,128)(2,1)S(1)}, u32[]{:S(2)}, u32[]{:S(2)}) %collective-permute-start.21) | collective-permute-done | bytes 73760 | tf_op jit(solution)/shard_map/ppermute | solution.py:349
  86.8 1.8 %collective-permute-start.23 = (bf16[192,192]{1,0:T(8,128)(2,1)S(1)}, bf16[192,192]{1,0:T(8,128)(2,1)S(1)}, u32[]{:S(2)}, u32[]{:S(2)}) collective-permute-start(bf16[192,192]{1,0:T(8,128)(2,1)S(1)} %get-tuple-element.23), channel_id=1, source_target_pairs={{0,6},{1,7},{2,4},{3,5},{4,2},{5,3},{6,0},{7,1},{8,14},{9,15},{10,... | collective-permute-start | bytes 221192 | tf_op jit(solution)/shard_map/ppermute | solution.py:349
  89.4 2.9 %collective-permute-done.23.refs_3_ = bf16[192,192]{1,0:T(8,128)(2,1)S(1)} collective-permute-done((bf16[192,192]{1,0:T(8,128)(2,1)S(1)}, bf16[192,192]{1,0:T(8,128)(2,1)S(1)}, u32[]{:S(2)}, u32[]{:S(2)}) %collective-permute-start.23) | collective-permute-done | bytes 73760 | tf_op jit(solution)/shard_map/ppermute | solution.py:349
  92.3 2.3 %shard_map.97 = bf16[1,192,768]{2,1,0:T(8,128)(2,1)} custom-call(bf16[192,192]{1,0:T(8,128)(2,1)S(1)} %get-tuple-element.20.refs_0_, bf16[192,192]{1,0:T(8,128)(2,1)S(1)} %collective-permute-done.21.refs_1_, bf16[192,192]{1,0:T(8,128)(2,1)S(1)} %collective-permute-done.22.refs_2_, bf16[192,192]{1,0:T(8,128)(2,1)S(1)} %collective-permute-done.23.refs_3_, ...), custom_call_target="tpu_custom_call" | custom-call | tf_op jit(solution)/shard_map/pallas_call | solution.py:418
  (66 shorter events, 18.7 us)
Async XLA Ops:
  3.6 8.1 %collective-permute-start.14 = (bf16[3,104,192]{2,1,0:T(8,128)(2,1)}, bf16[3,104,192]{2,1,0:T(8,128)(2,1)S(1)}, u32[]{:S(2)}, u32[]{:S(2)}) collective-permute-start(bf16[3,104,192]{2,1,0:T(8,128)(2,1)} %get-tuple-element.17), channel_id=1, source_target_pairs={{0,2},{1,3},{2,0},{3,1},{4,6},{5,7},{6,4},{7,5},{8,10},{9,11},{10,... | collective-permute-start | bytes 359432 | tf_op jit(solution)/shard_map/ppermute | solution.py:349
  6.5 9.4 %collective-permute-start.15 = (bf16[3,104,192]{2,1,0:T(8,128)(2,1)}, bf16[3,104,192]{2,1,0:T(8,128)(2,1)S(1)}, u32[]{:S(2)}, u32[]{:S(2)}) collective-permute-start(bf16[3,104,192]{2,1,0:T(8,128)(2,1)} %get-tuple-element.18), channel_id=1, source_target_pairs={{0,4},{1,5},{2,6},{3,7},{4,0},{5,1},{6,2},{7,3},{8,12},{9,13},{10,... | collective-permute-start | bytes 359432 | tf_op jit(solution)/shard_map/ppermute | solution.py:349
  8.0 10.3 %collective-permute-start.16 = (bf16[3,104,192]{2,1,0:T(8,128)(2,1)}, bf16[3,104,192]{2,1,0:T(8,128)(2,1)S(1)}, u32[]{:S(2)}, u32[]{:S(2)}) collective-permute-start(bf16[3,104,192]{2,1,0:T(8,128)(2,1)} %get-tuple-element.19), channel_id=1, source_target_pairs={{0,6},{1,7},{2,4},{3,5},{4,2},{5,3},{6,0},{7,1},{8,14},{9,15},{10,... | collective-permute-start | bytes 359432 | tf_op jit(solution)/shard_map/ppermute | solution.py:349
  9.0 9.3 %collective-permute-start = (bf16[96,768]{1,0:T(8,128)(2,1)S(1)}, bf16[96,768]{1,0:T(8,128)(2,1)S(1)}, u32[]{:S(2)}, u32[]{:S(2)}) collective-permute-start(bf16[96,768]{1,0:T(8,128)(2,1)S(1)} %get-tuple-element.31.refs_0_), channel_id=1, source_target_pairs={{0,2},{1,3},{2,0},{3,1},{4,6},{5,7},{6,4},{7,5},{8,10},{9,11},{10,... | collective-permute-start | bytes 442376 | tf_op jit(solution)/shard_map/ppermute | solution.py:349
  11.1 7.2 %collective-permute-start.17 = (bf16[3,104,192]{2,1,0:T(8,128)(2,1)S(1)}, bf16[3,104,192]{2,1,0:T(8,128)(2,1)S(1)}, u32[]{:S(2)}, u32[]{:S(2)}) collective-permute-start(bf16[3,104,192]{2,1,0:T(8,128)(2,1)S(1)} %get-tuple-element.16.refs_16_), channel_id=1, source_target_pairs={{0,1},{1,0},{2,3},{3,2},{4,5},{5,4},{6,7},{7,6},{8,9},{9,8},{10,11... | collective-permute-start | bytes 359432 | tf_op jit(solution)/shard_map/ppermute | solution.py:349
  11.6 7.4 %collective-permute-start.3 = (bf16[96,768]{1,0:T(8,128)(2,1)S(1)}, bf16[96,768]{1,0:T(8,128)(2,1)S(1)}, u32[]{:S(2)}, u32[]{:S(2)}) collective-permute-start(bf16[96,768]{1,0:T(8,128)(2,1)S(1)} %get-tuple-element.30.refs_1_), channel_id=1, source_target_pairs={{0,4},{1,5},{2,6},{3,7},{4,0},{5,1},{6,2},{7,3},{8,12},{9,13},{10,... | collective-permute-start | bytes 442376 | tf_op jit(solution)/shard_map/ppermute | solution.py:349
  15.9 6.1 %collective-permute-start.2 = (bf16[96,768]{1,0:T(8,128)(2,1)S(1)}, bf16[96,768]{1,0:T(8,128)(2,1)S(1)}, u32[]{:S(2)}, u32[]{:S(2)}) collective-permute-start(bf16[96,768]{1,0:T(8,128)(2,1)S(1)} %get-tuple-element.31.refs_0_), channel_id=1, source_target_pairs={{0,4},{1,5},{2,6},{3,7},{4,0},{5,1},{6,2},{7,3},{8,12},{9,13},{10,... | collective-permute-start | bytes 442376 | tf_op jit(solution)/shard_map/ppermute | solution.py:349
  23.4 6.3 %collective-permute-start.4 = (bf16[96,768]{1,0:T(8,128)(2,1)S(1)}, bf16[96,768]{1,0:T(8,128)(2,1)S(1)}, u32[]{:S(2)}, u32[]{:S(2)}) collective-permute-start(bf16[96,768]{1,0:T(8,128)(2,1)S(1)} %collective-permute-done.refs_2_), channel_id=1, source_target_pairs={{0,4},{1,5},{2,6},{3,7},{4,0},{5,1},{6,2},{7,3},{8,12},{9,13},{10,... | collective-permute-start | bytes 442376 | tf_op jit(solution)/shard_map/ppermute | solution.py:349
  24.6 7.1 %collective-permute-start.8 = (bf16[96,768]{1,0:T(8,128)(2,1)S(1)}, bf16[96,768]{1,0:T(8,128)(2,1)S(1)}, u32[]{:S(2)}, u32[]{:S(2)}) collective-permute-start(bf16[96,768]{1,0:T(8,128)(2,1)S(1)} %collective-permute-done.refs_2_), channel_id=1, source_target_pairs={{0,1},{1,0},{2,3},{3,2},{4,5},{5,4},{6,7},{7,6},{8,9},{9,8},{10,11... | collective-permute-start | bytes 442376 | tf_op jit(solution)/shard_map/ppermute | solution.py:349
  25.1 8.1 %collective-permute-start.10 = (bf16[96,768]{1,0:T(8,128)(2,1)S(1)}, bf16[96,768]{1,0:T(8,128)(2,1)S(1)}, u32[]{:S(2)}, u32[]{:S(2)}) collective-permute-start(bf16[96,768]{1,0:T(8,128)(2,1)S(1)} %collective-permute-done.2.refs_4_), channel_id=1, source_target_pairs={{0,1},{1,0},{2,3},{3,2},{4,5},{5,4},{6,7},{7,6},{8,9},{9,8},{10,11... | collective-permute-start | bytes 442376 | tf_op jit(solution)/shard_map/ppermute | solution.py:349
  29.8 16.3 %collective-permute-start.24 = (bf16[288,768]{1,0:T(8,128)(2,1)S(1)}, bf16[288,768]{1,0:T(8,128)(2,1)S(1)}, u32[]{:S(2)}, u32[]{:S(2)}) collective-permute-start(bf16[288,768]{1,0:T(8,128)(2,1)S(1)} %get-tuple-element.24.refs_4_.refs_2_.refs_6_), channel_id=1, source_target_pairs={{0,2},{1,3},{2,0},{3,1},{4,6},{5,7},{6,4},{7,5},{8,10},{9,11},{10,... | collective-permute-start | bytes 1327112 | tf_op jit(solution)/shard_map/ppermute | solution.py:349
  30.2 15.9 %collective-permute-start.25 = (bf16[288,768]{1,0:T(8,128)(2,1)S(1)}, bf16[288,768]{1,0:T(8,128)(2,1)S(1)}, u32[]{:S(2)}, u32[]{:S(2)}) collective-permute-start(bf16[288,768]{1,0:T(8,128)(2,1)S(1)} %get-tuple-element.24.refs_4_.refs_2_.refs_6_), channel_id=1, source_target_pairs={{0,4},{1,5},{2,6},{3,7},{4,0},{5,1},{6,2},{7,3},{8,12},{9,13},{10,... | collective-permute-start | bytes 1327112 | tf_op jit(solution)/shard_map/ppermute | solution.py:349
  31.7 20.1 %collective-permute-start.26 = (bf16[288,768]{1,0:T(8,128)(2,1)S(1)}, bf16[288,768]{1,0:T(8,128)(2,1)S(1)}, u32[]{:S(2)}, u32[]{:S(2)}) collective-permute-start(bf16[288,768]{1,0:T(8,128)(2,1)S(1)} %get-tuple-element.24.refs_4_.refs_2_.refs_6_), channel_id=1, source_target_pairs={{0,6},{1,7},{2,4},{3,5},{4,2},{5,3},{6,0},{7,1},{8,14},{9,15},{10,... | collective-permute-start | bytes 1327112 | tf_op jit(solution)/shard_map/ppermute | solution.py:349
  33.3 18.6 %collective-permute-start.27 = (bf16[288,768]{1,0:T(8,128)(2,1)S(1)}, bf16[288,768]{1,0:T(8,128)(2,1)S(1)}, u32[]{:S(2)}, u32[]{:S(2)}) collective-permute-start(bf16[288,768]{1,0:T(8,128)(2,1)S(1)} %get-tuple-element.24.refs_4_.refs_2_.refs_6_), channel_id=1, source_target_pairs={{0,1},{1,0},{2,3},{3,2},{4,5},{5,4},{6,7},{7,6},{8,9},{9,8},{10,11... | collective-permute-start | bytes 1327112 | tf_op jit(solution)/shard_map/ppermute | solution.py:349
  58.7 5.9 %collective-permute-start.33 = (bf16[96,192]{1,0:T(8,128)(2,1)S(1)}, bf16[96,192]{1,0:T(8,128)(2,1)S(1)}, u32[]{:S(2)}, u32[]{:S(2)}) collective-permute-start(bf16[96,192]{1,0:T(8,128)(2,1)S(1)} %get-tuple-element.38), channel_id=1, source_target_pairs={{0,16},{8,24},{16,0},{24,8},{1,17},{9,25},{17,1},{25,9},{2,18},{10... | collective-permute-start | bytes 110600 | tf_op jit(solution)/shard_map/ppermute | solution.py:431
  61.3 5.9 %collective-permute-start.34 = (bf16[96,192]{1,0:T(8,128)(2,1)S(1)}, bf16[96,192]{1,0:T(8,128)(2,1)S(1)}, u32[]{:S(2)}, u32[]{:S(2)}) collective-permute-start(bf16[96,192]{1,0:T(8,128)(2,1)S(1)} %get-tuple-element.37), channel_id=1, source_target_pairs={{0,24},{8,16},{16,8},{24,0},{1,25},{9,17},{17,9},{25,1},{2,26},{10... | collective-permute-start | bytes 110600 | tf_op jit(solution)/shard_map/ppermute | solution.py:431
  61.7 30.6 %collective-permute-start.28 = (bf16[288,768]{1,0:T(8,128)(2,1)S(1)}, bf16[288,768]{1,0:T(8,128)(2,1)S(1)}, u32[]{:S(2)}, u32[]{:S(2)}) collective-permute-start(bf16[288,768]{1,0:T(8,128)(2,1)S(1)} %collective-permute-done.24.refs_5_.refs_3_), channel_id=1, source_target_pairs={{0,1},{1,0},{2,3},{3,2},{4,5},{5,4},{6,7},{7,6},{8,9},{9,8},{10,11... | collective-permute-start | bytes 1327112 | tf_op jit(solution)/shard_map/ppermute | solution.py:349
  61.7 30.6 %collective-permute-start.29 = (bf16[288,768]{1,0:T(8,128)(2,1)S(1)}, bf16[288,768]{1,0:T(8,128)(2,1)S(1)}, u32[]{:S(2)}, u32[]{:S(2)}) collective-permute-start(bf16[288,768]{1,0:T(8,128)(2,1)S(1)} %collective-permute-done.25.refs_6_.refs_4_), channel_id=1, source_target_pairs={{0,1},{1,0},{2,3},{3,2},{4,5},{5,4},{6,7},{7,6},{8,9},{9,8},{10,11... | collective-permute-start | bytes 1327112 | tf_op jit(solution)/shard_map/ppermute | solution.py:349
  62.2 30.1 %collective-permute-start.30 = (bf16[288,768]{1,0:T(8,128)(2,1)S(1)}, bf16[288,768]{1,0:T(8,128)(2,1)}, u32[]{:S(2)}, u32[]{:S(2)}) collective-permute-start(bf16[288,768]{1,0:T(8,128)(2,1)S(1)} %collective-permute-done.26.refs_7_.refs_5_), channel_id=1, source_target_pairs={{0,1},{1,0},{2,3},{3,2},{4,5},{5,4},{6,7},{7,6},{8,9},{9,8},{10,11... | collective-permute-start | bytes 1327112 | tf_op jit(solution)/shard_map/ppermute | solution.py:349
  67.8 7.9 %collective-permute-start.35 = (bf16[96,192]{1,0:T(8,128)(2,1)}, bf16[96,192]{1,0:T(8,128)(2,1)S(1)}, u32[]{:S(2)}, u32[]{:S(2)}) collective-permute-start(bf16[96,192]{1,0:T(8,128)(2,1)} %fusion.2), channel_id=1, source_target_pairs={{0,24},{1,25},{2,26},{3,27},{4,28},{5,29},{6,30},{7,31},{8,18},{9,... | collective-permute-start | bytes 110600 | tf_op jit(solution)/shard_map/ppermute | solution.py:439
  68.9 6.9 %collective-permute-start.36 = (bf16[96,192]{1,0:T(8,128)(2,1)}, bf16[96,192]{1,0:T(8,128)(2,1)S(1)}, u32[]{:S(2)}, u32[]{:S(2)}) collective-permute-start(bf16[96,192]{1,0:T(8,128)(2,1)} %fusion.2), channel_id=1, source_target_pairs={{0,16},{1,17},{2,18},{3,19},{4,20},{5,21},{6,22},{7,23},{8,26},{9,... | collective-permute-start | bytes 110600 | tf_op jit(solution)/shard_map/ppermute | solution.py:439
  75.8 7.1 %collective-permute-start.38 = (bf16[96,192]{1,0:T(8,128)(2,1)}, bf16[96,192]{1,0:T(8,128)(2,1)}, u32[]{:S(2)}, u32[]{:S(2)}) collective-permute-start(bf16[96,192]{1,0:T(8,128)(2,1)} %fusion.2), channel_id=1, source_target_pairs={{0,0},{1,1},{2,2},{3,3},{4,4},{5,5},{6,6},{7,7},{8,10},{9,11},{10,... | collective-permute-start | bytes 110600 | tf_op jit(solution)/shard_map/ppermute | solution.py:439
  81.1 5.8 %collective-permute-start.21 = (bf16[192,192]{1,0:T(8,128)(2,1)}, bf16[192,192]{1,0:T(8,128)(2,1)S(1)}, u32[]{:S(2)}, u32[]{:S(2)}) collective-permute-start(bf16[192,192]{1,0:T(8,128)(2,1)} %copy-done), channel_id=1, source_target_pairs={{0,2},{1,3},{2,0},{3,1},{4,6},{5,7},{6,4},{7,5},{8,10},{9,11},{10,... | collective-permute-start | bytes 221192 | tf_op jit(solution)/shard_map/ppermute | solution.py:349
  82.9 6.5 %collective-permute-start.22 = (bf16[192,192]{1,0:T(8,128)(2,1)S(1)}, bf16[192,192]{1,0:T(8,128)(2,1)S(1)}, u32[]{:S(2)}, u32[]{:S(2)}) collective-permute-start(bf16[192,192]{1,0:T(8,128)(2,1)S(1)} %get-tuple-element.22), channel_id=1, source_target_pairs={{0,4},{1,5},{2,6},{3,7},{4,0},{5,1},{6,2},{7,3},{8,12},{9,13},{10,... | collective-permute-start | bytes 221192 | tf_op jit(solution)/shard_map/ppermute | solution.py:349
  (16 other events, 77.5 us)

commit v6 on v5

--- a/solution.py
+++ b/solution.py
@@ -31,7 +31,6 @@
 def pack_kernel(hg, tg, wr, cw, count, wq, wk, wv, seg, cot, wout, *outs):
     group = lax.axis_index("seq") // tg
     rows = cot.shape[0]
-    merged = outs[hg]
     for k in range(hg):
         for part in range(hg):
 
@@ -46,9 +45,21 @@
             outs[k][i, wr:] = jnp.broadcast_to(seg[...], (8, cw)).astype(jnp.bfloat16)
     position = lax.axis_index("seq") * rows + lax.broadcasted_iota(jnp.int32, cot.shape, 0)
     masked = jnp.where(position < count[0], cot[...].astype(jnp.float32), 0.0)
-    merged[:rows, :] = masked.astype(jnp.bfloat16)
-    if merged.shape[0] > rows:
-        merged[rows:, :] = wout[...]
+    outs[hg][...] = masked.astype(jnp.bfloat16)
+    outs[hg + 1][...] = wout[...]
+
+
+def column_kernel(hg, tg, cw, by_dp, *refs):
+    pieces, out = refs[:hg], refs[hg]
+    index = lax.axis_index("seq") // tg
+    if by_dp:
+        index = index ^ lax.axis_index("dp")
+    for part in range(hg):
+        for m in range(hg):
+
+            @pl.when((index ^ part) == m)
+            def _():
+                out[:, part * cw : (part + 1) * cw] = pieces[m][...].astype(jnp.float32)
 
 
 def place_rows(scratch, pieces, member, wr):
@@ -341,8 +352,6 @@
     cw = width // hg
     head_dim = width // HEADS
     by_dp = dp == hg
-    own = lax.axis_index("seq")
-    group = own // tg
     bf16 = jnp.bfloat16
 
     def hop(x, step):
@@ -360,15 +369,14 @@
     wide = bf16 if wr % 16 == 0 else jnp.float32
     parts = 2 if hg == 4 and rows % 32 == 0 else 1
     segment_line = segment_of.reshape(1, rows)
-    joined = fits(n * rows)
-    own_shape = pltpu.VMEM if joined else jax.ShapeDtypeStruct
-    *packed, merged = pl.pallas_call(
+    own_shape = pltpu.VMEM if fits(n * rows) else jax.ShapeDtypeStruct
+    *packed, own_cot, own_wout = pl.pallas_call(
         functools.partial(pack_kernel, hg, tg, wr, cw),
         out_shape=[own_shape((3, wr + 8, cw), bf16)]
         + [jax.ShapeDtypeStruct((3, wr + 8, cw), bf16)] * (hg - 1)
-        + [own_shape((rows + wr if joined else rows, width), bf16)],
+        + [own_shape((rows, width), bf16), own_shape((wr, width), bf16)],
         in_specs=[SM] + [VM] * 6,
-        out_specs=[VM] * (hg + 1),
+        out_specs=[VM] * (hg + 2),
     )(tissue_count, w_query, w_key, w_value, segment_line, cotangent[0], w_out)
     weight_table = over_members(over_groups(packed))
     if parts == 2:
@@ -386,11 +394,8 @@
         for piece in tile_pieces
     ]
     flat_tiles = [x for piece in tile_pieces for x in piece]
-    cots = over_groups([merged] * hg)
-    if joined:
-        wout_table = over_members(cots)
-    else:
-        wout_table = over_members(over_groups([w_out] * hg))
+    cots = over_groups([own_cot] * hg)
+    wout_table = over_members(over_groups([own_wout] + [w_out] * (hg - 1)))
 
     def near_core(arrays):
         if not fits(n * rows):
@@ -425,7 +430,6 @@
     )(*near_core(attention), *near_core(flat(wout_table)))
 
     if by_dp:
-        own_dp = lax.axis_index("dp")
         mine = summed[0].astype(jnp.float32)
         for m in range(1, hg):
             got = lax.ppermute(summed[m], "dp", [(z, z ^ m) for z in range(dp)])
@@ -437,18 +441,17 @@
                 (z * n + s, (z ^ m) * n + (s ^ (z * tg))) for z in range(dp) for s in range(n)
             ]
             pieces.append(lax.ppermute(mine, ("dp", "seq"), pairs))
-        index = group ^ own_dp
     else:
         total = lax.psum(summed, "dp")
         pieces = over_groups([total[k] for k in range(hg)])
-        index = group
-    columns = []
-    for p in range(hg):
-        piece = pieces[0]
-        for m in range(1, hg):
-            piece = jnp.where((index ^ p) == m, pieces[m], piece)
-        columns.append(piece)
-    return (layer_rows, jnp.concatenate(columns, axis=1).astype(jnp.float32))
+    grad = pl.pallas_call(
+        functools.partial(column_kernel, hg, tg, cw, by_dp),
+        out_shape=jax.ShapeDtypeStruct((wr, width), jnp.float32),
+        in_specs=[VM] * hg,
+        out_specs=VM,
+        compiler_params=SMALL,
+    )(*near_core(pieces))
+    return (layer_rows, grad)
 
 
 def solution(mesh):

time: 94.9 us -> 84.3 us (0.89)
  waiting for transfers between devices: 42.3 us -> 25.2 us
  starting transfers between devices: 29.7 us -> 38.6 us
  other arithmetic: 2.35 us -> 0.08 us
    ppermute x32 -> x35, waiting for transfers between devices: 27.4 us -> 18.7 us  [hop(): return lax.ppermute(x, 'seq', [(s, s ^ step) for s in range(n)])]
    ppermute x3, waiting for transfers between devices: 4.89 us -> 0.1 us  [local(): got = lax.ppermute(summed[m], 'dp', [(z, z ^ m) for z in range(dp)])]
    ppermute x4, starting transfers between devices: 3.11 us -> 7.58 us  [local(): pieces.append(lax.ppermute(mine, ('dp', 'seq'), pairs))]
    ppermute x4, waiting for transfers between devices: 10.1 us -> 6.39 us  [local(): pieces.append(lax.ppermute(mine, ('dp', 'seq'), pairs))]
    ppermute x3, starting transfers between devices: 4.45 us -> 7.45 us  [local(): got = lax.ppermute(summed[m], 'dp', [(z, z ^ m) for z in range(dp)])]
    ppermute x32 -> x35, starting transfers between devices: 22.2 us -> 23.6 us  [hop(): return lax.ppermute(x, 'seq', [(s, s ^ step) for s in range(n)])]
    pallas_call x1, Pallas kernels: 2.27 us -> 1.28 us  [local(): pl.pallas_call(functools.partial(proj_kernel, hg, tg, wr), out_shape=jax....]
  transfers between devices with their start and end apart: 39 -> 42, of which waited for: 17 -> 13; matrix products, arithmetic and copies ran while one was open for 3% -> 1% of each run, Pallas kernels for 10% -> 17%
where the time goes in v6:
time: 84.3 us; the launch traced here: 84.1 us
  starting transfers between devices  38.6 us (46%)
  waiting for transfers between devices  25.2 us (30%)
  Pallas kernels  17.7 us (21%)
  between operations  1.46 us (2%)
  local copies, waits for them, and re-layouts  1.02 us (1%)
    ppermute x35, starting transfers between devices, hop(): return lax.ppermute(x, 'seq', [(s, s ^ step) for s in range(n)])  23.6 us
    ppermute x35, waiting for transfers between devices, hop(): return lax.ppermute(x, 'seq', [(s, s ^ step) for s in range(n)])  18.7 us
    pallas_call x1, Pallas kernels, local(): attention_call(hg, tg, parts, rows, width, wr, cw, head_dim)  9.38 us
    ppermute x4, starting transfers between devices, local(): pieces.append(lax.ppermute(mine, ('dp', 'seq'), pairs))  7.58 us
    ppermute x3, starting transfers between devices, local(): got = lax.ppermute(summed[m], 'dp', [(z, z ^ m) for z in range(dp)])  7.45 us
    ppermute x4, waiting for transfers between devices, local(): pieces.append(lax.ppermute(mine, ('dp', 'seq'), pairs))  6.39 us
    pallas_call x1, Pallas kernels, local(): gradient_call(hg, tg, parts, rows, width, wr, cw, head_dim, by_dp)  3.81 us
    pallas_call x1, Pallas kernels, local(): pl.pallas_call(functools.partial(pack_kernel, hg, tg, wr, cw), out_shape=...  2.3 us
  transfers between devices with their start and end apart: 42, of which 13 were waited for; matrix products, arithmetic and copies ran while one was open for 1% of the time, Pallas kernels for 17%

profile of v6, /device:TPU:0, one launch (start us, length us, event | category | flops | bytes accessed | tf_op | source)
XLA Modules:
  0.0 84.1 jit_solution(16660415668334505611)
XLA Ops:
  1.3 2.3 %shard_map.95 = (bf16[3,104,192]{2,1,0:T(8,128)(2,1)S(1)}, bf16[3,104,192]{2,1,0:T(8,128)(2,1)}, bf16[3,104,192]{2,1,0:T(8,128)(2,1)}, bf16[3,104,192]{2,1,0:T(8...) custom-call(s32[1]{0:T(128)S(6)} %copy.10.count, bf16[96,768]{1,0:T(8,128)(2,1)} %wq.1, ...), custom_call_target="tpu_custom_call" | custom-call | tf_op jit(solution)/shard_map/pallas_call | solution.py:373
  3.6 3.0 %collective-permute-start.14 = (bf16[3,104,192]{2,1,0:T(8,128)(2,1)}, bf16[3,104,192]{2,1,0:T(8,128)(2,1)S(1)}, u32[]{:S(2)}, u32[]{:S(2)}) collective-permute-start(bf16[3,104,192]{2,1,0:T(8,128)(2,1)} %get-tuple-element.18), channel_id=1, source_target_pairs={{0,2},{1,3},{2,0},{3,1},{4,6},{5,7},{6,4},{7,5},{8,10},{9,11},{10,... | collective-permute-start | bytes 359432 | tf_op jit(solution)/shard_map/ppermute | solution.py:358
  6.5 1.5 %collective-permute-start.15 = (bf16[3,104,192]{2,1,0:T(8,128)(2,1)}, bf16[3,104,192]{2,1,0:T(8,128)(2,1)S(1)}, u32[]{:S(2)}, u32[]{:S(2)}) collective-permute-start(bf16[3,104,192]{2,1,0:T(8,128)(2,1)} %get-tuple-element.19), channel_id=1, source_target_pairs={{0,4},{1,5},{2,6},{3,7},{4,0},{5,1},{6,2},{7,3},{8,12},{9,13},{10,... | collective-permute-start | bytes 359432 | tf_op jit(solution)/shard_map/ppermute | solution.py:358
  9.1 2.0 %collective-permute-start = (bf16[96,768]{1,0:T(8,128)(2,1)S(1)}, bf16[96,768]{1,0:T(8,128)(2,1)S(1)}, u32[]{:S(2)}, u32[]{:S(2)}) collective-permute-start(bf16[96,768]{1,0:T(8,128)(2,1)S(1)} %get-tuple-element.33.refs_0_), channel_id=1, source_target_pairs={{0,2},{1,3},{2,0},{3,1},{4,6},{5,7},{6,4},{7,5},{8,10},{9,11},{10,... | collective-permute-start | bytes 442376 | tf_op jit(solution)/shard_map/ppermute | solution.py:358
  11.6 2.0 %collective-permute-start.3 = (bf16[96,768]{1,0:T(8,128)(2,1)S(1)}, bf16[96,768]{1,0:T(8,128)(2,1)S(1)}, u32[]{:S(2)}, u32[]{:S(2)}) collective-permute-start(bf16[96,768]{1,0:T(8,128)(2,1)S(1)} %get-tuple-element.32.refs_1_), channel_id=1, source_target_pairs={{0,4},{1,5},{2,6},{3,7},{4,0},{5,1},{6,2},{7,3},{8,12},{9,13},{10,... | collective-permute-start | bytes 442376 | tf_op jit(solution)/shard_map/ppermute | solution.py:358
  13.7 2.3 %collective-permute-done.15.refs_18_ = bf16[3,104,192]{2,1,0:T(8,128)(2,1)S(1)} collective-permute-done((bf16[3,104,192]{2,1,0:T(8,128)(2,1)}, bf16[3,104,192]{2,1,0:T(8,128)(2,1)S(1)}, u32[]{:S(2)}, u32[]{:S(2)}) %collective-permute-start.15) | collective-permute-done | bytes 119840 | tf_op jit(solution)/shard_map/ppermute | solution.py:358
  15.9 2.4 %collective-permute-start.2 = (bf16[96,768]{1,0:T(8,128)(2,1)S(1)}, bf16[96,768]{1,0:T(8,128)(2,1)S(1)}, u32[]{:S(2)}, u32[]{:S(2)}) collective-permute-start(bf16[96,768]{1,0:T(8,128)(2,1)S(1)} %get-tuple-element.33.refs_0_), channel_id=1, source_target_pairs={{0,4},{1,5},{2,6},{3,7},{4,0},{5,1},{6,2},{7,3},{8,12},{9,13},{10,... | collective-permute-start | bytes 442376 | tf_op jit(solution)/shard_map/ppermute | solution.py:358
  19.1 3.0 %collective-permute-done.2.refs_4_ = bf16[96,768]{1,0:T(8,128)(2,1)S(1)} collective-permute-done((bf16[96,768]{1,0:T(8,128)(2,1)S(1)}, bf16[96,768]{1,0:T(8,128)(2,1)S(1)}, u32[]{:S(2)}, u32[]{:S(2)}) %collective-permute-start.2) | collective-permute-done | bytes 147488 | tf_op jit(solution)/shard_map/ppermute | solution.py:358
  25.2 4.5 %collective-permute-done.4.refs_6_ = bf16[96,768]{1,0:T(8,128)(2,1)S(1)} collective-permute-done((bf16[96,768]{1,0:T(8,128)(2,1)S(1)}, bf16[96,768]{1,0:T(8,128)(2,1)S(1)}, u32[]{:S(2)}, u32[]{:S(2)}) %collective-permute-start.4) | collective-permute-done | bytes 147488 | tf_op jit(solution)/shard_map/ppermute | solution.py:358
  30.2 1.5 %collective-permute-start.32 = (bf16[192,768]{1,0:T(8,128)(2,1)S(1)}, bf16[192,768]{1,0:T(8,128)(2,1)S(1)}, u32[]{:S(2)}, u32[]{:S(2)}) collective-permute-start(bf16[192,768]{1,0:T(8,128)(2,1)S(1)} %get-tuple-element.28.refs_2_), channel_id=1, source_target_pairs={{0,4},{1,5},{2,6},{3,7},{4,0},{5,1},{6,2},{7,3},{8,12},{9,13},{10,... | collective-permute-start | bytes 884744 | tf_op jit(solution)/shard_map/ppermute | solution.py:358
  31.8 2.0 %collective-permute-start.33 = (bf16[192,768]{1,0:T(8,128)(2,1)S(1)}, bf16[192,768]{1,0:T(8,128)(2,1)S(1)}, u32[]{:S(2)}, u32[]{:S(2)}) collective-permute-start(bf16[192,768]{1,0:T(8,128)(2,1)S(1)} %get-tuple-element.28.refs_2_), channel_id=1, source_target_pairs={{0,6},{1,7},{2,4},{3,5},{4,2},{5,3},{6,0},{7,1},{8,14},{9,15},{10,... | collective-permute-start | bytes 884744 | tf_op jit(solution)/shard_map/ppermute | solution.py:358
  35.2 9.4 %shard_map.96 = (bf16[192,192]{1,0:T(8,128)(2,1)S(1)}, bf16[192,192]{1,0:T(8,128)(2,1)S(1)}, bf16[192,192]{1,0:T(8,128)(2,1)S(1)}, bf16[192,192]{1,0:T(8,128)(2,...) custom-call(s32[1]{0:T(128)S(6)} %copy.10.count, ...), custom_call_target="tpu_custom_call" | custom-call | tf_op jit(solution)/shard_map/pallas_call | solution.py:405
  44.6 2.5 %collective-permute-done.33.refs_5_ = bf16[192,768]{1,0:T(8,128)(2,1)S(1)} collective-permute-done((bf16[192,768]{1,0:T(8,128)(2,1)S(1)}, bf16[192,768]{1,0:T(8,128)(2,1)S(1)}, u32[]{:S(2)}, u32[]{:S(2)}) %collective-permute-start.33) | collective-permute-done | bytes 294944 | tf_op jit(solution)/shard_map/ppermute | solution.py:358
  47.1 3.8 %shard_map.98 = (bf16[4,96,192]{2,1,0:T(8,128)(2,1)S(1)}, bf16[4,96,192]{2,1,0:T(8,128)(2,1)S(1)}) custom-call(bf16[4,3,192,1536]{3,2,1,0:T(8,128)(2,1)S(1)} %get-tuple-element.26.refs_0_, bf16[1536,768]{1,0:T(8,128)(2,1)S(1)} %get-tuple-element.27.refs_1_, bf16[192,768]{1,0:T(8,128)(2,1)S(1)} %get-tuple-element.28.refs_2_, ...), custom_call_target="tpu_custom_call" | custom-call | tf_op jit(solution)/shard_map/pallas_call | solution.py:412
  53.0 1.5 %collective-permute-start.35 = (bf16[96,192]{1,0:T(8,128)(2,1)S(1)}, bf16[96,192]{1,0:T(8,128)(2,1)S(1)}, u32[]{:S(2)}, u32[]{:S(2)}) collective-permute-start(bf16[96,192]{1,0:T(8,128)(2,1)S(1)} %get-tuple-element.34), channel_id=1, source_target_pairs={{0,8},{8,0},{16,24},{24,16},{1,9},{9,1},{17,25},{25,17},{2,10},{10... | collective-permute-start | bytes 110600 | tf_op jit(solution)/shard_map/ppermute | solution.py:435
  54.4 2.6 %collective-permute-start.36 = (bf16[96,192]{1,0:T(8,128)(2,1)S(1)}, bf16[96,192]{1,0:T(8,128)(2,1)S(1)}, u32[]{:S(2)}, u32[]{:S(2)}) collective-permute-start(bf16[96,192]{1,0:T(8,128)(2,1)S(1)} %get-tuple-element.36), channel_id=1, source_target_pairs={{0,16},{8,24},{16,0},{24,8},{1,17},{9,25},{17,1},{25,9},{2,18},{10... | collective-permute-start | bytes 110600 | tf_op jit(solution)/shard_map/ppermute | solution.py:435
  57.0 3.4 %collective-permute-done.25.refs_6_ = bf16[96,768]{1,0:T(8,128)(2,1)S(1)} collective-permute-done((bf16[96,768]{1,0:T(8,128)(2,1)S(1)}, bf16[96,768]{1,0:T(8,128)(2,1)S(1)}, u32[]{:S(2)}, u32[]{:S(2)}) %collective-permute-start.25) | collective-permute-done | bytes 147488 | tf_op jit(solution)/shard_map/ppermute | solution.py:358
  60.4 3.4 %collective-permute-start.37 = (bf16[96,192]{1,0:T(8,128)(2,1)S(1)}, bf16[96,192]{1,0:T(8,128)(2,1)S(1)}, u32[]{:S(2)}, u32[]{:S(2)}) collective-permute-start(bf16[96,192]{1,0:T(8,128)(2,1)S(1)} %get-tuple-element.35), channel_id=1, source_target_pairs={{0,24},{8,16},{16,8},{24,0},{1,25},{9,17},{17,9},{25,1},{2,26},{10... | collective-permute-start | bytes 110600 | tf_op jit(solution)/shard_map/ppermute | solution.py:435
  64.7 1.5 %collective-permute-start.22 = (bf16[192,192]{1,0:T(8,128)(2,1)S(1)}, bf16[192,192]{1,0:T(8,128)(2,1)S(1)}, u32[]{:S(2)}, u32[]{:S(2)}) collective-permute-start(bf16[192,192]{1,0:T(8,128)(2,1)S(1)} %get-tuple-element.23), channel_id=1, source_target_pairs={{0,4},{1,5},{2,6},{3,7},{4,0},{5,1},{6,2},{7,3},{8,12},{9,13},{10,... | collective-permute-start | bytes 221192 | tf_op jit(solution)/shard_map/ppermute | solution.py:358
  66.3 1.5 %collective-permute-start.23 = (bf16[192,192]{1,0:T(8,128)(2,1)S(1)}, bf16[192,192]{1,0:T(8,128)(2,1)S(1)}, u32[]{:S(2)}, u32[]{:S(2)}) collective-permute-start(bf16[192,192]{1,0:T(8,128)(2,1)S(1)} %get-tuple-element.24), channel_id=1, source_target_pairs={{0,6},{1,7},{2,4},{3,5},{4,2},{5,3},{6,0},{7,1},{8,14},{9,15},{10,... | collective-permute-start | bytes 221192 | tf_op jit(solution)/shard_map/ppermute | solution.py:358
  68.6 1.7 %collective-permute-start.39 = (bf16[96,192]{1,0:T(8,128)(2,1)S(1)}, bf16[96,192]{1,0:T(8,128)(2,1)S(1)}, u32[]{:S(2)}, u32[]{:S(2)}) collective-permute-start(bf16[96,192]{1,0:T(8,128)(2,1)S(1)} %fusion.2), channel_id=1, source_target_pairs={{0,8},{1,9},{2,10},{3,11},{4,12},{5,13},{6,14},{7,15},{8,2},{9,3},... | collective-permute-start | bytes 110600 | tf_op jit(solution)/shard_map/ppermute | solution.py:443
  70.3 5.2 %collective-permute-start.40 = (bf16[96,192]{1,0:T(8,128)(2,1)S(1)}, bf16[96,192]{1,0:T(8,128)(2,1)S(1)}, u32[]{:S(2)}, u32[]{:S(2)}) collective-permute-start(bf16[96,192]{1,0:T(8,128)(2,1)S(1)} %fusion.2), channel_id=1, source_target_pairs={{0,16},{1,17},{2,18},{3,19},{4,20},{5,21},{6,22},{7,23},{8,26},{9,... | collective-permute-start | bytes 110600 | tf_op jit(solution)/shard_map/ppermute | solution.py:443
  76.8 1.4 %collective-permute-done.40.refs_2_ = bf16[96,192]{1,0:T(8,128)(2,1)S(1)} collective-permute-done((bf16[96,192]{1,0:T(8,128)(2,1)S(1)}, bf16[96,192]{1,0:T(8,128)(2,1)S(1)}, u32[]{:S(2)}, u32[]{:S(2)}) %collective-permute-start.40) | collective-permute-done | bytes 36896 | tf_op jit(solution)/shard_map/ppermute | solution.py:443
  78.2 5.0 %collective-permute-done.41.refs_3_ = bf16[96,192]{1,0:T(8,128)(2,1)S(1)} collective-permute-done((bf16[96,192]{1,0:T(8,128)(2,1)S(1)}, bf16[96,192]{1,0:T(8,128)(2,1)S(1)}, u32[]{:S(2)}, u32[]{:S(2)}) %collective-permute-start.41) | collective-permute-done | bytes 36896 | tf_op jit(solution)/shard_map/ppermute | solution.py:443
  (71 shorter events, 13.3 us)
Async XLA Ops:
  3.6 8.1 %collective-permute-start.14 = (bf16[3,104,192]{2,1,0:T(8,128)(2,1)}, bf16[3,104,192]{2,1,0:T(8,128)(2,1)S(1)}, u32[]{:S(2)}, u32[]{:S(2)}) collective-permute-start(bf16[3,104,192]{2,1,0:T(8,128)(2,1)} %get-tuple-element.18), channel_id=1, source_target_pairs={{0,2},{1,3},{2,0},{3,1},{4,6},{5,7},{6,4},{7,5},{8,10},{9,11},{10,... | collective-permute-start | bytes 359432 | tf_op jit(solution)/shard_map/ppermute | solution.py:358
  6.5 9.4 %collective-permute-start.15 = (bf16[3,104,192]{2,1,0:T(8,128)(2,1)}, bf16[3,104,192]{2,1,0:T(8,128)(2,1)S(1)}, u32[]{:S(2)}, u32[]{:S(2)}) collective-permute-start(bf16[3,104,192]{2,1,0:T(8,128)(2,1)} %get-tuple-element.19), channel_id=1, source_target_pairs={{0,4},{1,5},{2,6},{3,7},{4,0},{5,1},{6,2},{7,3},{8,12},{9,13},{10,... | collective-permute-start | bytes 359432 | tf_op jit(solution)/shard_map/ppermute | solution.py:358
  8.0 10.3 %collective-permute-start.16 = (bf16[3,104,192]{2,1,0:T(8,128)(2,1)}, bf16[3,104,192]{2,1,0:T(8,128)(2,1)S(1)}, u32[]{:S(2)}, u32[]{:S(2)}) collective-permute-start(bf16[3,104,192]{2,1,0:T(8,128)(2,1)} %get-tuple-element.20), channel_id=1, source_target_pairs={{0,6},{1,7},{2,4},{3,5},{4,2},{5,3},{6,0},{7,1},{8,14},{9,15},{10,... | collective-permute-start | bytes 359432 | tf_op jit(solution)/shard_map/ppermute | solution.py:358
  9.1 9.3 %collective-permute-start = (bf16[96,768]{1,0:T(8,128)(2,1)S(1)}, bf16[96,768]{1,0:T(8,128)(2,1)S(1)}, u32[]{:S(2)}, u32[]{:S(2)}) collective-permute-start(bf16[96,768]{1,0:T(8,128)(2,1)S(1)} %get-tuple-element.33.refs_0_), channel_id=1, source_target_pairs={{0,2},{1,3},{2,0},{3,1},{4,6},{5,7},{6,4},{7,5},{8,10},{9,11},{10,... | collective-permute-start | bytes 442376 | tf_op jit(solution)/shard_map/ppermute | solution.py:358
  11.1 7.2 %collective-permute-start.17 = (bf16[3,104,192]{2,1,0:T(8,128)(2,1)S(1)}, bf16[3,104,192]{2,1,0:T(8,128)(2,1)S(1)}, u32[]{:S(2)}, u32[]{:S(2)}) collective-permute-start(bf16[3,104,192]{2,1,0:T(8,128)(2,1)S(1)} %get-tuple-element.17.refs_16_), channel_id=1, source_target_pairs={{0,1},{1,0},{2,3},{3,2},{4,5},{5,4},{6,7},{7,6},{8,9},{9,8},{10,11... | collective-permute-start | bytes 359432 | tf_op jit(solution)/shard_map/ppermute | solution.py:358
  11.6 7.4 %collective-permute-start.3 = (bf16[96,768]{1,0:T(8,128)(2,1)S(1)}, bf16[96,768]{1,0:T(8,128)(2,1)S(1)}, u32[]{:S(2)}, u32[]{:S(2)}) collective-permute-start(bf16[96,768]{1,0:T(8,128)(2,1)S(1)} %get-tuple-element.32.refs_1_), channel_id=1, source_target_pairs={{0,4},{1,5},{2,6},{3,7},{4,0},{5,1},{6,2},{7,3},{8,12},{9,13},{10,... | collective-permute-start | bytes 442376 | tf_op jit(solution)/shard_map/ppermute | solution.py:358
  23.4 6.3 %collective-permute-start.4 = (bf16[96,768]{1,0:T(8,128)(2,1)S(1)}, bf16[96,768]{1,0:T(8,128)(2,1)S(1)}, u32[]{:S(2)}, u32[]{:S(2)}) collective-permute-start(bf16[96,768]{1,0:T(8,128)(2,1)S(1)} %collective-permute-done.refs_2_), channel_id=1, source_target_pairs={{0,4},{1,5},{2,6},{3,7},{4,0},{5,1},{6,2},{7,3},{8,12},{9,13},{10,... | collective-permute-start | bytes 442376 | tf_op jit(solution)/shard_map/ppermute | solution.py:358
  25.2 6.6 %collective-permute-start.10 = (bf16[96,768]{1,0:T(8,128)(2,1)S(1)}, bf16[96,768]{1,0:T(8,128)(2,1)S(1)}, u32[]{:S(2)}, u32[]{:S(2)}) collective-permute-start(bf16[96,768]{1,0:T(8,128)(2,1)S(1)} %collective-permute-done.2.refs_4_), channel_id=1, source_target_pairs={{0,1},{1,0},{2,3},{3,2},{4,5},{5,4},{6,7},{7,6},{8,9},{9,8},{10,11... | collective-permute-start | bytes 442376 | tf_op jit(solution)/shard_map/ppermute | solution.py:358
  30.2 14.3 %collective-permute-start.31 = (bf16[192,768]{1,0:T(8,128)(2,1)S(1)}, bf16[192,768]{1,0:T(8,128)(2,1)S(1)}, u32[]{:S(2)}, u32[]{:S(2)}) collective-permute-start(bf16[192,768]{1,0:T(8,128)(2,1)S(1)} %get-tuple-element.28.refs_2_), channel_id=1, source_target_pairs={{0,2},{1,3},{2,0},{3,1},{4,6},{5,7},{6,4},{7,5},{8,10},{9,11},{10,... | collective-permute-start | bytes 884744 | tf_op jit(solution)/shard_map/ppermute | solution.py:358
  30.2 14.3 %collective-permute-start.32 = (bf16[192,768]{1,0:T(8,128)(2,1)S(1)}, bf16[192,768]{1,0:T(8,128)(2,1)S(1)}, u32[]{:S(2)}, u32[]{:S(2)}) collective-permute-start(bf16[192,768]{1,0:T(8,128)(2,1)S(1)} %get-tuple-element.28.refs_2_), channel_id=1, source_target_pairs={{0,4},{1,5},{2,6},{3,7},{4,0},{5,1},{6,2},{7,3},{8,12},{9,13},{10,... | collective-permute-start | bytes 884744 | tf_op jit(solution)/shard_map/ppermute | solution.py:358
  31.8 15.3 %collective-permute-start.33 = (bf16[192,768]{1,0:T(8,128)(2,1)S(1)}, bf16[192,768]{1,0:T(8,128)(2,1)S(1)}, u32[]{:S(2)}, u32[]{:S(2)}) collective-permute-start(bf16[192,768]{1,0:T(8,128)(2,1)S(1)} %get-tuple-element.28.refs_2_), channel_id=1, source_target_pairs={{0,6},{1,7},{2,4},{3,5},{4,2},{5,3},{6,0},{7,1},{8,14},{9,15},{10,... | collective-permute-start | bytes 884744 | tf_op jit(solution)/shard_map/ppermute | solution.py:358
  33.8 10.8 %collective-permute-start.27 = (bf16[96,768]{1,0:T(8,128)(2,1)S(1)}, bf16[96,768]{1,0:T(8,128)(2,1)S(1)}, u32[]{:S(2)}, u32[]{:S(2)}) collective-permute-start(bf16[96,768]{1,0:T(8,128)(2,1)S(1)} %get-tuple-element.25.refs_4_.refs_6_), channel_id=1, source_target_pairs={{0,1},{1,0},{2,3},{3,2},{4,5},{5,4},{6,7},{7,6},{8,9},{9,8},{10,11... | collective-permute-start | bytes 442376 | tf_op jit(solution)/shard_map/ppermute | solution.py:358
  35.1 17.8 %collective-permute-start.24 = (bf16[96,768]{1,0:T(8,128)(2,1)}, bf16[96,768]{1,0:T(8,128)(2,1)S(1)}, u32[]{:S(2)}, u32[]{:S(2)}) collective-permute-start(bf16[96,768]{1,0:T(8,128)(2,1)} %wout.1), channel_id=1, source_target_pairs={{0,2},{1,3},{2,0},{3,1},{4,6},{5,7},{6,4},{7,5},{8,10},{9,11},{10,... | collective-permute-start | bytes 442376 | tf_op jit(solution)/shard_map/ppermute | solution.py:358
  51.0 9.4 %collective-permute-start.25 = (bf16[96,768]{1,0:T(8,128)(2,1)S(1)}, bf16[96,768]{1,0:T(8,128)(2,1)S(1)}, u32[]{:S(2)}, u32[]{:S(2)}) collective-permute-start(bf16[96,768]{1,0:T(8,128)(2,1)S(1)} %copy-done), channel_id=1, source_target_pairs={{0,4},{1,5},{2,6},{3,7},{4,0},{5,1},{6,2},{7,3},{8,12},{9,13},{10,... | collective-permute-start | bytes 442376 | tf_op jit(solution)/shard_map/ppermute | solution.py:358
  51.9 11.9 %collective-permute-start.26 = (bf16[96,768]{1,0:T(8,128)(2,1)S(1)}, bf16[96,768]{1,0:T(8,128)(2,1)S(1)}, u32[]{:S(2)}, u32[]{:S(2)}) collective-permute-start(bf16[96,768]{1,0:T(8,128)(2,1)S(1)} %copy-done), channel_id=1, source_target_pairs={{0,6},{1,7},{2,4},{3,5},{4,2},{5,3},{6,0},{7,1},{8,14},{9,15},{10,... | collective-permute-start | bytes 442376 | tf_op jit(solution)/shard_map/ppermute | solution.py:358
  52.9 11.0 %collective-permute-start.28 = (bf16[96,768]{1,0:T(8,128)(2,1)S(1)}, bf16[96,768]{1,0:T(8,128)(2,1)S(1)}, u32[]{:S(2)}, u32[]{:S(2)}) collective-permute-start(bf16[96,768]{1,0:T(8,128)(2,1)S(1)} %collective-permute-done.24.refs_5_), channel_id=1, source_target_pairs={{0,1},{1,0},{2,3},{3,2},{4,5},{5,4},{6,7},{7,6},{8,9},{9,8},{10,11... | collective-permute-start | bytes 442376 | tf_op jit(solution)/shard_map/ppermute | solution.py:358
  53.0 11.4 %collective-permute-start.35 = (bf16[96,192]{1,0:T(8,128)(2,1)S(1)}, bf16[96,192]{1,0:T(8,128)(2,1)S(1)}, u32[]{:S(2)}, u32[]{:S(2)}) collective-permute-start(bf16[96,192]{1,0:T(8,128)(2,1)S(1)} %get-tuple-element.34), channel_id=1, source_target_pairs={{0,8},{8,0},{16,24},{24,16},{1,9},{9,1},{17,25},{25,17},{2,10},{10... | collective-permute-start | bytes 110600 | tf_op jit(solution)/shard_map/ppermute | solution.py:435
  54.4 10.3 %collective-permute-start.36 = (bf16[96,192]{1,0:T(8,128)(2,1)S(1)}, bf16[96,192]{1,0:T(8,128)(2,1)S(1)}, u32[]{:S(2)}, u32[]{:S(2)}) collective-permute-start(bf16[96,192]{1,0:T(8,128)(2,1)S(1)} %get-tuple-element.36), channel_id=1, source_target_pairs={{0,16},{8,24},{16,0},{24,8},{1,17},{9,25},{17,1},{25,9},{2,18},{10... | collective-permute-start | bytes 110600 | tf_op jit(solution)/shard_map/ppermute | solution.py:435
  64.7 10.8 %collective-permute-start.22 = (bf16[192,192]{1,0:T(8,128)(2,1)S(1)}, bf16[192,192]{1,0:T(8,128)(2,1)S(1)}, u32[]{:S(2)}, u32[]{:S(2)}) collective-permute-start(bf16[192,192]{1,0:T(8,128)(2,1)S(1)} %get-tuple-element.23), channel_id=1, source_target_pairs={{0,4},{1,5},{2,6},{3,7},{4,0},{5,1},{6,2},{7,3},{8,12},{9,13},{10,... | collective-permute-start | bytes 221192 | tf_op jit(solution)/shard_map/ppermute | solution.py:358
  66.3 9.2 %collective-permute-start.23 = (bf16[192,192]{1,0:T(8,128)(2,1)S(1)}, bf16[192,192]{1,0:T(8,128)(2,1)S(1)}, u32[]{:S(2)}, u32[]{:S(2)}) collective-permute-start(bf16[192,192]{1,0:T(8,128)(2,1)S(1)} %get-tuple-element.24), channel_id=1, source_target_pairs={{0,6},{1,7},{2,4},{3,5},{4,2},{5,3},{6,0},{7,1},{8,14},{9,15},{10,... | collective-permute-start | bytes 221192 | tf_op jit(solution)/shard_map/ppermute | solution.py:358
  67.9 8.9 %collective-permute-start.38 = (bf16[96,192]{1,0:T(8,128)(2,1)S(1)}, bf16[96,192]{1,0:T(8,128)(2,1)S(1)}, u32[]{:S(2)}, u32[]{:S(2)}) collective-permute-start(bf16[96,192]{1,0:T(8,128)(2,1)S(1)} %fusion.2), channel_id=1, source_target_pairs={{0,0},{1,1},{2,2},{3,3},{4,4},{5,5},{6,6},{7,7},{8,10},{9,11},{10,... | collective-permute-start | bytes 110600 | tf_op jit(solution)/shard_map/ppermute | solution.py:443
  68.6 8.2 %collective-permute-start.39 = (bf16[96,192]{1,0:T(8,128)(2,1)S(1)}, bf16[96,192]{1,0:T(8,128)(2,1)S(1)}, u32[]{:S(2)}, u32[]{:S(2)}) collective-permute-start(bf16[96,192]{1,0:T(8,128)(2,1)S(1)} %fusion.2), channel_id=1, source_target_pairs={{0,8},{1,9},{2,10},{3,11},{4,12},{5,13},{6,14},{7,15},{8,2},{9,3},... | collective-permute-start | bytes 110600 | tf_op jit(solution)/shard_map/ppermute | solution.py:443
  70.3 7.9 %collective-permute-start.40 = (bf16[96,192]{1,0:T(8,128)(2,1)S(1)}, bf16[96,192]{1,0:T(8,128)(2,1)S(1)}, u32[]{:S(2)}, u32[]{:S(2)}) collective-permute-start(bf16[96,192]{1,0:T(8,128)(2,1)S(1)} %fusion.2), channel_id=1, source_target_pairs={{0,16},{1,17},{2,18},{3,19},{4,20},{5,21},{6,22},{7,23},{8,26},{9,... | collective-permute-start | bytes 110600 | tf_op jit(solution)/shard_map/ppermute | solution.py:443
  75.5 7.7 %collective-permute-start.41 = (bf16[96,192]{1,0:T(8,128)(2,1)S(1)}, bf16[96,192]{1,0:T(8,128)(2,1)S(1)}, u32[]{:S(2)}, u32[]{:S(2)}) collective-permute-start(bf16[96,192]{1,0:T(8,128)(2,1)S(1)} %fusion.2), channel_id=1, source_target_pairs={{0,24},{1,25},{2,26},{3,27},{4,28},{5,29},{6,30},{7,31},{8,18},{9,... | collective-permute-start | bytes 110600 | tf_op jit(solution)/shard_map/ppermute | solution.py:443
  (19 other events, 98.0 us)

commit v7 on v6

--- a/solution.py
+++ b/solution.py
@@ -82,10 +82,10 @@
     out[0] = total.astype(jnp.bfloat16)
 
 
-def attention_kernel(hg, tg, parts, rows, wr, head_dim, resident, count, *refs):
+def attention_kernel(hg, tg, counts, rows, wr, head_dim, resident, count, *refs):
     n = hg * tg
     refs = list(refs)
-    tiles = [[refs.pop(0) for _ in range(parts)] for _ in range(n)]
+    tiles = [[refs.pop(0) for _ in range(counts[r])] for r in range(n)]
     packed = [refs.pop(0) for _ in range(n)]
     o_out = [refs.pop(0) for _ in range(hg)]
     scaled_out, p_out = refs.pop(0), refs.pop(0)
@@ -102,20 +102,19 @@
     member = own % tg
     keys = n * rows
     heads = cw // head_dim
-    size = rows // parts
     if not resident:
         packed_copies = [
-            pltpu.make_async_copy(packed[r], wp_s.at[r], sems.at[n * parts + r]) for r in range(n)
+            pltpu.make_async_copy(packed[r], wp_s.at[r], sems.at[n + r]) for r in range(n)
         ]
         tile_copies = [
-            pltpu.make_async_copy(
-                tiles[r][i], t_s.at[pl.ds(r * rows + i * size, size), :], sems.at[r * parts + i]
-            )
+            pltpu.make_async_copy(tiles[r][0], t_s.at[pl.ds(r * rows, rows), :], sems.at[r])
             for r in range(n)
-            for i in range(parts)
         ]
         for copy in packed_copies + tile_copies:
             copy.start()
+    else:
+        own_tile = pltpu.make_async_copy(tiles[0][0], t_s.at[pl.ds(0, rows), :], sems.at[0])
+        own_tile.start()
     for tau in range(tg):
         for k in range(hg):
             r = tau * hg + k
@@ -133,11 +132,20 @@
             seg_s[0:1, columns] = line
             seg_s[1:2, columns] = jnp.where(at < count[0], line, -1.0)
     for r in range(n):
-        for i in range(parts):
-            if resident:
-                t_s[r * rows + i * size : r * rows + (i + 1) * size, :] = tiles[r][i][...]
-            else:
-                tile_copies[r * parts + i].wait()
+        if not resident:
+            tile_copies[r].wait()
+        elif r == 0:
+            own_tile.wait()
+        elif len(tiles[r]) == 1:
+            t_s[r * rows : (r + 1) * rows, :] = tiles[r][0][...]
+        else:
+            parity = (member ^ (r // hg)) % 2
+            for i in range(2):
+
+                @pl.when(parity == i)
+                def _():
+                    t_s[r * rows : (r + 1) * rows, :] = tiles[r][i][...]
+
     for tau in range(tg):
         at = slice(tau * hg * rows, (tau + 1) * hg * rows)
         block = t_s[at, :]
@@ -157,7 +165,7 @@
 
     def p_copy(k):
         slot = k % slots
-        return pltpu.make_async_copy(p_s.at[slot], p_out.at[k], sems.at[n * parts + n + slot])
+        return pltpu.make_async_copy(p_s.at[slot], p_out.at[k], sems.at[2 * n + slot])
 
     def chunk(k, carry):
         start = k * rows if isinstance(k, int) else pl.multiple_of(k * rows, rows)
@@ -213,7 +221,7 @@
     return keys <= 2048
 
 
-def attention_call(hg, tg, parts, rows, width, wr, cw, head_dim):
+def attention_call(hg, tg, counts, rows, width, wr, cw, head_dim):
     n = hg * tg
     keys = n * rows
     heads = cw // head_dim
@@ -232,9 +240,9 @@
             pltpu.VMEM((n, 3, wr + 8, cw), bf16),
         ]
     return pl.pallas_call(
-        functools.partial(attention_kernel, hg, tg, parts, rows, wr, head_dim, resident),
+        functools.partial(attention_kernel, hg, tg, counts, rows, wr, head_dim, resident),
         out_shape=[own((rows, cw), bf16)] * hg + [own((hg * rows, cw), jnp.float32)] + kept,
-        in_specs=[SM] + [VM if resident else ANY] * (n * parts + n),
+        in_specs=[SM, ANY] + [VM if resident else ANY] * (sum(counts) + n - 1),
         out_specs=[VM] * (hg + 1) + [VM if resident else ANY] * len(kept),
         scratch_shapes=local
         + [
@@ -246,19 +254,19 @@
             pltpu.VMEM((keys, cw), bf16),
             pltpu.VMEM((rows, keys), jnp.float32),
             pltpu.VMEM((hg * rows, cw), bf16),
-            pltpu.SemaphoreType.DMA((n * parts + n + hg,)),
+            pltpu.SemaphoreType.DMA((2 * n + hg,)),
         ],
         compiler_params=pltpu.CompilerParams(vmem_limit_bytes=(30 if resident else 60) * 1024 * 1024),
     )
 
 
-def gradient_kernel(hg, tg, parts, rows, wr, head_dim, by_dp, resident, *refs):
+def gradient_kernel(hg, tg, rows, wr, head_dim, by_dp, resident, *refs):
     n = hg * tg
     refs = list(refs)
     if resident:
         p_s, t_s = refs.pop(0), refs.pop(0)
     else:
-        tiles = [[refs.pop(0) for _ in range(parts)] for _ in range(n)]
+        tiles = [refs.pop(0) for _ in range(n)]
         p_in = refs.pop(0)
     cots = [refs.pop(0) for _ in range(hg)]
     wout_pieces = [refs.pop(0) for _ in range(tg)]
@@ -272,22 +280,18 @@
     group = own // tg
     member = own % tg
     heads = cw // head_dim
-    size = rows // parts
     slots = p_s.shape[0]
     p_copies, tile_copies = [], []
     if not resident:
         p_copies = [
             pltpu.make_async_copy(
-                p_in.at[k], p_s.at[k % slots], sems.at[n * parts + k % slots]
+                p_in.at[k], p_s.at[k % slots], sems.at[n + k % slots]
             )
             for k in range(hg)
         ]
         tile_copies = [
-            pltpu.make_async_copy(
-                tiles[r][i], t_s.at[pl.ds(r * rows + i * size, size), :], sems.at[r * parts + i]
-            )
+            pltpu.make_async_copy(tiles[r], t_s.at[pl.ds(r * rows, rows), :], sems.at[r])
             for r in range(n)
-            for i in range(parts)
         ]
     for copy in p_copies[:slots] + tile_copies:
         copy.start()
@@ -315,7 +319,7 @@
             g_out[tau][m] = grad_s[pl.ds(to, wr), :].astype(jnp.bfloat16)
 
 
-def gradient_call(hg, tg, parts, rows, width, wr, cw, head_dim, by_dp):
+def gradient_call(hg, tg, rows, width, wr, cw, head_dim, by_dp):
     n = hg * tg
     keys = n * rows
     heads = cw // head_dim
@@ -326,9 +330,9 @@
     if not resident:
         local = [pltpu.VMEM((1, heads, rows, keys), bf16), pltpu.VMEM((keys, width), bf16)]
     return pl.pallas_call(
-        functools.partial(gradient_kernel, hg, tg, parts, rows, wr, head_dim, by_dp, resident),
+        functools.partial(gradient_kernel, hg, tg, rows, wr, head_dim, by_dp, resident),
         out_shape=[jax.ShapeDtypeStruct((hg, wr, cw), bf16)] * tg,
-        in_specs=([VM] * 2 if resident else [ANY] * (n * parts + 1))
+        in_specs=([VM] * 2 if resident else [ANY] * (n + 1))
         + [VM] * (hg + tg + 1),
         out_specs=[VM] * tg,
         scratch_shapes=local
@@ -336,7 +340,7 @@
             pltpu.VMEM((cw, width), wide),
             pltpu.VMEM((cw, keys), jnp.float32),
             pltpu.VMEM((width, cw), jnp.float32),
-            pltpu.SemaphoreType.DMA((n * parts + hg,)),
+            pltpu.SemaphoreType.DMA((n + hg,)),
         ],
         compiler_params=pltpu.CompilerParams(vmem_limit_bytes=(30 if resident else 60) * 1024 * 1024),
     )
@@ -354,8 +358,9 @@
     by_dp = dp == hg
     bf16 = jnp.bfloat16
 
-    def hop(x, step):
-        return lax.ppermute(x, "seq", [(s, s ^ step) for s in range(n)])
+    def hop(x, step, senders=(0, 1)):
+        pairs = [(s, s ^ step) for s in range(n) if s % tg % 2 in senders]
+        return lax.ppermute(x, "seq", pairs)
 
     def over_groups(pieces):
         return [pieces[0]] + [hop(pieces[k], k * tg) for k in range(1, hg)]
@@ -367,7 +372,7 @@
         return [table[tau][k] for tau in range(tg) for k in range(hg)]
 
     wide = bf16 if wr % 16 == 0 else jnp.float32
-    parts = 2 if hg == 4 and rows % 32 == 0 else 1
+    relayed = hg == 4 and tg % 2 == 0 and fits(n * rows)
     segment_line = segment_of.reshape(1, rows)
     own_shape = pltpu.VMEM if fits(n * rows) else jax.ShapeDtypeStruct
     *packed, own_cot, own_wout = pl.pallas_call(
@@ -379,20 +384,18 @@
         out_specs=[VM] * (hg + 2),
     )(tissue_count, w_query, w_key, w_value, segment_line, cotangent[0], w_out)
     weight_table = over_members(over_groups(packed))
-    if parts == 2:
-        half = rows // 2
-        upper, lower = tiles[0, :half], tiles[0, half:]
-        first = [hop(upper, tg), hop(lower, tg)]
-        second = [hop(upper, 2 * tg), hop(lower, 2 * tg)]
-        third = [hop(first[0], 2 * tg), hop(second[1], tg)]
-        tile_pieces = [[upper, lower], first, second, third]
+    if relayed:
+        first, second = hop(tiles[0], tg), hop(tiles[0], 2 * tg)
+        third = [hop(first, 2 * tg, (0,)), hop(second, tg, (1,))]
+        tile_pieces = [[tiles[0]], [first], [second], third]
     else:
         tile_pieces = [[x] for x in over_groups([tiles[0]] * hg)]
     tile_pieces = tile_pieces + [
-        [hop(x, tau) for x in piece]
+        [hop(x, tau, (0, 1) if len(piece) == 1 else (i,)) for i, x in enumerate(piece)]
         for tau in range(1, tg)
         for piece in tile_pieces
     ]
+    counts = [len(piece) for piece in tile_pieces]
     flat_tiles = [x for piece in tile_pieces for x in piece]
     cots = over_groups([own_cot] * hg)
     wout_table = over_members(over_groups([own_wout] + [w_out] * (hg - 1)))
@@ -402,14 +405,15 @@
             return arrays
         return [pltpu.with_memory_space_constraint(x, pltpu.VMEM) for x in arrays]
 
-    results = attention_call(hg, tg, parts, rows, width, wr, cw, head_dim)(
-        tissue_count, *near_core(flat_tiles), *near_core(flat(weight_table))
+    far_tile = pltpu.with_memory_space_constraint(flat_tiles[0], pltpu.HBM)
+    results = attention_call(hg, tg, counts, rows, width, wr, cw, head_dim)(
+        tissue_count, far_tile, *near_core(flat_tiles[1:]), *near_core(flat(weight_table))
     )
     attention, scaled, kept = results[:hg], results[hg], results[hg + 1 :]
     if not fits(n * rows):
         kept = [*flat_tiles, *kept]
     attention = over_groups(attention)
-    grads = gradient_call(hg, tg, parts, rows, width, wr, cw, head_dim, by_dp)(
+    grads = gradient_call(hg, tg, rows, width, wr, cw, head_dim, by_dp)(
         *near_core(kept),
         *near_core(cots),
         *near_core([line[0] for line in wout_table]),

time: 84.3 us -> 84.8 us (level)
  starting transfers between devices: 38.6 us -> 49.5 us
  waiting for transfers between devices: 25.2 us -> 15.4 us
  local copies, waits for them, and re-layouts: 1.02 us -> 0.02 us
    ppermute x35 -> x30, starting transfers between devices: 23.6 us -> 34.3 us  [hop(): return lax.ppermute(x, 'seq', pairs)]
    ppermute x35 -> x30, waiting for transfers between devices: 18.7 us -> 9.02 us  [hop(): return lax.ppermute(x, 'seq', pairs)]
    squeeze x1 -> x0, local copies, waits for them, and re-layouts: 1 us -> none  [local(): upper, lower = (tiles[0, :half], tiles[0, half:])]
  transfers between devices with their start and end apart: 42 -> 37, of which waited for: 13 -> 7; matrix products, arithmetic and copies ran while one was open for 1% -> 0% of each run, Pallas kernels for 17% -> 20%
where the time goes in v7:
time: 84.8 us; the launch traced here: 84.5 us
  starting transfers between devices  49.5 us (58%)
  Pallas kernels  18.1 us (21%)
  waiting for transfers between devices  15.4 us (18%)
  between operations  1.45 us (2%)
    ppermute x30, starting transfers between devices, hop(): return lax.ppermute(x, 'seq', pairs)  34.3 us
    pallas_call x1, Pallas kernels, local(): attention_call(hg, tg, counts, rows, width, wr, cw, head_dim)  10 us
    ppermute x30, waiting for transfers between devices, hop(): return lax.ppermute(x, 'seq', pairs)  9.02 us
    ppermute x3, starting transfers between devices, local(): got = lax.ppermute(summed[m], 'dp', [(z, z ^ m) for z in range(dp)])  7.84 us
    ppermute x4, starting transfers between devices, local(): pieces.append(lax.ppermute(mine, ('dp', 'seq'), pairs))  7.33 us
    ppermute x4, waiting for transfers between devices, local(): pieces.append(lax.ppermute(mine, ('dp', 'seq'), pairs))  6.38 us
    pallas_call x1, Pallas kernels, local(): gradient_call(hg, tg, rows, width, wr, cw, head_dim, by_dp)  3.57 us
    pallas_call x1, Pallas kernels, local(): pl.pallas_call(functools.partial(pack_kernel, hg, tg, wr, cw), out_shape=...  2.29 us
  transfers between devices with their start and end apart: 37, of which 7 were waited for; matrix products, arithmetic and copies ran while one was open for 0% of the time, Pallas kernels for 20%

profile of v7, /device:TPU:0, one launch (start us, length us, event | category | flops | bytes accessed | tf_op | source)
XLA Modules:
  0.0 84.5 jit_solution(16380878237907528067)
XLA Ops:
  0.6 3.0 %collective-permute-start = (bf16[192,768]{1,0:T(8,128)(2,1)}, bf16[192,768]{1,0:T(8,128)(2,1)S(1)}, u32[]{:S(2)}, u32[]{:S(2)}) collective-permute-start(bf16[192,768]{1,0:T(8,128)(2,1)} %bitcast.14), channel_id=1, source_target_pairs={{0,2},{1,3},{2,0},{3,1},{4,6},{5,7},{6,4},{7,5},{8,10},{9,11},{10,... | collective-permute-start | bytes 884744 | tf_op jit(solution)/shard_map/ppermute | solution.py:363
  4.3 2.3 %shard_map.95 = (bf16[3,104,192]{2,1,0:T(8,128)(2,1)S(1)}, bf16[3,104,192]{2,1,0:T(8,128)(2,1)}, bf16[3,104,192]{2,1,0:T(8,128)(2,1)}, bf16[3,104,192]{2,1,0:T(8...) custom-call(s32[1]{0:T(128)S(6)} %copy.10.count, bf16[96,768]{1,0:T(8,128)(2,1)} %wq.1, ...), custom_call_target="tpu_custom_call" | custom-call | tf_op jit(solution)/shard_map/pallas_call | solution.py:378
  6.6 2.0 %collective-permute-start.1 = (bf16[192,768]{1,0:T(8,128)(2,1)}, bf16[192,768]{1,0:T(8,128)(2,1)S(1)}, u32[]{:S(2)}, u32[]{:S(2)}) collective-permute-start(bf16[192,768]{1,0:T(8,128)(2,1)} %bitcast.15), channel_id=1, source_target_pairs={{0,4},{1,5},{2,6},{3,7},{4,0},{5,1},{6,2},{7,3},{8,12},{9,13},{10,... | collective-permute-start | bytes 884744 | tf_op jit(solution)/shard_map/ppermute | solution.py:363
  8.7 2.9 %collective-permute-start.11 = (bf16[3,104,192]{2,1,0:T(8,128)(2,1)}, bf16[3,104,192]{2,1,0:T(8,128)(2,1)S(1)}, u32[]{:S(2)}, u32[]{:S(2)}) collective-permute-start(bf16[3,104,192]{2,1,0:T(8,128)(2,1)} %get-tuple-element.20), channel_id=1, source_target_pairs={{0,6},{1,7},{2,4},{3,5},{4,2},{5,3},{6,0},{7,1},{8,14},{9,15},{10,... | collective-permute-start | bytes 359432 | tf_op jit(solution)/shard_map/ppermute | solution.py:363
  11.6 3.6 %collective-permute-done.9.refs_11_ = bf16[3,104,192]{2,1,0:T(8,128)(2,1)S(1)} collective-permute-done((bf16[3,104,192]{2,1,0:T(8,128)(2,1)}, bf16[3,104,192]{2,1,0:T(8,128)(2,1)S(1)}, u32[]{:S(2)}, u32[]{:S(2)}) %collective-permute-start.9) | collective-permute-done | bytes 119840 | tf_op jit(solution)/shard_map/ppermute | solution.py:363
  15.2 3.9 %collective-permute-start.2 = (bf16[192,768]{1,0:T(8,128)(2,1)S(1)}, bf16[192,768]{1,0:T(8,128)(2,1)S(1)}, u32[]{:S(2)}, u32[]{:S(2)}) collective-permute-start(bf16[192,768]{1,0:T(8,128)(2,1)S(1)} %collective-permute-done.refs_1_), channel_id=1, source_target_pairs={{0,4},{2,6},{4,0},{6,2},{8,12},{10,14},{12,8},{14,10},{16,20},{18,... | collective-permute-start | bytes 884744 | tf_op jit(solution)/shard_map/ppermute | solution.py:363
  19.1 3.0 %collective-permute-done.10.refs_12_ = bf16[3,104,192]{2,1,0:T(8,128)(2,1)S(1)} collective-permute-done((bf16[3,104,192]{2,1,0:T(8,128)(2,1)}, bf16[3,104,192]{2,1,0:T(8,128)(2,1)S(1)}, u32[]{:S(2)}, u32[]{:S(2)}) %collective-permute-start.10) | collective-permute-done | bytes 119840 | tf_op jit(solution)/shard_map/ppermute | solution.py:363
  23.5 3.1 %collective-permute-start.4 = (bf16[192,768]{1,0:T(8,128)(2,1)}, bf16[192,768]{1,0:T(8,128)(2,1)S(1)}, u32[]{:S(2)}, u32[]{:S(2)}) collective-permute-start(bf16[192,768]{1,0:T(8,128)(2,1)} %bitcast.16), channel_id=1, source_target_pairs={{0,1},{1,0},{2,3},{3,2},{4,5},{5,4},{6,7},{7,6},{8,9},{9,8},{10,11... | collective-permute-start | bytes 884744 | tf_op jit(solution)/shard_map/ppermute | solution.py:363
  27.1 2.0 %collective-permute-start.7 = (bf16[192,768]{1,0:T(8,128)(2,1)S(1)}, bf16[192,768]{1,0:T(8,128)(2,1)S(1)}, u32[]{:S(2)}, u32[]{:S(2)}) collective-permute-start(bf16[192,768]{1,0:T(8,128)(2,1)S(1)} %collective-permute-done.2.refs_3_), channel_id=1, source_target_pairs={{0,1},{2,3},{4,5},{6,7},{8,9},{10,11},{12,13},{14,15},{16,17},{18,... | collective-permute-start | bytes 884744 | tf_op jit(solution)/shard_map/ppermute | solution.py:363
  30.8 1.7 %collective-permute-start.27 = (bf16[192,768]{1,0:T(8,128)(2,1)S(1)}, bf16[192,768]{1,0:T(8,128)(2,1)S(1)}, u32[]{:S(2)}, u32[]{:S(2)}) collective-permute-start(bf16[192,768]{1,0:T(8,128)(2,1)S(1)} %get-tuple-element.28.refs_2_), channel_id=1, source_target_pairs={{0,4},{1,5},{2,6},{3,7},{4,0},{5,1},{6,2},{7,3},{8,12},{9,13},{10,... | collective-permute-start | bytes 884744 | tf_op jit(solution)/shard_map/ppermute | solution.py:363
  32.6 1.5 %collective-permute-start.28 = (bf16[192,768]{1,0:T(8,128)(2,1)S(1)}, bf16[192,768]{1,0:T(8,128)(2,1)S(1)}, u32[]{:S(2)}, u32[]{:S(2)}) collective-permute-start(bf16[192,768]{1,0:T(8,128)(2,1)S(1)} %get-tuple-element.28.refs_2_), channel_id=1, source_target_pairs={{0,6},{1,7},{2,4},{3,5},{4,2},{5,3},{6,0},{7,1},{8,14},{9,15},{10,... | collective-permute-start | bytes 884744 | tf_op jit(solution)/shard_map/ppermute | solution.py:363
  34.8 1.6 %collective-permute-start.19 = (bf16[96,768]{1,0:T(8,128)(2,1)}, bf16[96,768]{1,0:T(8,128)(2,1)S(1)}, u32[]{:S(2)}, u32[]{:S(2)}) collective-permute-start(bf16[96,768]{1,0:T(8,128)(2,1)} %wout.1), channel_id=1, source_target_pairs={{0,2},{1,3},{2,0},{3,1},{4,6},{5,7},{6,4},{7,5},{8,10},{9,11},{10,... | collective-permute-start | bytes 442376 | tf_op jit(solution)/shard_map/ppermute | solution.py:363
  36.4 10.0 %shard_map.96 = (bf16[192,192]{1,0:T(8,128)(2,1)S(1)}, bf16[192,192]{1,0:T(8,128)(2,1)S(1)}, bf16[192,192]{1,0:T(8,128)(2,1)S(1)}, bf16[192,192]{1,0:T(8,128)(2,...) custom-call(s32[1]{0:T(128)S(6)} %copy.10.count, ...), custom_call_target="tpu_custom_call" | custom-call | tf_op jit(solution)/shard_map/pallas_call | solution.py:409
  46.9 3.6 %shard_map.98 = (bf16[4,96,192]{2,1,0:T(8,128)(2,1)S(1)}, bf16[4,96,192]{2,1,0:T(8,128)(2,1)S(1)}) custom-call(bf16[4,3,192,1536]{3,2,1,0:T(8,128)(2,1)S(1)} %get-tuple-element.26.refs_0_, bf16[1536,768]{1,0:T(8,128)(2,1)S(1)} %get-tuple-element.27.refs_1_, bf16[192,768]{1,0:T(8,128)(2,1)S(1)} %get-tuple-element.28.refs_2_, ...), custom_call_target="tpu_custom_call" | custom-call | tf_op jit(solution)/shard_map/pallas_call | solution.py:416
  52.5 2.2 %collective-permute-start.21 = (bf16[96,768]{1,0:T(8,128)(2,1)S(1)}, bf16[96,768]{1,0:T(8,128)(2,1)S(1)}, u32[]{:S(2)}, u32[]{:S(2)}) collective-permute-start(bf16[96,768]{1,0:T(8,128)(2,1)S(1)} %copy-done), channel_id=1, source_target_pairs={{0,6},{1,7},{2,4},{3,5},{4,2},{5,3},{6,0},{7,1},{8,14},{9,15},{10,... | collective-permute-start | bytes 442376 | tf_op jit(solution)/shard_map/ppermute | solution.py:363
  54.8 1.6 %collective-permute-start.30 = (bf16[96,192]{1,0:T(8,128)(2,1)S(1)}, bf16[96,192]{1,0:T(8,128)(2,1)S(1)}, u32[]{:S(2)}, u32[]{:S(2)}) collective-permute-start(bf16[96,192]{1,0:T(8,128)(2,1)S(1)} %get-tuple-element.32), channel_id=1, source_target_pairs={{0,8},{8,0},{16,24},{24,16},{1,9},{9,1},{17,25},{25,17},{2,10},{10... | collective-permute-start | bytes 110600 | tf_op jit(solution)/shard_map/ppermute | solution.py:439
  56.5 2.6 %collective-permute-start.31 = (bf16[96,192]{1,0:T(8,128)(2,1)S(1)}, bf16[96,192]{1,0:T(8,128)(2,1)S(1)}, u32[]{:S(2)}, u32[]{:S(2)}) collective-permute-start(bf16[96,192]{1,0:T(8,128)(2,1)S(1)} %get-tuple-element.34), channel_id=1, source_target_pairs={{0,16},{8,24},{16,0},{24,8},{1,17},{9,25},{17,1},{25,9},{2,18},{10... | collective-permute-start | bytes 110600 | tf_op jit(solution)/shard_map/ppermute | solution.py:439
  59.1 1.8 %collective-permute-done.20.refs_6_ = bf16[96,768]{1,0:T(8,128)(2,1)S(1)} collective-permute-done((bf16[96,768]{1,0:T(8,128)(2,1)S(1)}, bf16[96,768]{1,0:T(8,128)(2,1)S(1)}, u32[]{:S(2)}, u32[]{:S(2)}) %collective-permute-start.20) | collective-permute-done | bytes 147488 | tf_op jit(solution)/shard_map/ppermute | solution.py:363
  60.9 3.6 %collective-permute-start.32 = (bf16[96,192]{1,0:T(8,128)(2,1)S(1)}, bf16[96,192]{1,0:T(8,128)(2,1)S(1)}, u32[]{:S(2)}, u32[]{:S(2)}) collective-permute-start(bf16[96,192]{1,0:T(8,128)(2,1)S(1)} %get-tuple-element.33), channel_id=1, source_target_pairs={{0,24},{8,16},{16,8},{24,0},{1,25},{9,17},{17,9},{25,1},{2,26},{10... | collective-permute-start | bytes 110600 | tf_op jit(solution)/shard_map/ppermute | solution.py:439
  66.9 1.6 %collective-permute-start.18 = (bf16[192,192]{1,0:T(8,128)(2,1)S(1)}, bf16[192,192]{1,0:T(8,128)(2,1)S(1)}, u32[]{:S(2)}, u32[]{:S(2)}) collective-permute-start(bf16[192,192]{1,0:T(8,128)(2,1)S(1)} %get-tuple-element.24), channel_id=1, source_target_pairs={{0,6},{1,7},{2,4},{3,5},{4,2},{5,3},{6,0},{7,1},{8,14},{9,15},{10,... | collective-permute-start | bytes 221192 | tf_op jit(solution)/shard_map/ppermute | solution.py:363
  69.2 2.3 %collective-permute-start.34 = (bf16[96,192]{1,0:T(8,128)(2,1)S(1)}, bf16[96,192]{1,0:T(8,128)(2,1)S(1)}, u32[]{:S(2)}, u32[]{:S(2)}) collective-permute-start(bf16[96,192]{1,0:T(8,128)(2,1)S(1)} %fusion.2), channel_id=1, source_target_pairs={{0,8},{1,9},{2,10},{3,11},{4,12},{5,13},{6,14},{7,15},{8,2},{9,3},... | collective-permute-start | bytes 110600 | tf_op jit(solution)/shard_map/ppermute | solution.py:447
  71.5 4.4 %collective-permute-start.35 = (bf16[96,192]{1,0:T(8,128)(2,1)S(1)}, bf16[96,192]{1,0:T(8,128)(2,1)S(1)}, u32[]{:S(2)}, u32[]{:S(2)}) collective-permute-start(bf16[96,192]{1,0:T(8,128)(2,1)S(1)} %fusion.2), channel_id=1, source_target_pairs={{0,16},{1,17},{2,18},{3,19},{4,20},{5,21},{6,22},{7,23},{8,26},{9,... | collective-permute-start | bytes 110600 | tf_op jit(solution)/shard_map/ppermute | solution.py:447
  77.2 1.6 %collective-permute-done.35.refs_2_ = bf16[96,192]{1,0:T(8,128)(2,1)S(1)} collective-permute-done((bf16[96,192]{1,0:T(8,128)(2,1)S(1)}, bf16[96,192]{1,0:T(8,128)(2,1)S(1)}, u32[]{:S(2)}, u32[]{:S(2)}) %collective-permute-start.35) | collective-permute-done | bytes 36896 | tf_op jit(solution)/shard_map/ppermute | solution.py:447
  78.9 4.7 %collective-permute-done.36.refs_3_ = bf16[96,192]{1,0:T(8,128)(2,1)S(1)} collective-permute-done((bf16[96,192]{1,0:T(8,128)(2,1)S(1)}, bf16[96,192]{1,0:T(8,128)(2,1)S(1)}, u32[]{:S(2)}, u32[]{:S(2)}) %collective-permute-start.36) | collective-permute-done | bytes 36896 | tf_op jit(solution)/shard_map/ppermute | solution.py:447
  (60 shorter events, 12.3 us)
Async XLA Ops:
  0.6 14.5 %collective-permute-start = (bf16[192,768]{1,0:T(8,128)(2,1)}, bf16[192,768]{1,0:T(8,128)(2,1)S(1)}, u32[]{:S(2)}, u32[]{:S(2)}) collective-permute-start(bf16[192,768]{1,0:T(8,128)(2,1)} %bitcast.14), channel_id=1, source_target_pairs={{0,2},{1,3},{2,0},{3,1},{4,6},{5,7},{6,4},{7,5},{8,10},{9,11},{10,... | collective-permute-start | bytes 884744 | tf_op jit(solution)/shard_map/ppermute | solution.py:363
  6.6 8.5 %collective-permute-start.9 = (bf16[3,104,192]{2,1,0:T(8,128)(2,1)}, bf16[3,104,192]{2,1,0:T(8,128)(2,1)S(1)}, u32[]{:S(2)}, u32[]{:S(2)}) collective-permute-start(bf16[3,104,192]{2,1,0:T(8,128)(2,1)} %get-tuple-element.18), channel_id=1, source_target_pairs={{0,2},{1,3},{2,0},{3,1},{4,6},{5,7},{6,4},{7,5},{8,10},{9,11},{10,... | collective-permute-start | bytes 359432 | tf_op jit(solution)/shard_map/ppermute | solution.py:363
  6.6 16.1 %collective-permute-start.1 = (bf16[192,768]{1,0:T(8,128)(2,1)}, bf16[192,768]{1,0:T(8,128)(2,1)S(1)}, u32[]{:S(2)}, u32[]{:S(2)}) collective-permute-start(bf16[192,768]{1,0:T(8,128)(2,1)} %bitcast.15), channel_id=1, source_target_pairs={{0,4},{1,5},{2,6},{3,7},{4,0},{5,1},{6,2},{7,3},{8,12},{9,13},{10,... | collective-permute-start | bytes 884744 | tf_op jit(solution)/shard_map/ppermute | solution.py:363
  8.6 13.5 %collective-permute-start.10 = (bf16[3,104,192]{2,1,0:T(8,128)(2,1)}, bf16[3,104,192]{2,1,0:T(8,128)(2,1)S(1)}, u32[]{:S(2)}, u32[]{:S(2)}) collective-permute-start(bf16[3,104,192]{2,1,0:T(8,128)(2,1)} %get-tuple-element.19), channel_id=1, source_target_pairs={{0,4},{1,5},{2,6},{3,7},{4,0},{5,1},{6,2},{7,3},{8,12},{9,13},{10,... | collective-permute-start | bytes 359432 | tf_op jit(solution)/shard_map/ppermute | solution.py:363
  8.7 13.5 %collective-permute-start.11 = (bf16[3,104,192]{2,1,0:T(8,128)(2,1)}, bf16[3,104,192]{2,1,0:T(8,128)(2,1)S(1)}, u32[]{:S(2)}, u32[]{:S(2)}) collective-permute-start(bf16[3,104,192]{2,1,0:T(8,128)(2,1)} %get-tuple-element.20), channel_id=1, source_target_pairs={{0,6},{1,7},{2,4},{3,5},{4,2},{5,3},{6,0},{7,1},{8,14},{9,15},{10,... | collective-permute-start | bytes 359432 | tf_op jit(solution)/shard_map/ppermute | solution.py:363
  15.2 7.5 %collective-permute-start.12 = (bf16[3,104,192]{2,1,0:T(8,128)(2,1)S(1)}, bf16[3,104,192]{2,1,0:T(8,128)(2,1)S(1)}, u32[]{:S(2)}, u32[]{:S(2)}) collective-permute-start(bf16[3,104,192]{2,1,0:T(8,128)(2,1)S(1)} %get-tuple-element.17.refs_10_), channel_id=1, source_target_pairs={{0,1},{1,0},{2,3},{3,2},{4,5},{5,4},{6,7},{7,6},{8,9},{9,8},{10,11... | collective-permute-start | bytes 359432 | tf_op jit(solution)/shard_map/ppermute | solution.py:363
  15.2 12.0 %collective-permute-start.2 = (bf16[192,768]{1,0:T(8,128)(2,1)S(1)}, bf16[192,768]{1,0:T(8,128)(2,1)S(1)}, u32[]{:S(2)}, u32[]{:S(2)}) collective-permute-start(bf16[192,768]{1,0:T(8,128)(2,1)S(1)} %collective-permute-done.refs_1_), channel_id=1, source_target_pairs={{0,4},{2,6},{4,0},{6,2},{8,12},{10,14},{12,8},{14,10},{16,20},{18,... | collective-permute-start | bytes 884744 | tf_op jit(solution)/shard_map/ppermute | solution.py:363
  23.5 6.9 %collective-permute-start.4 = (bf16[192,768]{1,0:T(8,128)(2,1)}, bf16[192,768]{1,0:T(8,128)(2,1)S(1)}, u32[]{:S(2)}, u32[]{:S(2)}) collective-permute-start(bf16[192,768]{1,0:T(8,128)(2,1)} %bitcast.16), channel_id=1, source_target_pairs={{0,1},{1,0},{2,3},{3,2},{4,5},{5,4},{6,7},{7,6},{8,9},{9,8},{10,11... | collective-permute-start | bytes 884744 | tf_op jit(solution)/shard_map/ppermute | solution.py:363
  30.5 16.0 %collective-permute-start.26 = (bf16[192,768]{1,0:T(8,128)(2,1)S(1)}, bf16[192,768]{1,0:T(8,128)(2,1)S(1)}, u32[]{:S(2)}, u32[]{:S(2)}) collective-permute-start(bf16[192,768]{1,0:T(8,128)(2,1)S(1)} %get-tuple-element.28.refs_2_), channel_id=1, source_target_pairs={{0,2},{1,3},{2,0},{3,1},{4,6},{5,7},{6,4},{7,5},{8,10},{9,11},{10,... | collective-permute-start | bytes 884744 | tf_op jit(solution)/shard_map/ppermute | solution.py:363
  30.8 15.6 %collective-permute-start.27 = (bf16[192,768]{1,0:T(8,128)(2,1)S(1)}, bf16[192,768]{1,0:T(8,128)(2,1)S(1)}, u32[]{:S(2)}, u32[]{:S(2)}) collective-permute-start(bf16[192,768]{1,0:T(8,128)(2,1)S(1)} %get-tuple-element.28.refs_2_), channel_id=1, source_target_pairs={{0,4},{1,5},{2,6},{3,7},{4,0},{5,1},{6,2},{7,3},{8,12},{9,13},{10,... | collective-permute-start | bytes 884744 | tf_op jit(solution)/shard_map/ppermute | solution.py:363
  32.6 14.3 %collective-permute-start.28 = (bf16[192,768]{1,0:T(8,128)(2,1)S(1)}, bf16[192,768]{1,0:T(8,128)(2,1)S(1)}, u32[]{:S(2)}, u32[]{:S(2)}) collective-permute-start(bf16[192,768]{1,0:T(8,128)(2,1)S(1)} %get-tuple-element.28.refs_2_), channel_id=1, source_target_pairs={{0,6},{1,7},{2,4},{3,5},{4,2},{5,3},{6,0},{7,1},{8,14},{9,15},{10,... | collective-permute-start | bytes 884744 | tf_op jit(solution)/shard_map/ppermute | solution.py:363
  34.0 12.4 %collective-permute-start.22 = (bf16[96,768]{1,0:T(8,128)(2,1)S(1)}, bf16[96,768]{1,0:T(8,128)(2,1)S(1)}, u32[]{:S(2)}, u32[]{:S(2)}) collective-permute-start(bf16[96,768]{1,0:T(8,128)(2,1)S(1)} %get-tuple-element.25.refs_4_.refs_6_), channel_id=1, source_target_pairs={{0,1},{1,0},{2,3},{3,2},{4,5},{5,4},{6,7},{7,6},{8,9},{9,8},{10,11... | collective-permute-start | bytes 442376 | tf_op jit(solution)/shard_map/ppermute | solution.py:363
  34.8 20.0 %collective-permute-start.19 = (bf16[96,768]{1,0:T(8,128)(2,1)}, bf16[96,768]{1,0:T(8,128)(2,1)S(1)}, u32[]{:S(2)}, u32[]{:S(2)}) collective-permute-start(bf16[96,768]{1,0:T(8,128)(2,1)} %wout.1), channel_id=1, source_target_pairs={{0,2},{1,3},{2,0},{3,1},{4,6},{5,7},{6,4},{7,5},{8,10},{9,11},{10,... | collective-permute-start | bytes 442376 | tf_op jit(solution)/shard_map/ppermute | solution.py:363
  51.9 9.0 %collective-permute-start.20 = (bf16[96,768]{1,0:T(8,128)(2,1)S(1)}, bf16[96,768]{1,0:T(8,128)(2,1)S(1)}, u32[]{:S(2)}, u32[]{:S(2)}) collective-permute-start(bf16[96,768]{1,0:T(8,128)(2,1)S(1)} %copy-done), channel_id=1, source_target_pairs={{0,4},{1,5},{2,6},{3,7},{4,0},{5,1},{6,2},{7,3},{8,12},{9,13},{10,... | collective-permute-start | bytes 442376 | tf_op jit(solution)/shard_map/ppermute | solution.py:363
  52.5 12.0 %collective-permute-start.21 = (bf16[96,768]{1,0:T(8,128)(2,1)S(1)}, bf16[96,768]{1,0:T(8,128)(2,1)S(1)}, u32[]{:S(2)}, u32[]{:S(2)}) collective-permute-start(bf16[96,768]{1,0:T(8,128)(2,1)S(1)} %copy-done), channel_id=1, source_target_pairs={{0,6},{1,7},{2,4},{3,5},{4,2},{5,3},{6,0},{7,1},{8,14},{9,15},{10,... | collective-permute-start | bytes 442376 | tf_op jit(solution)/shard_map/ppermute | solution.py:363
  54.8 9.7 %collective-permute-start.23 = (bf16[96,768]{1,0:T(8,128)(2,1)S(1)}, bf16[96,768]{1,0:T(8,128)(2,1)S(1)}, u32[]{:S(2)}, u32[]{:S(2)}) collective-permute-start(bf16[96,768]{1,0:T(8,128)(2,1)S(1)} %collective-permute-done.19.refs_5_), channel_id=1, source_target_pairs={{0,1},{1,0},{2,3},{3,2},{4,5},{5,4},{6,7},{7,6},{8,9},{9,8},{10,11... | collective-permute-start | bytes 442376 | tf_op jit(solution)/shard_map/ppermute | solution.py:363
  54.8 10.2 %collective-permute-start.30 = (bf16[96,192]{1,0:T(8,128)(2,1)S(1)}, bf16[96,192]{1,0:T(8,128)(2,1)S(1)}, u32[]{:S(2)}, u32[]{:S(2)}) collective-permute-start(bf16[96,192]{1,0:T(8,128)(2,1)S(1)} %get-tuple-element.32), channel_id=1, source_target_pairs={{0,8},{8,0},{16,24},{24,16},{1,9},{9,1},{17,25},{25,17},{2,10},{10... | collective-permute-start | bytes 110600 | tf_op jit(solution)/shard_map/ppermute | solution.py:439
  56.5 9.9 %collective-permute-start.31 = (bf16[96,192]{1,0:T(8,128)(2,1)S(1)}, bf16[96,192]{1,0:T(8,128)(2,1)S(1)}, u32[]{:S(2)}, u32[]{:S(2)}) collective-permute-start(bf16[96,192]{1,0:T(8,128)(2,1)S(1)} %get-tuple-element.34), channel_id=1, source_target_pairs={{0,16},{8,24},{16,0},{24,8},{1,17},{9,25},{17,1},{25,9},{2,18},{10... | collective-permute-start | bytes 110600 | tf_op jit(solution)/shard_map/ppermute | solution.py:439
  66.4 9.5 %collective-permute-start.17 = (bf16[192,192]{1,0:T(8,128)(2,1)S(1)}, bf16[192,192]{1,0:T(8,128)(2,1)S(1)}, u32[]{:S(2)}, u32[]{:S(2)}) collective-permute-start(bf16[192,192]{1,0:T(8,128)(2,1)S(1)} %get-tuple-element.23), channel_id=1, source_target_pairs={{0,4},{1,5},{2,6},{3,7},{4,0},{5,1},{6,2},{7,3},{8,12},{9,13},{10,... | collective-permute-start | bytes 221192 | tf_op jit(solution)/shard_map/ppermute | solution.py:363
  66.9 9.0 %collective-permute-start.18 = (bf16[192,192]{1,0:T(8,128)(2,1)S(1)}, bf16[192,192]{1,0:T(8,128)(2,1)S(1)}, u32[]{:S(2)}, u32[]{:S(2)}) collective-permute-start(bf16[192,192]{1,0:T(8,128)(2,1)S(1)} %get-tuple-element.24), channel_id=1, source_target_pairs={{0,6},{1,7},{2,4},{3,5},{4,2},{5,3},{6,0},{7,1},{8,14},{9,15},{10,... | collective-permute-start | bytes 221192 | tf_op jit(solution)/shard_map/ppermute | solution.py:363
  68.6 8.7 %collective-permute-start.33 = (bf16[96,192]{1,0:T(8,128)(2,1)S(1)}, bf16[96,192]{1,0:T(8,128)(2,1)S(1)}, u32[]{:S(2)}, u32[]{:S(2)}) collective-permute-start(bf16[96,192]{1,0:T(8,128)(2,1)S(1)} %fusion.2), channel_id=1, source_target_pairs={{0,0},{1,1},{2,2},{3,3},{4,4},{5,5},{6,6},{7,7},{8,10},{9,11},{10,... | collective-permute-start | bytes 110600 | tf_op jit(solution)/shard_map/ppermute | solution.py:447
  69.2 8.0 %collective-permute-start.34 = (bf16[96,192]{1,0:T(8,128)(2,1)S(1)}, bf16[96,192]{1,0:T(8,128)(2,1)S(1)}, u32[]{:S(2)}, u32[]{:S(2)}) collective-permute-start(bf16[96,192]{1,0:T(8,128)(2,1)S(1)} %fusion.2), channel_id=1, source_target_pairs={{0,8},{1,9},{2,10},{3,11},{4,12},{5,13},{6,14},{7,15},{8,2},{9,3},... | collective-permute-start | bytes 110600 | tf_op jit(solution)/shard_map/ppermute | solution.py:447
  71.5 7.4 %collective-permute-start.35 = (bf16[96,192]{1,0:T(8,128)(2,1)S(1)}, bf16[96,192]{1,0:T(8,128)(2,1)S(1)}, u32[]{:S(2)}, u32[]{:S(2)}) collective-permute-start(bf16[96,192]{1,0:T(8,128)(2,1)S(1)} %fusion.2), channel_id=1, source_target_pairs={{0,16},{1,17},{2,18},{3,19},{4,20},{5,21},{6,22},{7,23},{8,26},{9,... | collective-permute-start | bytes 110600 | tf_op jit(solution)/shard_map/ppermute | solution.py:447
  75.9 7.7 %collective-permute-start.36 = (bf16[96,192]{1,0:T(8,128)(2,1)S(1)}, bf16[96,192]{1,0:T(8,128)(2,1)S(1)}, u32[]{:S(2)}, u32[]{:S(2)}) collective-permute-start(bf16[96,192]{1,0:T(8,128)(2,1)S(1)} %fusion.2), channel_id=1, source_target_pairs={{0,24},{1,25},{2,26},{3,27},{4,28},{5,29},{6,30},{7,31},{8,18},{9,... | collective-permute-start | bytes 110600 | tf_op jit(solution)/shard_map/ppermute | solution.py:447
  (14 other events, 82.3 us)

commit v8 on v6

--- a/solution.py
+++ b/solution.py
@@ -197,7 +197,39 @@
     for k in range(hg):
         line = jnp.where(square_row == square_col, seg_s[0:1, k * rows : (k + 1) * rows], 0.0)
         col_s[k] = jnp.sum(line, axis=1, keepdims=True)
-    if slots == hg:
+
+    def pair(k):
+        both = 2 * rows
+        at = slice(k * rows, k * rows + both)
+        for j in (0, 1):
+            start = (k + j) * rows
+            in_block = (column >= start) & (column < start + rows) & (label >= 0.0)
+            same_value = jnp.where(in_block, 1.0, 0.0)
+            other_value = jnp.where(in_block, 0.0, NEG_BIG)
+            bias = jnp.where(col_s[k + j] == label, same_value, other_value)
+            bias_s[j * rows : (j + 1) * rows, :] = jnp.where(row_at + start == col_at, 1.0, bias)
+        head_of = lax.broadcasted_iota(jnp.int32, (both, cw), 1) // head_dim
+        q = q_s[at, :]
+        scaled = jnp.zeros((both, cw), jnp.float32)
+        acc = jnp.zeros((both, cw), jnp.float32)
+        for h in range(heads):
+            qh = jnp.where(head_of == h, q, jnp.zeros_like(q))
+            s = dot_last(qh, k_s[...]) * scale + bias_s[...]
+            top = jnp.max(s, axis=1, keepdims=True)
+            p = jnp.exp2(s - top)
+            total = jnp.sum(p, axis=1, keepdims=True)
+            weight = p.astype(jnp.bfloat16)
+            p_s[k, h] = weight[:rows]
+            p_s[k + 1, h] = weight[rows:]
+            scaled = jnp.where(head_of == h, 1.0 / total, scaled)
+            acc = jnp.where(head_of == h, dot(weight, v_s[...]), acc)
+        scaled_out[at, :] = scaled
+        o_s[at, :] = (acc * scaled).astype(jnp.bfloat16)
+
+    if resident and hg % 2 == 0:
+        for k in range(0, hg, 2):
+            pair(k)
+    elif slots == hg:
         for k in range(hg):
             chunk(k, 0)
     else:
@@ -244,7 +276,7 @@
             pltpu.VMEM((hg * rows, cw), bf16),
             pltpu.VMEM((keys, cw), bf16),
             pltpu.VMEM((keys, cw), bf16),
-            pltpu.VMEM((rows, keys), jnp.float32),
+            pltpu.VMEM(((2 if resident else 1) * rows, keys), jnp.float32),
             pltpu.VMEM((hg * rows, cw), bf16),
             pltpu.SemaphoreType.DMA((n * parts + n + hg,)),
         ],

time: 84.3 us -> 84.3 us (level)
  transfers between devices with their start and end apart: 42 -> 42, of which waited for: 13 -> 14; matrix products, arithmetic and copies ran while one was open for 1% -> 1% of each run, Pallas kernels for 17% -> 16%
where the time goes in v8:
time: 84.3 us; the launch traced here: 84.1 us
  starting transfers between devices  38.6 us (46%)
  waiting for transfers between devices  25.9 us (31%)
  Pallas kernels  17 us (20%)
  between operations  1.45 us (2%)
  local copies, waits for them, and re-layouts  1.02 us (1%)
    ppermute x35, starting transfers between devices, hop(): return lax.ppermute(x, 'seq', [(s, s ^ step) for s in range(n)])  23.6 us
    ppermute x35, waiting for transfers between devices, hop(): return lax.ppermute(x, 'seq', [(s, s ^ step) for s in range(n)])  19.5 us
    pallas_call x1, Pallas kernels, local(): attention_call(hg, tg, parts, rows, width, wr, cw, head_dim)  8.67 us
    ppermute x4, starting transfers between devices, local(): pieces.append(lax.ppermute(mine, ('dp', 'seq'), pairs))  7.58 us
    ppermute x3, starting transfers between devices, local(): got = lax.ppermute(summed[m], 'dp', [(z, z ^ m) for z in range(dp)])  7.46 us
    ppermute x4, waiting for transfers between devices, local(): pieces.append(lax.ppermute(mine, ('dp', 'seq'), pairs))  6.39 us
    pallas_call x1, Pallas kernels, local(): gradient_call(hg, tg, parts, rows, width, wr, cw, head_dim, by_dp)  3.81 us
    pallas_call x1, Pallas kernels, local(): pl.pallas_call(functools.partial(pack_kernel, hg, tg, wr, cw), out_shape=...  2.3 us
  transfers between devices with their start and end apart: 42, of which 14 were waited for; matrix products, arithmetic and copies ran while one was open for 1% of the time, Pallas kernels for 16%

profile of v8, /device:TPU:0, one launch (start us, length us, event | category | flops | bytes accessed | tf_op | source)
XLA Modules:
  0.0 84.1 jit_solution(1378938889270178971)
XLA Ops:
  1.3 2.3 %shard_map.95 = (bf16[3,104,192]{2,1,0:T(8,128)(2,1)S(1)}, bf16[3,104,192]{2,1,0:T(8,128)(2,1)}, bf16[3,104,192]{2,1,0:T(8,128)(2,1)}, bf16[3,104,192]{2,1,0:T(8...) custom-call(s32[1]{0:T(128)S(6)} %copy.10.count, bf16[96,768]{1,0:T(8,128)(2,1)} %wq.1, ...), custom_call_target="tpu_custom_call" | custom-call | tf_op jit(solution)/shard_map/pallas_call | solution.py:405
  3.6 3.0 %collective-permute-start.14 = (bf16[3,104,192]{2,1,0:T(8,128)(2,1)}, bf16[3,104,192]{2,1,0:T(8,128)(2,1)S(1)}, u32[]{:S(2)}, u32[]{:S(2)}) collective-permute-start(bf16[3,104,192]{2,1,0:T(8,128)(2,1)} %get-tuple-element.18), channel_id=1, source_target_pairs={{0,2},{1,3},{2,0},{3,1},{4,6},{5,7},{6,4},{7,5},{8,10},{9,11},{10,... | collective-permute-start | bytes 359432 | tf_op jit(solution)/shard_map/ppermute | solution.py:390
  6.5 1.5 %collective-permute-start.15 = (bf16[3,104,192]{2,1,0:T(8,128)(2,1)}, bf16[3,104,192]{2,1,0:T(8,128)(2,1)S(1)}, u32[]{:S(2)}, u32[]{:S(2)}) collective-permute-start(bf16[3,104,192]{2,1,0:T(8,128)(2,1)} %get-tuple-element.19), channel_id=1, source_target_pairs={{0,4},{1,5},{2,6},{3,7},{4,0},{5,1},{6,2},{7,3},{8,12},{9,13},{10,... | collective-permute-start | bytes 359432 | tf_op jit(solution)/shard_map/ppermute | solution.py:390
  9.1 2.0 %collective-permute-start = (bf16[96,768]{1,0:T(8,128)(2,1)S(1)}, bf16[96,768]{1,0:T(8,128)(2,1)S(1)}, u32[]{:S(2)}, u32[]{:S(2)}) collective-permute-start(bf16[96,768]{1,0:T(8,128)(2,1)S(1)} %get-tuple-element.33.refs_0_), channel_id=1, source_target_pairs={{0,2},{1,3},{2,0},{3,1},{4,6},{5,7},{6,4},{7,5},{8,10},{9,11},{10,... | collective-permute-start | bytes 442376 | tf_op jit(solution)/shard_map/ppermute | solution.py:390
  11.6 2.0 %collective-permute-start.3 = (bf16[96,768]{1,0:T(8,128)(2,1)S(1)}, bf16[96,768]{1,0:T(8,128)(2,1)S(1)}, u32[]{:S(2)}, u32[]{:S(2)}) collective-permute-start(bf16[96,768]{1,0:T(8,128)(2,1)S(1)} %get-tuple-element.32.refs_1_), channel_id=1, source_target_pairs={{0,4},{1,5},{2,6},{3,7},{4,0},{5,1},{6,2},{7,3},{8,12},{9,13},{10,... | collective-permute-start | bytes 442376 | tf_op jit(solution)/shard_map/ppermute | solution.py:390
  13.7 2.3 %collective-permute-done.15.refs_18_ = bf16[3,104,192]{2,1,0:T(8,128)(2,1)S(1)} collective-permute-done((bf16[3,104,192]{2,1,0:T(8,128)(2,1)}, bf16[3,104,192]{2,1,0:T(8,128)(2,1)S(1)}, u32[]{:S(2)}, u32[]{:S(2)}) %collective-permute-start.15) | collective-permute-done | bytes 119840 | tf_op jit(solution)/shard_map/ppermute | solution.py:390
  15.9 2.4 %collective-permute-start.2 = (bf16[96,768]{1,0:T(8,128)(2,1)S(1)}, bf16[96,768]{1,0:T(8,128)(2,1)S(1)}, u32[]{:S(2)}, u32[]{:S(2)}) collective-permute-start(bf16[96,768]{1,0:T(8,128)(2,1)S(1)} %get-tuple-element.33.refs_0_), channel_id=1, source_target_pairs={{0,4},{1,5},{2,6},{3,7},{4,0},{5,1},{6,2},{7,3},{8,12},{9,13},{10,... | collective-permute-start | bytes 442376 | tf_op jit(solution)/shard_map/ppermute | solution.py:390
  19.1 3.0 %collective-permute-done.2.refs_4_ = bf16[96,768]{1,0:T(8,128)(2,1)S(1)} collective-permute-done((bf16[96,768]{1,0:T(8,128)(2,1)S(1)}, bf16[96,768]{1,0:T(8,128)(2,1)S(1)}, u32[]{:S(2)}, u32[]{:S(2)}) %collective-permute-start.2) | collective-permute-done | bytes 147488 | tf_op jit(solution)/shard_map/ppermute | solution.py:390
  25.2 4.5 %collective-permute-done.4.refs_6_ = bf16[96,768]{1,0:T(8,128)(2,1)S(1)} collective-permute-done((bf16[96,768]{1,0:T(8,128)(2,1)S(1)}, bf16[96,768]{1,0:T(8,128)(2,1)S(1)}, u32[]{:S(2)}, u32[]{:S(2)}) %collective-permute-start.4) | collective-permute-done | bytes 147488 | tf_op jit(solution)/shard_map/ppermute | solution.py:390
  30.2 1.5 %collective-permute-start.32 = (bf16[192,768]{1,0:T(8,128)(2,1)S(1)}, bf16[192,768]{1,0:T(8,128)(2,1)S(1)}, u32[]{:S(2)}, u32[]{:S(2)}) collective-permute-start(bf16[192,768]{1,0:T(8,128)(2,1)S(1)} %get-tuple-element.28.refs_2_), channel_id=1, source_target_pairs={{0,4},{1,5},{2,6},{3,7},{4,0},{5,1},{6,2},{7,3},{8,12},{9,13},{10,... | collective-permute-start | bytes 884744 | tf_op jit(solution)/shard_map/ppermute | solution.py:390
  31.8 2.0 %collective-permute-start.33 = (bf16[192,768]{1,0:T(8,128)(2,1)S(1)}, bf16[192,768]{1,0:T(8,128)(2,1)S(1)}, u32[]{:S(2)}, u32[]{:S(2)}) collective-permute-start(bf16[192,768]{1,0:T(8,128)(2,1)S(1)} %get-tuple-element.28.refs_2_), channel_id=1, source_target_pairs={{0,6},{1,7},{2,4},{3,5},{4,2},{5,3},{6,0},{7,1},{8,14},{9,15},{10,... | collective-permute-start | bytes 884744 | tf_op jit(solution)/shard_map/ppermute | solution.py:390
  35.2 8.7 %shard_map.96 = (bf16[192,192]{1,0:T(8,128)(2,1)S(1)}, bf16[192,192]{1,0:T(8,128)(2,1)S(1)}, bf16[192,192]{1,0:T(8,128)(2,1)S(1)}, bf16[192,192]{1,0:T(8,128)(2,...) custom-call(s32[1]{0:T(128)S(6)} %copy.10.count, ...), custom_call_target="tpu_custom_call" | custom-call | tf_op jit(solution)/shard_map/pallas_call | solution.py:437
  44.0 3.1 %collective-permute-done.33.refs_5_ = bf16[192,768]{1,0:T(8,128)(2,1)S(1)} collective-permute-done((bf16[192,768]{1,0:T(8,128)(2,1)S(1)}, bf16[192,768]{1,0:T(8,128)(2,1)S(1)}, u32[]{:S(2)}, u32[]{:S(2)}) %collective-permute-start.33) | collective-permute-done | bytes 294944 | tf_op jit(solution)/shard_map/ppermute | solution.py:390
  47.1 3.8 %shard_map.98 = (bf16[4,96,192]{2,1,0:T(8,128)(2,1)S(1)}, bf16[4,96,192]{2,1,0:T(8,128)(2,1)S(1)}) custom-call(bf16[4,3,192,1536]{3,2,1,0:T(8,128)(2,1)S(1)} %get-tuple-element.26.refs_0_, bf16[1536,768]{1,0:T(8,128)(2,1)S(1)} %get-tuple-element.27.refs_1_, bf16[192,768]{1,0:T(8,128)(2,1)S(1)} %get-tuple-element.28.refs_2_, ...), custom_call_target="tpu_custom_call" | custom-call | tf_op jit(solution)/shard_map/pallas_call | solution.py:444
  53.0 1.5 %collective-permute-start.35 = (bf16[96,192]{1,0:T(8,128)(2,1)S(1)}, bf16[96,192]{1,0:T(8,128)(2,1)S(1)}, u32[]{:S(2)}, u32[]{:S(2)}) collective-permute-start(bf16[96,192]{1,0:T(8,128)(2,1)S(1)} %get-tuple-element.34), channel_id=1, source_target_pairs={{0,8},{8,0},{16,24},{24,16},{1,9},{9,1},{17,25},{25,17},{2,10},{10... | collective-permute-start | bytes 110600 | tf_op jit(solution)/shard_map/ppermute | solution.py:467
  54.4 2.6 %collective-permute-start.36 = (bf16[96,192]{1,0:T(8,128)(2,1)S(1)}, bf16[96,192]{1,0:T(8,128)(2,1)S(1)}, u32[]{:S(2)}, u32[]{:S(2)}) collective-permute-start(bf16[96,192]{1,0:T(8,128)(2,1)S(1)} %get-tuple-element.36), channel_id=1, source_target_pairs={{0,16},{8,24},{16,0},{24,8},{1,17},{9,25},{17,1},{25,9},{2,18},{10... | collective-permute-start | bytes 110600 | tf_op jit(solution)/shard_map/ppermute | solution.py:467
  57.0 3.4 %collective-permute-done.25.refs_6_ = bf16[96,768]{1,0:T(8,128)(2,1)S(1)} collective-permute-done((bf16[96,768]{1,0:T(8,128)(2,1)S(1)}, bf16[96,768]{1,0:T(8,128)(2,1)S(1)}, u32[]{:S(2)}, u32[]{:S(2)}) %collective-permute-start.25) | collective-permute-done | bytes 147488 | tf_op jit(solution)/shard_map/ppermute | solution.py:390
  60.4 3.4 %collective-permute-start.37 = (bf16[96,192]{1,0:T(8,128)(2,1)S(1)}, bf16[96,192]{1,0:T(8,128)(2,1)S(1)}, u32[]{:S(2)}, u32[]{:S(2)}) collective-permute-start(bf16[96,192]{1,0:T(8,128)(2,1)S(1)} %get-tuple-element.35), channel_id=1, source_target_pairs={{0,24},{8,16},{16,8},{24,0},{1,25},{9,17},{17,9},{25,1},{2,26},{10... | collective-permute-start | bytes 110600 | tf_op jit(solution)/shard_map/ppermute | solution.py:467
  64.7 1.5 %collective-permute-start.22 = (bf16[192,192]{1,0:T(8,128)(2,1)S(1)}, bf16[192,192]{1,0:T(8,128)(2,1)S(1)}, u32[]{:S(2)}, u32[]{:S(2)}) collective-permute-start(bf16[192,192]{1,0:T(8,128)(2,1)S(1)} %get-tuple-element.23), channel_id=1, source_target_pairs={{0,4},{1,5},{2,6},{3,7},{4,0},{5,1},{6,2},{7,3},{8,12},{9,13},{10,... | collective-permute-start | bytes 221192 | tf_op jit(solution)/shard_map/ppermute | solution.py:390
  66.3 1.6 %collective-permute-start.23 = (bf16[192,192]{1,0:T(8,128)(2,1)S(1)}, bf16[192,192]{1,0:T(8,128)(2,1)S(1)}, u32[]{:S(2)}, u32[]{:S(2)}) collective-permute-start(bf16[192,192]{1,0:T(8,128)(2,1)S(1)} %get-tuple-element.24), channel_id=1, source_target_pairs={{0,6},{1,7},{2,4},{3,5},{4,2},{5,3},{6,0},{7,1},{8,14},{9,15},{10,... | collective-permute-start | bytes 221192 | tf_op jit(solution)/shard_map/ppermute | solution.py:390
  68.6 1.7 %collective-permute-start.39 = (bf16[96,192]{1,0:T(8,128)(2,1)S(1)}, bf16[96,192]{1,0:T(8,128)(2,1)S(1)}, u32[]{:S(2)}, u32[]{:S(2)}) collective-permute-start(bf16[96,192]{1,0:T(8,128)(2,1)S(1)} %fusion.2), channel_id=1, source_target_pairs={{0,8},{1,9},{2,10},{3,11},{4,12},{5,13},{6,14},{7,15},{8,2},{9,3},... | collective-permute-start | bytes 110600 | tf_op jit(solution)/shard_map/ppermute | solution.py:475
  70.3 5.2 %collective-permute-start.40 = (bf16[96,192]{1,0:T(8,128)(2,1)S(1)}, bf16[96,192]{1,0:T(8,128)(2,1)S(1)}, u32[]{:S(2)}, u32[]{:S(2)}) collective-permute-start(bf16[96,192]{1,0:T(8,128)(2,1)S(1)} %fusion.2), channel_id=1, source_target_pairs={{0,16},{1,17},{2,18},{3,19},{4,20},{5,21},{6,22},{7,23},{8,26},{9,... | collective-permute-start | bytes 110600 | tf_op jit(solution)/shard_map/ppermute | solution.py:475
  76.8 1.4 %collective-permute-done.40.refs_2_ = bf16[96,192]{1,0:T(8,128)(2,1)S(1)} collective-permute-done((bf16[96,192]{1,0:T(8,128)(2,1)S(1)}, bf16[96,192]{1,0:T(8,128)(2,1)S(1)}, u32[]{:S(2)}, u32[]{:S(2)}) %collective-permute-start.40) | collective-permute-done | bytes 36896 | tf_op jit(solution)/shard_map/ppermute | solution.py:475
  78.2 5.0 %collective-permute-done.41.refs_3_ = bf16[96,192]{1,0:T(8,128)(2,1)S(1)} collective-permute-done((bf16[96,192]{1,0:T(8,128)(2,1)S(1)}, bf16[96,192]{1,0:T(8,128)(2,1)S(1)}, u32[]{:S(2)}, u32[]{:S(2)}) %collective-permute-start.41) | collective-permute-done | bytes 36896 | tf_op jit(solution)/shard_map/ppermute | solution.py:475
  (71 shorter events, 13.4 us)
Async XLA Ops:
  3.6 8.1 %collective-permute-start.14 = (bf16[3,104,192]{2,1,0:T(8,128)(2,1)}, bf16[3,104,192]{2,1,0:T(8,128)(2,1)S(1)}, u32[]{:S(2)}, u32[]{:S(2)}) collective-permute-start(bf16[3,104,192]{2,1,0:T(8,128)(2,1)} %get-tuple-element.18), channel_id=1, source_target_pairs={{0,2},{1,3},{2,0},{3,1},{4,6},{5,7},{6,4},{7,5},{8,10},{9,11},{10,... | collective-permute-start | bytes 359432 | tf_op jit(solution)/shard_map/ppermute | solution.py:390
  6.5 9.4 %collective-permute-start.15 = (bf16[3,104,192]{2,1,0:T(8,128)(2,1)}, bf16[3,104,192]{2,1,0:T(8,128)(2,1)S(1)}, u32[]{:S(2)}, u32[]{:S(2)}) collective-permute-start(bf16[3,104,192]{2,1,0:T(8,128)(2,1)} %get-tuple-element.19), channel_id=1, source_target_pairs={{0,4},{1,5},{2,6},{3,7},{4,0},{5,1},{6,2},{7,3},{8,12},{9,13},{10,... | collective-permute-start | bytes 359432 | tf_op jit(solution)/shard_map/ppermute | solution.py:390
  8.0 10.3 %collective-permute-start.16 = (bf16[3,104,192]{2,1,0:T(8,128)(2,1)}, bf16[3,104,192]{2,1,0:T(8,128)(2,1)S(1)}, u32[]{:S(2)}, u32[]{:S(2)}) collective-permute-start(bf16[3,104,192]{2,1,0:T(8,128)(2,1)} %get-tuple-element.20), channel_id=1, source_target_pairs={{0,6},{1,7},{2,4},{3,5},{4,2},{5,3},{6,0},{7,1},{8,14},{9,15},{10,... | collective-permute-start | bytes 359432 | tf_op jit(solution)/shard_map/ppermute | solution.py:390
  9.1 9.3 %collective-permute-start = (bf16[96,768]{1,0:T(8,128)(2,1)S(1)}, bf16[96,768]{1,0:T(8,128)(2,1)S(1)}, u32[]{:S(2)}, u32[]{:S(2)}) collective-permute-start(bf16[96,768]{1,0:T(8,128)(2,1)S(1)} %get-tuple-element.33.refs_0_), channel_id=1, source_target_pairs={{0,2},{1,3},{2,0},{3,1},{4,6},{5,7},{6,4},{7,5},{8,10},{9,11},{10,... | collective-permute-start | bytes 442376 | tf_op jit(solution)/shard_map/ppermute | solution.py:390
  11.1 7.2 %collective-permute-start.17 = (bf16[3,104,192]{2,1,0:T(8,128)(2,1)S(1)}, bf16[3,104,192]{2,1,0:T(8,128)(2,1)S(1)}, u32[]{:S(2)}, u32[]{:S(2)}) collective-permute-start(bf16[3,104,192]{2,1,0:T(8,128)(2,1)S(1)} %get-tuple-element.17.refs_16_), channel_id=1, source_target_pairs={{0,1},{1,0},{2,3},{3,2},{4,5},{5,4},{6,7},{7,6},{8,9},{9,8},{10,11... | collective-permute-start | bytes 359432 | tf_op jit(solution)/shard_map/ppermute | solution.py:390
  11.6 7.4 %collective-permute-start.3 = (bf16[96,768]{1,0:T(8,128)(2,1)S(1)}, bf16[96,768]{1,0:T(8,128)(2,1)S(1)}, u32[]{:S(2)}, u32[]{:S(2)}) collective-permute-start(bf16[96,768]{1,0:T(8,128)(2,1)S(1)} %get-tuple-element.32.refs_1_), channel_id=1, source_target_pairs={{0,4},{1,5},{2,6},{3,7},{4,0},{5,1},{6,2},{7,3},{8,12},{9,13},{10,... | collective-permute-start | bytes 442376 | tf_op jit(solution)/shard_map/ppermute | solution.py:390
  23.4 6.3 %collective-permute-start.4 = (bf16[96,768]{1,0:T(8,128)(2,1)S(1)}, bf16[96,768]{1,0:T(8,128)(2,1)S(1)}, u32[]{:S(2)}, u32[]{:S(2)}) collective-permute-start(bf16[96,768]{1,0:T(8,128)(2,1)S(1)} %collective-permute-done.refs_2_), channel_id=1, source_target_pairs={{0,4},{1,5},{2,6},{3,7},{4,0},{5,1},{6,2},{7,3},{8,12},{9,13},{10,... | collective-permute-start | bytes 442376 | tf_op jit(solution)/shard_map/ppermute | solution.py:390
  25.2 6.6 %collective-permute-start.10 = (bf16[96,768]{1,0:T(8,128)(2,1)S(1)}, bf16[96,768]{1,0:T(8,128)(2,1)S(1)}, u32[]{:S(2)}, u32[]{:S(2)}) collective-permute-start(bf16[96,768]{1,0:T(8,128)(2,1)S(1)} %collective-permute-done.2.refs_4_), channel_id=1, source_target_pairs={{0,1},{1,0},{2,3},{3,2},{4,5},{5,4},{6,7},{7,6},{8,9},{9,8},{10,11... | collective-permute-start | bytes 442376 | tf_op jit(solution)/shard_map/ppermute | solution.py:390
  30.2 13.6 %collective-permute-start.31 = (bf16[192,768]{1,0:T(8,128)(2,1)S(1)}, bf16[192,768]{1,0:T(8,128)(2,1)S(1)}, u32[]{:S(2)}, u32[]{:S(2)}) collective-permute-start(bf16[192,768]{1,0:T(8,128)(2,1)S(1)} %get-tuple-element.28.refs_2_), channel_id=1, source_target_pairs={{0,2},{1,3},{2,0},{3,1},{4,6},{5,7},{6,4},{7,5},{8,10},{9,11},{10,... | collective-permute-start | bytes 884744 | tf_op jit(solution)/shard_map/ppermute | solution.py:390
  30.2 13.8 %collective-permute-start.32 = (bf16[192,768]{1,0:T(8,128)(2,1)S(1)}, bf16[192,768]{1,0:T(8,128)(2,1)S(1)}, u32[]{:S(2)}, u32[]{:S(2)}) collective-permute-start(bf16[192,768]{1,0:T(8,128)(2,1)S(1)} %get-tuple-element.28.refs_2_), channel_id=1, source_target_pairs={{0,4},{1,5},{2,6},{3,7},{4,0},{5,1},{6,2},{7,3},{8,12},{9,13},{10,... | collective-permute-start | bytes 884744 | tf_op jit(solution)/shard_map/ppermute | solution.py:390
  31.8 15.3 %collective-permute-start.33 = (bf16[192,768]{1,0:T(8,128)(2,1)S(1)}, bf16[192,768]{1,0:T(8,128)(2,1)S(1)}, u32[]{:S(2)}, u32[]{:S(2)}) collective-permute-start(bf16[192,768]{1,0:T(8,128)(2,1)S(1)} %get-tuple-element.28.refs_2_), channel_id=1, source_target_pairs={{0,6},{1,7},{2,4},{3,5},{4,2},{5,3},{6,0},{7,1},{8,14},{9,15},{10,... | collective-permute-start | bytes 884744 | tf_op jit(solution)/shard_map/ppermute | solution.py:390
  33.8 10.1 %collective-permute-start.27 = (bf16[96,768]{1,0:T(8,128)(2,1)S(1)}, bf16[96,768]{1,0:T(8,128)(2,1)S(1)}, u32[]{:S(2)}, u32[]{:S(2)}) collective-permute-start(bf16[96,768]{1,0:T(8,128)(2,1)S(1)} %get-tuple-element.25.refs_4_.refs_6_), channel_id=1, source_target_pairs={{0,1},{1,0},{2,3},{3,2},{4,5},{5,4},{6,7},{7,6},{8,9},{9,8},{10,11... | collective-permute-start | bytes 442376 | tf_op jit(solution)/shard_map/ppermute | solution.py:390
  35.1 17.8 %collective-permute-start.24 = (bf16[96,768]{1,0:T(8,128)(2,1)}, bf16[96,768]{1,0:T(8,128)(2,1)S(1)}, u32[]{:S(2)}, u32[]{:S(2)}) collective-permute-start(bf16[96,768]{1,0:T(8,128)(2,1)} %wout.1), channel_id=1, source_target_pairs={{0,2},{1,3},{2,0},{3,1},{4,6},{5,7},{6,4},{7,5},{8,10},{9,11},{10,... | collective-permute-start | bytes 442376 | tf_op jit(solution)/shard_map/ppermute | solution.py:390
  51.0 9.4 %collective-permute-start.25 = (bf16[96,768]{1,0:T(8,128)(2,1)S(1)}, bf16[96,768]{1,0:T(8,128)(2,1)S(1)}, u32[]{:S(2)}, u32[]{:S(2)}) collective-permute-start(bf16[96,768]{1,0:T(8,128)(2,1)S(1)} %copy-done), channel_id=1, source_target_pairs={{0,4},{1,5},{2,6},{3,7},{4,0},{5,1},{6,2},{7,3},{8,12},{9,13},{10,... | collective-permute-start | bytes 442376 | tf_op jit(solution)/shard_map/ppermute | solution.py:390
  51.9 11.9 %collective-permute-start.26 = (bf16[96,768]{1,0:T(8,128)(2,1)S(1)}, bf16[96,768]{1,0:T(8,128)(2,1)S(1)}, u32[]{:S(2)}, u32[]{:S(2)}) collective-permute-start(bf16[96,768]{1,0:T(8,128)(2,1)S(1)} %copy-done), channel_id=1, source_target_pairs={{0,6},{1,7},{2,4},{3,5},{4,2},{5,3},{6,0},{7,1},{8,14},{9,15},{10,... | collective-permute-start | bytes 442376 | tf_op jit(solution)/shard_map/ppermute | solution.py:390
  52.9 11.0 %collective-permute-start.28 = (bf16[96,768]{1,0:T(8,128)(2,1)S(1)}, bf16[96,768]{1,0:T(8,128)(2,1)S(1)}, u32[]{:S(2)}, u32[]{:S(2)}) collective-permute-start(bf16[96,768]{1,0:T(8,128)(2,1)S(1)} %collective-permute-done.24.refs_5_), channel_id=1, source_target_pairs={{0,1},{1,0},{2,3},{3,2},{4,5},{5,4},{6,7},{7,6},{8,9},{9,8},{10,11... | collective-permute-start | bytes 442376 | tf_op jit(solution)/shard_map/ppermute | solution.py:390
  53.0 11.4 %collective-permute-start.35 = (bf16[96,192]{1,0:T(8,128)(2,1)S(1)}, bf16[96,192]{1,0:T(8,128)(2,1)S(1)}, u32[]{:S(2)}, u32[]{:S(2)}) collective-permute-start(bf16[96,192]{1,0:T(8,128)(2,1)S(1)} %get-tuple-element.34), channel_id=1, source_target_pairs={{0,8},{8,0},{16,24},{24,16},{1,9},{9,1},{17,25},{25,17},{2,10},{10... | collective-permute-start | bytes 110600 | tf_op jit(solution)/shard_map/ppermute | solution.py:467
  54.4 10.3 %collective-permute-start.36 = (bf16[96,192]{1,0:T(8,128)(2,1)S(1)}, bf16[96,192]{1,0:T(8,128)(2,1)S(1)}, u32[]{:S(2)}, u32[]{:S(2)}) collective-permute-start(bf16[96,192]{1,0:T(8,128)(2,1)S(1)} %get-tuple-element.36), channel_id=1, source_target_pairs={{0,16},{8,24},{16,0},{24,8},{1,17},{9,25},{17,1},{25,9},{2,18},{10... | collective-permute-start | bytes 110600 | tf_op jit(solution)/shard_map/ppermute | solution.py:467
  64.7 10.8 %collective-permute-start.22 = (bf16[192,192]{1,0:T(8,128)(2,1)S(1)}, bf16[192,192]{1,0:T(8,128)(2,1)S(1)}, u32[]{:S(2)}, u32[]{:S(2)}) collective-permute-start(bf16[192,192]{1,0:T(8,128)(2,1)S(1)} %get-tuple-element.23), channel_id=1, source_target_pairs={{0,4},{1,5},{2,6},{3,7},{4,0},{5,1},{6,2},{7,3},{8,12},{9,13},{10,... | collective-permute-start | bytes 221192 | tf_op jit(solution)/shard_map/ppermute | solution.py:390
  66.3 9.2 %collective-permute-start.23 = (bf16[192,192]{1,0:T(8,128)(2,1)S(1)}, bf16[192,192]{1,0:T(8,128)(2,1)S(1)}, u32[]{:S(2)}, u32[]{:S(2)}) collective-permute-start(bf16[192,192]{1,0:T(8,128)(2,1)S(1)} %get-tuple-element.24), channel_id=1, source_target_pairs={{0,6},{1,7},{2,4},{3,5},{4,2},{5,3},{6,0},{7,1},{8,14},{9,15},{10,... | collective-permute-start | bytes 221192 | tf_op jit(solution)/shard_map/ppermute | solution.py:390
  67.9 8.9 %collective-permute-start.38 = (bf16[96,192]{1,0:T(8,128)(2,1)S(1)}, bf16[96,192]{1,0:T(8,128)(2,1)S(1)}, u32[]{:S(2)}, u32[]{:S(2)}) collective-permute-start(bf16[96,192]{1,0:T(8,128)(2,1)S(1)} %fusion.2), channel_id=1, source_target_pairs={{0,0},{1,1},{2,2},{3,3},{4,4},{5,5},{6,6},{7,7},{8,10},{9,11},{10,... | collective-permute-start | bytes 110600 | tf_op jit(solution)/shard_map/ppermute | solution.py:475
  68.6 8.2 %collective-permute-start.39 = (bf16[96,192]{1,0:T(8,128)(2,1)S(1)}, bf16[96,192]{1,0:T(8,128)(2,1)S(1)}, u32[]{:S(2)}, u32[]{:S(2)}) collective-permute-start(bf16[96,192]{1,0:T(8,128)(2,1)S(1)} %fusion.2), channel_id=1, source_target_pairs={{0,8},{1,9},{2,10},{3,11},{4,12},{5,13},{6,14},{7,15},{8,2},{9,3},... | collective-permute-start | bytes 110600 | tf_op jit(solution)/shard_map/ppermute | solution.py:475
  70.3 7.9 %collective-permute-start.40 = (bf16[96,192]{1,0:T(8,128)(2,1)S(1)}, bf16[96,192]{1,0:T(8,128)(2,1)S(1)}, u32[]{:S(2)}, u32[]{:S(2)}) collective-permute-start(bf16[96,192]{1,0:T(8,128)(2,1)S(1)} %fusion.2), channel_id=1, source_target_pairs={{0,16},{1,17},{2,18},{3,19},{4,20},{5,21},{6,22},{7,23},{8,26},{9,... | collective-permute-start | bytes 110600 | tf_op jit(solution)/shard_map/ppermute | solution.py:475
  75.5 7.7 %collective-permute-start.41 = (bf16[96,192]{1,0:T(8,128)(2,1)S(1)}, bf16[96,192]{1,0:T(8,128)(2,1)S(1)}, u32[]{:S(2)}, u32[]{:S(2)}) collective-permute-start(bf16[96,192]{1,0:T(8,128)(2,1)S(1)} %fusion.2), channel_id=1, source_target_pairs={{0,24},{1,25},{2,26},{3,27},{4,28},{5,29},{6,30},{7,31},{8,18},{9,... | collective-permute-start | bytes 110600 | tf_op jit(solution)/shard_map/ppermute | solution.py:475
  (19 other events, 98.1 us)
